TPU v7x, 32 devices: a whole 2x2x4 slice. The times are simulated.
32 devices in a mesh: row: 4 (over z), col: 8 (over y, x, core).
Axes of the slice: x: 2, y: 2, z: 4, core: 2. Of those that a mesh axis runs over, the one named last changes fastest.
Arguments:
- resistance: float32 [768, 1024], P('row', 'col'), may hold values from 1 to 100
- ground: float32 [768, 1024], P('row', 'col'), may hold values from 0.001 to 0.01
- nodata: int32 [768, 1024], P('row', 'col'), may hold values 0 or 1
- patch_ids: int32 [768, 1024], P('row', 'col'), may hold values from 0 to 8
Outputs:
- correction: float32 [8, 768, 1024], P(None, 'row', 'col')
All inputs are finite; a program needn't handle non-finite values. No bound on the sum of `nodata` on one device may be relied on, other than what follows from the above.
Results may differ from a plain program's by a relative error of at most 0.0003.
Values sent between devices are 32-bit elements; how exact they have to be, the bound alone decides.
No kernel may reach another device: no remote copies, remote signals or barrier semaphores. Data moves between devices by JAX's collectives and lax.ppermute only.
A program may use at most 128 MiB of HBM per device.

v0:
```python
from functools import partial

import jax
import jax.numpy as jnp
from jax import lax
from jax.sharding import PartitionSpec as P

RHS = 8
ITERS = 4


OMEGA = 0.8


def padded_2(block, sides, width):
    for axis, dim in sides:
        count = lax.axis_size(axis)
        forward = [(i, i + 1) for i in range(count - 1)]
        backward = [(target, source) for source, target in forward]
        low = lax.ppermute(
            lax.slice_in_dim(block, block.shape[dim] - width, None, axis=dim), axis, forward
        )
        high = lax.ppermute(lax.slice_in_dim(block, 0, width, axis=dim), axis, backward)
        block = jnp.concatenate([low, block, high], axis=dim)
    return block


def shifted(block, axis, distance):
    devices = range(lax.axis_size(axis))
    route = [(i - distance, i) for i in devices if i - distance in devices]
    return lax.ppermute(block, axis, route)


def partner_2(shard, axis, apart):
    return lax.ppermute(shard, axis, [(i, i ^ 1 << apart) for i in range(lax.axis_size(axis))])


def conductance(resist, validity, near_resist, near_valid):
    return validity * near_valid * (2.0 / (resist + near_resist))


def edge_terms(res_pad, val_pad):
    resist = res_pad[1:-1, 1:-1]
    validity = val_pad[1:-1, 1:-1]
    north_link = conductance(resist, validity, res_pad[:-2, 1:-1], val_pad[:-2, 1:-1])
    south_link = conductance(resist, validity, res_pad[2:, 1:-1], val_pad[2:, 1:-1])
    west_link = conductance(resist, validity, res_pad[1:-1, :-2], val_pad[1:-1, :-2])
    east_link = conductance(resist, validity, res_pad[1:-1, 2:], val_pad[1:-1, 2:])
    return (north_link, south_link, west_link, east_link)


def diagonal_of(coeffs):
    return coeffs[0] + coeffs[1] + coeffs[2] + coeffs[3] + coeffs[4]


def apply_operator(values, coeffs, sides):
    above_cells, below_cells, left_cells, right_cells = sides
    pulled = (
        coeffs[1] * above_cells
        + coeffs[2] * below_cells
        + coeffs[3] * left_cells
        + coeffs[4] * right_cells
    )
    return diagonal_of(coeffs) * values - pulled


def restrict_field(values):
    count, rows_here, cols_here = values.shape
    return values.reshape(count, rows_here // 2, 2, cols_here // 2, 2).sum(axis=(2, 4))


def coarse_coeffs(coeffs):
    count, rows_here, cols_here = coeffs.shape
    blocks = coeffs.reshape(count, rows_here // 2, 2, cols_here // 2, 2)
    leakage = blocks[0].sum(axis=(1, 3))
    north_link = blocks[1][:, 0].sum(axis=-1)
    south_link = blocks[2][:, 1].sum(axis=-1)
    west_link = blocks[3][:, :, :, 0].sum(axis=1)
    east_link = blocks[4][:, :, :, 1].sum(axis=1)
    return jnp.stack([leakage, north_link, south_link, west_link, east_link])


def prolong(values):
    return jnp.repeat(jnp.repeat(values, 2, axis=1), 2, axis=2)


def halo_sides(values):
    padded = padded_2(values, (("row", 1), ("col", 2)), 1)
    return (padded[:, :-2, 1:-1], padded[:, 2:, 1:-1], padded[:, 1:-1, :-2], padded[:, 1:-1, 2:])


def rim_sides(values, distance):
    above_rim = shifted(values[:, -1:, :], "row", distance)
    below_rim = shifted(values[:, :1, :], "row", -distance)
    left_rim = shifted(values[:, :, -1:], "col", distance)
    right_rim = shifted(values[:, :, :1], "col", -distance)
    above_cells = jnp.concatenate([above_rim, values[:, :-1, :]], axis=1)
    below_cells = jnp.concatenate([values[:, 1:, :], below_rim], axis=1)
    left_cells = jnp.concatenate([left_rim, values[:, :, :-1]], axis=2)
    right_cells = jnp.concatenate([values[:, :, 1:], right_rim], axis=2)
    return (above_cells, below_cells, left_cells, right_cells)


def descend(residual, coeffs, sides_of):
    smoothed = OMEGA * residual / diagonal_of(coeffs)
    remainder = residual - apply_operator(smoothed, coeffs, sides_of(smoothed))
    return (smoothed, restrict_field(remainder), coarse_coeffs(coeffs))


def merge_tiles(payload, bit_index):
    partner = partner_2(payload, "row", bit_index)
    is_first = (lax.axis_index("row") >> bit_index) % 2 == 0
    payload = jnp.where(
        is_first,
        jnp.concatenate([payload, partner], axis=1),
        jnp.concatenate([partner, payload], axis=1),
    )
    partner = partner_2(payload, "col", bit_index)
    is_first = (lax.axis_index("col") >> bit_index) % 2 == 0
    return jnp.where(
        is_first,
        jnp.concatenate([payload, partner], axis=2),
        jnp.concatenate([partner, payload], axis=2),
    )


def merge_level(residual, coeffs, bit_index):
    sources = residual.shape[0]
    merged = merge_tiles(jnp.concatenate([residual, coeffs], axis=0), bit_index)
    return (merged[:sources], merged[sources:])


def own_part(whole_grid, shift_bits, pieces, rows_here, cols_here):
    row_at = (lax.axis_index("row") >> shift_bits) % pieces
    col_at = (lax.axis_index("col") >> shift_bits) % pieces
    starts = (jnp.int32(0), row_at * rows_here, col_at * cols_here)
    return lax.dynamic_slice(whole_grid, starts, (whole_grid.shape[0], rows_here, cols_here))


def coarse_solve(rhs_grid, coeffs):
    sides_of = partial(rim_sides, distance=4)
    owner_weight = jnp.logical_and(
        lax.axis_index("row") % 4 == 0, lax.axis_index("col") % 4 == 0
    ).astype(jnp.float32)

    def local_dot(first, second):
        return owner_weight * jnp.sum(first * second, axis=(1, 2))

    def norm_sum(values):
        return lax.psum(local_dot(values, values), ("row", "col"))

    def expand(scalars):
        return scalars[:, None, None]

    solution = jnp.zeros_like(rhs_grid)
    residual = rhs_grid
    direction = residual
    norm_now = norm_sum(residual)
    for sweep in range(ITERS):
        image = apply_operator(direction, coeffs, sides_of(direction))
        step_size = norm_now / lax.psum(local_dot(direction, image), ("row", "col"))
        solution = solution + expand(step_size) * direction
        if sweep + 1 < ITERS:
            residual = residual - expand(step_size) * image
            norm_next = norm_sum(residual)
            direction = residual + expand(norm_next / norm_now) * direction
            norm_now = norm_next
    return solution


def shards(resistance, ground, nodata, patch_ids):
    validity = (nodata == 0).astype(jnp.float32)
    padded = padded_2(jnp.stack([resistance, validity]), (("row", 1), ("col", 2)), 1)
    coeffs = jnp.stack([ground] + list(edge_terms(padded[0], padded[1])))
    sources = jnp.arange(RHS, dtype=jnp.int32)[:, None, None]
    residual = validity[None] * (
        (patch_ids[None] == sources + 1).astype(jnp.float32)
        - 0.125 * (patch_ids[None] > 0).astype(jnp.float32)
    )
    smooth_a, residual, coeffs_b = descend(residual, coeffs, halo_sides)
    smooth_b, residual, coeffs_c = descend(residual, coeffs_b, halo_sides)
    smooth_c, residual, coeffs_d = descend(residual, coeffs_c, halo_sides)
    rows_d = residual.shape[1]
    cols_d = residual.shape[2]
    residual, coeffs_d = merge_level(residual, coeffs_d, 0)
    smooth_d, residual, coeffs_e = descend(residual, coeffs_d, partial(rim_sides, distance=2))
    residual, coeffs_e = merge_level(residual, coeffs_e, 1)
    solution = coarse_solve(residual, coeffs_e)
    upward = smooth_d + own_part(prolong(solution), 1, 2, 2 * rows_d, 2 * cols_d)
    upward = own_part(prolong(upward), 0, 2, 2 * rows_d, 2 * cols_d)
    upward = smooth_c + upward
    upward = smooth_b + prolong(upward)
    return smooth_a + prolong(upward)


def solution(mesh):
    in_specs = (P("row", "col"), P("row", "col"), P("row", "col"), P("row", "col"))
    out_specs = P(None, "row", "col")
    return jax.shard_map(shards, mesh=mesh, in_specs=in_specs, out_specs=out_specs, check_vma=False)
```

profile of v0, /device:TPU:0, one launch (start us, length us, event | category | flops | bytes accessed | tf_op | source)
XLA Modules:
  0.0 562.5 jit_solution(4791267187569328202)
XLA Ops:
  1.6 4.9 collective-permute-start
  8.8 3.2 collective-permute-done.1
  17.3 8.4 %squeeze.46 = f32[96,2,64,2]{3,2,1,0:T(8,128)} reshape(f32[192,128]{1,0:T(8,128)} %param.5) | data formatting | bytes 196608 | tf_op jit(solution)/shard_map/squeeze | solution.py:75
  25.6 3.7 reduce_sum.289
  34.1 7.6 %squeeze.47 = f32[96,2,64,2]{3,2,1,0:T(8,128)} reshape(f32[192,128]{1,0:T(8,128)S(1)} %get-tuple-element.19) | data formatting | bytes 196608 | tf_op jit(solution)/shard_map/squeeze | solution.py:76
  41.6 7.6 %squeeze.48 = f32[96,2,64,2]{3,2,1,0:T(8,128)} reshape(f32[192,128]{1,0:T(8,128)S(1)} %get-tuple-element.20) | data formatting | bytes 196608 | tf_op jit(solution)/shard_map/squeeze | solution.py:77
  49.2 4.6 slice_reduce_fusion.2
  54.0 7.6 %squeeze.49 = f32[96,2,64,2]{3,2,1,0:T(8,128)} reshape(f32[192,128]{1,0:T(8,128)S(1)} %get-tuple-element.21) | data formatting | bytes 196608 | tf_op jit(solution)/shard_map/squeeze | solution.py:78
  61.6 7.8 %squeeze.50 = f32[96,2,64,2]{3,2,1,0:T(8,128)} reshape(f32[192,128]{1,0:T(8,128)S(1)} %get-tuple-element.22) | data formatting | bytes 196608 | tf_op jit(solution)/shard_map/squeeze | solution.py:79
  69.4 7.9 %slice_reduce_fusion = (f32[96,64]{1,0:T(8,128)S(1)}, f32[96,64]{1,0:T(8,128)S(1)}) fusion(f32[96,2,64,2]{3,2,1,0:T(8,128)} %squeeze.50, f32[96,2,64,2]{3,2,1,0:T(8,128)} %squeeze.49), kind=kLoop, calls=%fused_computation | loop fusion | flops 12288 | bytes 147456 | tf_op jit(solution)/shard_map/reduce_sum | solution.py:79
  86.7 3.5 collective-permute-start.4
  91.9 8.8 %collective-permute-done.4 = f32[8,1,128]{1,0,2:T(8,128)S(1)} collective-permute-done((f32[8,1,128]{1,0,2:T(8,128)S(1)}, f32[8,1,128]{1,0,2:T(8,128)S(1)}, u32[]{:S(2)}, u32[]{:S(2)}) %collective-permute-start.4) | collective-permute-done | bytes 4128 | tf_op jit(solution)/shard_map/ppermute | solution.py:20
  100.7 4.7 collective-permute-done.5
  106.2 3.3 collective-permute-start.6
  115.4 4.1 fusion.3
  119.5 7.0 %copy.453 = f32[8,192,128]{0,2,1:T(8,128)} copy(f32[8,192,128]{1,0,2:T(8,128)S(1)} %fusion.3) | data formatting | bytes 1572864 | tf_op jit(solution)/shard_map/sub | solution.py:106
  126.6 14.0 %reduce_sum.288 = f32[8,96,64]{0,2,1:T(8,128)S(1)} reduce(f32[8,96,2,64,2]{0,4,3,2,1:T(2,128)} %bitcast.80, f32[]{:T(128)} %constant.67.clone.1), dimensions={2,4}, to_apply=%region_0.0 | reduce | flops 147456 | bytes 983044 | tf_op jit(solution)/shard_map/reduce_sum | solution.py:69
  143.5 3.5 collective-permute-start.8
  151.0 4.7 collective-permute-done.9
  155.8 4.1 collective-permute-start.10
  162.9 3.6 collective-permute-done.11
  167.8 3.7 copy.461
  171.6 3.9 reduce_sum.294
  178.0 2.2 collective-permute-start.12
  183.4 3.9 collective-permute-done.13
  187.4 2.8 collective-permute-start.14
  193.2 2.5 collective-permute-done.15
  198.3 5.9 %collective-permute-done.16 = f32[13,24,16]{0,2,1:T(8,128)S(1)} collective-permute-done((f32[13,24,16]{0,2,1:T(8,128)S(1)}, f32[13,24,16]{0,2,1:T(8,128)S(1)}, u32[]{:S(2)}, u32[]{:S(2)}) %collective-permute-start.16) | collective-permute-done | bytes 20000 | tf_op jit(solution)/shard_map/ppermute | solution.py:35
  209.7 4.5 collective-permute-start.20
  221.6 3.6 collective-permute-start.22
  225.4 7.4 %collective-permute-done.22 = f32[13,24,16]{0,2,1:T(8,128)S(1)} collective-permute-done((f32[13,24,16]{0,2,1:T(8,128)S(1)}, f32[13,24,16]{0,2,1:T(8,128)S(1)}, u32[]{:S(2)}, u32[]{:S(2)}) %collective-permute-start.22) | collective-permute-done | bytes 20000 | tf_op jit(solution)/shard_map/ppermute | solution.py:35
  233.1 2.2 collective-permute-start.23
  235.3 3.2 collective-permute-done.23
  240.1 3.4 collective-permute-start.26
  244.8 4.2 collective-permute-done.27
  249.3 37.8 %all-reduce = (f32[8]{0:T(128)S(1)}, f32[8]{0:T(128)S(1)}) all-reduce(f32[8]{0:T(128)S(1)} %broadcast_multiply_fusion.7, f32[8]{0:T(128)S(1)} %broadcast_multiply_fusion.6), channel_id=1, replica_groups=mesh['row'=4,'col'=8] {'row','col'}, use_global_device_ids=true, to_apply=%region_25.26 | all-reduce | flops 16 | bytes 128 | tf_op jit(solution)/shard_map/psum | solution.py:150
  287.3 40.3 %psum.58 = f32[8]{0:T(128)S(1)} all-reduce(f32[8]{0:T(128)S(1)} %broadcast_multiply_fusion.5), channel_id=1, replica_groups=mesh['row'=4,'col'=8] {'row','col'}, use_global_device_ids=true, to_apply=%region_29.30 | all-reduce | flops 8 | bytes 64 | tf_op jit(solution)/shard_map/psum | solution.py:150
  329.2 4.2 collective-permute-start.30
  334.7 4.1 collective-permute-done.31
  339.1 37.6 %psum.59 = f32[8]{0:T(128)S(1)} all-reduce(f32[8]{0:T(128)S(1)} %broadcast_multiply_fusion.4), channel_id=1, replica_groups=mesh['row'=4,'col'=8] {'row','col'}, use_global_device_ids=true, to_apply=%region_31.32 | all-reduce | flops 8 | bytes 64 | tf_op jit(solution)/shard_map/psum | solution.py:161
  377.0 41.9 %psum.60 = f32[8]{0:T(128)S(1)} all-reduce(f32[8]{0:T(128)S(1)} %broadcast_multiply_fusion.3), channel_id=1, replica_groups=mesh['row'=4,'col'=8] {'row','col'}, use_global_device_ids=true, to_apply=%region_33.34 | all-reduce | flops 8 | bytes 64 | tf_op jit(solution)/shard_map/psum | solution.py:150
  420.5 4.2 collective-permute-start.34
  426.0 4.1 collective-permute-done.35
  430.4 37.6 %psum.61 = f32[8]{0:T(128)S(1)} all-reduce(f32[8]{0:T(128)S(1)} %broadcast_multiply_fusion.2), channel_id=1, replica_groups=mesh['row'=4,'col'=8] {'row','col'}, use_global_device_ids=true, to_apply=%region_35.36 | all-reduce | flops 8 | bytes 64 | tf_op jit(solution)/shard_map/psum | solution.py:161
  468.3 40.5 %psum.62 = f32[8]{0:T(128)S(1)} all-reduce(f32[8]{0:T(128)S(1)} %broadcast_multiply_fusion.1), channel_id=1, replica_groups=mesh['row'=4,'col'=8] {'row','col'}, use_global_device_ids=true, to_apply=%region_37.38 | all-reduce | flops 8 | bytes 64 | tf_op jit(solution)/shard_map/psum | solution.py:150
  510.4 4.2 collective-permute-start.38
  516.0 4.1 collective-permute-done.39
  520.3 37.8 %psum.63 = f32[8]{0:T(128)S(1)} all-reduce(f32[8]{0:T(128)S(1)} %broadcast_multiply_fusion), channel_id=1, replica_groups=mesh['row'=4,'col'=8] {'row','col'}, use_global_device_ids=true, to_apply=%region_39.40 | all-reduce | flops 8 | bytes 64 | tf_op jit(solution)/shard_map/psum | solution.py:161
  (282 shorter events, 84.4 us)
Async XLA Ops:
  1.6 7.2 %collective-permute-start = (f32[2,1,128]{2,1,0:T(1,128)S(1)}, f32[2,1,128]{2,1,0:T(1,128)S(1)}, u32[]{:S(2)}, u32[]{:S(2)}) collective-permute-start(f32[2,1,128]{2,1,0:T(1,128)S(1)} %get-tuple-element.60), channel_id=1, source_target_pairs={{0,8},{8,16},{16,24},{1,9},{9,17},{17,25},{2,10},{10,18},{18,26},{... | collective-permute-start | bytes 3080 | tf_op jit(solution)/shard_map/ppermute | solution.py:20
  6.6 5.5 collective-permute-start.1
  13.1 18.8 %collective-permute-start.2 = (f32[2,194,1]{2,1,0:T(8,128)S(1)}, f32[2,194,1]{2,1,0:T(8,128)S(1)}, u32[]{:S(2)}, u32[]{:S(2)}) collective-permute-start(f32[2,194,1]{2,1,0:T(8,128)S(1)} %get-tuple-element.58), channel_id=1, source_target_pairs={{0,1},{1,2},{2,3},{3,4},{4,5},{5,6},{6,7},{8,9},{9,10},{10,11},{11... | collective-permute-start | bytes 4664 | tf_op jit(solution)/shard_map/ppermute | solution.py:20
  14.4 17.5 %collective-permute-start.3 = (f32[2,194,1]{2,1,0:T(8,128)S(1)}, f32[2,194,1]{2,1,0:T(8,128)}, u32[]{:S(2)}, u32[]{:S(2)}) collective-permute-start(f32[2,194,1]{2,1,0:T(8,128)S(1)} %get-tuple-element.59), channel_id=1, source_target_pairs={{1,0},{2,1},{3,2},{4,3},{5,4},{6,5},{7,6},{9,8},{10,9},{11,10},{12... | collective-permute-start | bytes 4664 | tf_op jit(solution)/shard_map/ppermute | solution.py:23
  30.6 84.8 %copy-start = (f32[192,128]{0,1:T(8,128)}, f32[192,128]{0,1:T(8,128)S(1)}, u32[]{:S(2)}) copy-start(f32[192,128]{0,1:T(8,128)S(1)} %copy.445) | copy-start | bytes 294916
  30.7 84.7 %copy-start.2 = (f32[192,128]{0,1:T(8,128)}, f32[192,128]{0,1:T(8,128)S(1)}, u32[]{:S(2)}) copy-start(f32[192,128]{0,1:T(8,128)S(1)} %copy.447) | copy-start | bytes 294916
  53.9 24.9 %copy-start.13 = (f32[96,64]{0,1:T(8,128)}, f32[96,64]{0,1:T(8,128)S(1)}, u32[]{:S(2)}) copy-start(f32[96,64]{0,1:T(8,128)S(1)} %copy.457) | copy-start | bytes 73732
  54.0 26.3 %copy-start.15 = (f32[96,64]{0,1:T(8,128)}, f32[96,64]{0,1:T(8,128)S(1)}, u32[]{:S(2)}) copy-start(f32[96,64]{0,1:T(8,128)S(1)} %copy.456) | copy-start | bytes 73732
  85.4 30.0 %copy-start.4 = (f32[192,128]{0,1:T(8,128)}, f32[192,128]{0,1:T(8,128)S(1)}, u32[]{:S(2)}) copy-start(f32[192,128]{0,1:T(8,128)S(1)} %copy.448) | copy-start | bytes 294916
  85.4 25.4 %copy-start.21 = (f32[48,32]{0,1:T(8,128)S(1)}, f32[48,32]{0,1:T(8,128)}, u32[]{:S(2)}) copy-start(f32[48,32]{0,1:T(8,128)} %slice_reduce_fusion.5) | copy-start | bytes 18436
  85.5 25.4 %copy-start.24 = (f32[48,32]{0,1:T(8,128)S(1)}, f32[48,32]{0,1:T(8,128)}, u32[]{:S(2)}) copy-start(f32[48,32]{0,1:T(8,128)} %slice_reduce_fusion.6) | copy-start | bytes 18436
  85.5 25.4 %copy-start.30 = (f32[48,32]{0,1:T(8,128)S(1)}, f32[48,32]{0,1:T(8,128)}, u32[]{:S(2)}) copy-start(f32[48,32]{0,1:T(8,128)} %copy-done.29) | copy-start | bytes 18436
  86.7 13.9 %collective-permute-start.4 = (f32[8,1,128]{1,0,2:T(8,128)S(1)}, f32[8,1,128]{1,0,2:T(8,128)S(1)}, u32[]{:S(2)}, u32[]{:S(2)}) collective-permute-start(f32[8,1,128]{1,0,2:T(8,128)S(1)} %get-tuple-element.25), channel_id=1, source_target_pairs={{0,8},{8,16},{16,24},{1,9},{9,17},{17,25},{2,10},{10,18},{18,26},{... | collective-permute-start | bytes 12296 | tf_op jit(solution)/shard_map/ppermute | solution.py:20
  90.3 15.1 %collective-permute-start.5 = (f32[8,1,128]{1,0,2:T(8,128)S(1)}, f32[8,1,128]{1,0,2:T(8,128)S(1)}, u32[]{:S(2)}, u32[]{:S(2)}) collective-permute-start(f32[8,1,128]{1,0,2:T(8,128)S(1)} %get-tuple-element.26), channel_id=1, source_target_pairs={{8,0},{16,8},{24,16},{9,1},{17,9},{25,17},{10,2},{18,10},{26,18},{... | collective-permute-start | bytes 12296 | tf_op jit(solution)/shard_map/ppermute | solution.py:23
  106.2 8.8 %collective-permute-start.6 = (f32[8,194,1]{1,0,2:T(8,128)S(1)}, f32[8,194,1]{1,0,2:T(8,128)S(1)}, u32[]{:S(2)}, u32[]{:S(2)}) collective-permute-start(f32[8,194,1]{1,0,2:T(8,128)S(1)} %get-tuple-element.23), channel_id=1, source_target_pairs={{0,1},{1,2},{2,3},{3,4},{4,5},{5,6},{6,7},{8,9},{9,10},{10,11},{11... | collective-permute-start | bytes 18632 | tf_op jit(solution)/shard_map/ppermute | solution.py:20
  109.5 6.0 %collective-permute-start.7 = (f32[8,194,1]{1,0,2:T(8,128)S(1)}, f32[8,194,1]{1,0,2:T(8,128)S(1)}, u32[]{:S(2)}, u32[]{:S(2)}) collective-permute-start(f32[8,194,1]{1,0,2:T(8,128)S(1)} %get-tuple-element.24), channel_id=1, source_target_pairs={{1,0},{2,1},{3,2},{4,3},{5,4},{6,5},{7,6},{9,8},{10,9},{11,10},{12... | collective-permute-start | bytes 18632 | tf_op jit(solution)/shard_map/ppermute | solution.py:23
  143.5 7.5 %collective-permute-start.8 = (f32[8,1,64]{1,2,0:T(8,128)S(1)}, f32[8,1,64]{1,2,0:T(8,128)S(1)}, u32[]{:S(2)}, u32[]{:S(2)}) collective-permute-start(f32[8,1,64]{1,2,0:T(8,128)S(1)} %get-tuple-element.33), channel_id=1, source_target_pairs={{0,8},{8,16},{16,24},{1,9},{9,17},{17,25},{2,10},{10,18},{18,26},{... | collective-permute-start | bytes 6152 | tf_op jit(solution)/shard_map/ppermute | solution.py:20
  146.9 8.7 %collective-permute-start.9 = (f32[8,1,64]{1,2,0:T(8,128)S(1)}, f32[8,1,64]{1,2,0:T(8,128)S(1)}, u32[]{:S(2)}, u32[]{:S(2)}) collective-permute-start(f32[8,1,64]{1,2,0:T(8,128)S(1)} %get-tuple-element.34), channel_id=1, source_target_pairs={{8,0},{16,8},{24,16},{9,1},{17,9},{25,17},{10,2},{18,10},{26,18},{... | collective-permute-start | bytes 6152 | tf_op jit(solution)/shard_map/ppermute | solution.py:23
  155.8 7.1 %collective-permute-start.10 = (f32[8,98,1]{1,2,0:T(1,128)S(1)}, f32[8,98,1]{1,2,0:T(1,128)S(1)}, u32[]{:S(2)}, u32[]{:S(2)}) collective-permute-start(f32[8,98,1]{1,2,0:T(1,128)S(1)} %get-tuple-element.27), channel_id=1, source_target_pairs={{0,1},{1,2},{2,3},{3,4},{4,5},{5,6},{6,7},{8,9},{9,10},{10,11},{11... | collective-permute-start | bytes 9416 | tf_op jit(solution)/shard_map/ppermute | solution.py:20
  159.8 6.7 %collective-permute-start.11 = (f32[8,98,1]{1,2,0:T(1,128)S(1)}, f32[8,98,1]{1,2,0:T(1,128)S(1)}, u32[]{:S(2)}, u32[]{:S(2)}) collective-permute-start(f32[8,98,1]{1,2,0:T(1,128)S(1)} %get-tuple-element.28), channel_id=1, source_target_pairs={{1,0},{2,1},{3,2},{4,3},{5,4},{6,5},{7,6},{9,8},{10,9},{11,10},{12... | collective-permute-start | bytes 9416 | tf_op jit(solution)/shard_map/ppermute | solution.py:23
  178.0 5.5 collective-permute-start.12
  180.2 7.1 %collective-permute-start.13 = (f32[8,1,32]{1,2,0:T(8,128)S(1)}, f32[8,1,32]{1,2,0:T(8,128)S(1)}, u32[]{:S(2)}, u32[]{:S(2)}) collective-permute-start(f32[8,1,32]{1,2,0:T(8,128)S(1)} %get-tuple-element.95), channel_id=1, source_target_pairs={{8,0},{16,8},{24,16},{9,1},{17,9},{25,17},{10,2},{18,10},{26,18},{... | collective-permute-start | bytes 3080 | tf_op jit(solution)/shard_map/ppermute | solution.py:23
  187.4 5.7 %collective-permute-start.14 = (f32[8,50,1]{1,2,0:T(1,128)S(1)}, f32[8,50,1]{1,2,0:T(1,128)S(1)}, u32[]{:S(2)}, u32[]{:S(2)}) collective-permute-start(f32[8,50,1]{1,2,0:T(1,128)S(1)} %get-tuple-element.31), channel_id=1, source_target_pairs={{0,1},{1,2},{2,3},{3,4},{4,5},{5,6},{6,7},{8,9},{9,10},{10,11},{11... | collective-permute-start | bytes 4808 | tf_op jit(solution)/shard_map/ppermute | solution.py:20
  190.3 5.3 collective-permute-start.15
  197.7 6.4 %collective-permute-start.16 = (f32[13,24,16]{0,2,1:T(8,128)S(1)}, f32[13,24,16]{0,2,1:T(8,128)S(1)}, u32[]{:S(2)}, u32[]{:S(2)}) collective-permute-start(f32[13,24,16]{0,2,1:T(8,128)S(1)} %concatenate.161), channel_id=1, source_target_pairs={{0,8},{8,0},{16,24},{24,16},{1,9},{9,1},{17,25},{25,17},{2,10},{10... | collective-permute-start | bytes 59912 | tf_op jit(solution)/shard_map/ppermute | solution.py:35
  204.5 2.2 collective-permute-start.17
  207.0 11.3 %collective-permute-start.18 = (f32[8,1,32]{1,2,0:T(8,128)S(1)}, f32[8,1,32]{1,2,0:T(8,128)S(1)}, u32[]{:S(2)}, u32[]{:S(2)}) collective-permute-start(f32[8,1,32]{1,2,0:T(8,128)S(1)} %get-tuple-element.93), channel_id=1, source_target_pairs={{0,16},{8,24},{1,17},{9,25},{2,18},{10,26},{3,19},{11,27},{4,20},{... | collective-permute-start | bytes 3080 | tf_op jit(solution)/shard_map/ppermute | solution.py:31
  208.4 11.0 %collective-permute-start.19 = (f32[8,1,32]{1,2,0:T(8,128)S(1)}, f32[8,1,32]{1,2,0:T(8,128)S(1)}, u32[]{:S(2)}, u32[]{:S(2)}) collective-permute-start(f32[8,1,32]{1,2,0:T(8,128)S(1)} %get-tuple-element.92), channel_id=1, source_target_pairs={{16,0},{24,8},{17,1},{25,9},{18,2},{26,10},{19,3},{27,11},{20,4},{... | collective-permute-start | bytes 3080 | tf_op jit(solution)/shard_map/ppermute | solution.py:31
  209.7 9.7 %collective-permute-start.20 = (f32[8,48,1]{1,2,0:T(1,128)S(1)}, f32[8,48,1]{1,2,0:T(1,128)S(1)}, u32[]{:S(2)}, u32[]{:S(2)}) collective-permute-start(f32[8,48,1]{1,2,0:T(1,128)S(1)} %get-tuple-element.89), channel_id=1, source_target_pairs={{0,2},{1,3},{2,4},{3,5},{4,6},{5,7},{8,10},{9,11},{10,12},{11,13},... | collective-permute-start | bytes 4616 | tf_op jit(solution)/shard_map/ppermute | solution.py:31
  214.2 5.5 collective-permute-start.21
  221.6 11.2 %collective-permute-start.22 = (f32[13,24,16]{0,2,1:T(8,128)S(1)}, f32[13,24,16]{0,2,1:T(8,128)S(1)}, u32[]{:S(2)}, u32[]{:S(2)}) collective-permute-start(f32[13,24,16]{0,2,1:T(8,128)S(1)} %concatenate.170), channel_id=1, source_target_pairs={{0,16},{8,24},{16,0},{24,8},{1,17},{9,25},{17,1},{25,9},{2,18},{10... | collective-permute-start | bytes 59912 | tf_op jit(solution)/shard_map/ppermute | solution.py:35
  233.1 5.4 collective-permute-start.23
  238.8 6.0 %collective-permute-start.24 = (f32[8,1,32]{1,2,0:T(8,128)S(1)}, f32[8,1,32]{1,2,0:T(8,128)S(1)}, u32[]{:S(2)}, u32[]{:S(2)}) collective-permute-start(f32[8,1,32]{1,2,0:T(8,128)S(1)} %get-tuple-element.40), channel_id=1, source_target_pairs={} | collective-permute-start | bytes 3080 | tf_op jit(solution)/shard_map/ppermute | solution.py:31
  239.4 5.4 collective-permute-start.25
  240.1 4.7 collective-permute-start.26
  243.5 5.5 collective-permute-start.27
  327.8 6.8 %collective-permute-start.28 = (f32[8,1,32]{1,2,0:T(8,128)S(1)}, f32[8,1,32]{1,2,0:T(8,128)S(1)}, u32[]{:S(2)}, u32[]{:S(2)}) collective-permute-start(f32[8,1,32]{1,2,0:T(8,128)S(1)} %get-tuple-element.78), channel_id=1, source_target_pairs={} | collective-permute-start | bytes 3080 | tf_op jit(solution)/shard_map/ppermute | solution.py:31
  328.5 6.2 %collective-permute-start.29 = (f32[8,1,32]{1,2,0:T(8,128)S(1)}, f32[8,1,32]{1,2,0:T(8,128)S(1)}, u32[]{:S(2)}, u32[]{:S(2)}) collective-permute-start(f32[8,1,32]{1,2,0:T(8,128)S(1)} %get-tuple-element.79), channel_id=1, source_target_pairs={} | collective-permute-start | bytes 3080 | tf_op jit(solution)/shard_map/ppermute | solution.py:31
  329.2 5.5 collective-permute-start.30
  333.3 5.5 collective-permute-start.31
  419.2 6.8 %collective-permute-start.32 = (f32[8,1,32]{1,2,0:T(8,128)S(1)}, f32[8,1,32]{1,2,0:T(8,128)S(1)}, u32[]{:S(2)}, u32[]{:S(2)}) collective-permute-start(f32[8,1,32]{1,2,0:T(8,128)S(1)} %get-tuple-element.70), channel_id=1, source_target_pairs={} | collective-permute-start | bytes 3080 | tf_op jit(solution)/shard_map/ppermute | solution.py:31
  419.8 6.2 %collective-permute-start.33 = (f32[8,1,32]{1,2,0:T(8,128)S(1)}, f32[8,1,32]{1,2,0:T(8,128)S(1)}, u32[]{:S(2)}, u32[]{:S(2)}) collective-permute-start(f32[8,1,32]{1,2,0:T(8,128)S(1)} %get-tuple-element.71), channel_id=1, source_target_pairs={} | collective-permute-start | bytes 3080 | tf_op jit(solution)/shard_map/ppermute | solution.py:31
  420.5 5.5 collective-permute-start.34
  424.7 5.5 collective-permute-start.35
  509.0 6.9 %collective-permute-start.36 = (f32[8,1,32]{1,2,0:T(8,128)S(1)}, f32[8,1,32]{1,2,0:T(8,128)S(1)}, u32[]{:S(2)}, u32[]{:S(2)}) collective-permute-start(f32[8,1,32]{1,2,0:T(8,128)S(1)} %get-tuple-element.69), channel_id=1, source_target_pairs={} | collective-permute-start | bytes 3080 | tf_op jit(solution)/shard_map/ppermute | solution.py:31
  509.7 6.3 %collective-permute-start.37 = (f32[8,1,32]{1,2,0:T(8,128)S(1)}, f32[8,1,32]{1,2,0:T(8,128)S(1)}, u32[]{:S(2)}, u32[]{:S(2)}) collective-permute-start(f32[8,1,32]{1,2,0:T(8,128)S(1)} %get-tuple-element.68), channel_id=1, source_target_pairs={} | collective-permute-start | bytes 3080 | tf_op jit(solution)/shard_map/ppermute | solution.py:31
  510.4 5.6 collective-permute-start.38
  514.6 5.5 collective-permute-start.39
  (25 other events, 306.2 us)
where the time goes:
time: 573 us; the launch traced here: 562 us
  blocking collectives  273 us (48%)
  starting transfers between devices  78.8 us (14%)
  local copies, waits for them, and re-layouts  78.5 us (14%)
  waiting for transfers between devices  67.7 us (12%)
  other arithmetic  62.1 us (11%)
    psum x4, blocking collectives, norm_sum(): return lax.psum(local_dot(values, values), ('row', 'col'))  160 us
    psum x3, blocking collectives, coarse_solve(): step_size = norm_now / lax.psum(local_dot(direction, image), ('row', 'col'))  113 us
    ppermute x20, starting transfers between devices, shifted(): return lax.ppermute(block, axis, route)  35 us
    ppermute x8, starting transfers between devices, padded_2(): lax.ppermute(lax.slice_in_dim(block, block.shape[dim] - width, None, axis...  25.6 us
    ppermute x8, waiting for transfers between devices, padded_2(): lax.ppermute(lax.slice_in_dim(block, 0, width, axis=dim), axis, backward)  23 us
    reduce_sum x4, other arithmetic, restrict_field(): values.reshape(count, rows_here // 2, 2, cols_here // 2, 2).sum(axis=(2, 4))  19.1 us
    ppermute x20, waiting for transfers between devices, shifted(): return lax.ppermute(block, axis, route)  18 us
    ppermute x4, waiting for transfers between devices, partner_2(): lax.ppermute(shard, axis, [(i, i ^ 1 << apart) for i in range(lax.axis_si...  17.4 us
  transfers between devices with their start and end apart: 40, of which 19 were waited for; matrix products, arithmetic and copies ran while one was open for 6% of the time, Pallas kernels for 0%

commit v1 on v0

v1 whole, which is shorter than its diff:
```python
import functools

import jax
import jax.numpy as jnp
from jax import lax
from jax.experimental import pallas as pl
from jax.experimental.pallas import tpu as pltpu
from jax.sharding import PartitionSpec as P

RHS = 8
ITERS = 4
OMEGA = 0.8
HALO = 16
LANES = 128
F32 = jnp.float32
BF16 = jnp.bfloat16
PIECES = 3


def iota(shape, dim):
    return lax.broadcasted_iota(jnp.int32, shape, dim)


def selection(rows, test):
    shape = (rows, LANES)
    return jnp.where(test(iota(shape, 0), iota(shape, 1)), 1.0, 0.0).astype(BF16)


def dot01(values, matrix, pieces=PIECES):
    total = None
    for piece in range(pieces):
        part = values.astype(BF16)
        term = jnp.dot(part, matrix, preferred_element_type=F32)
        total = term if total is None else total + term
        if piece + 1 < pieces:
            values = values - part.astype(F32)
    return total


def rot(values, shift, axis):
    return pltpu.roll(values, shift % values.shape[axis], axis)


def lanes_of(values, lane):
    return iota(values.shape, 1) if lane is None else lane


def pack_rows_kernel(res_ref, ground_ref, nodata_ref, patch_ref, down_ref, up_ref):
    rows = res_ref.shape[0]
    for out_ref, start in ((down_ref, rows - HALO), (up_ref, 0)):
        part = pl.ds(start, HALO)
        out_ref[0:HALO] = res_ref[part]
        out_ref[HALO : 2 * HALO] = ground_ref[part]
        out_ref[2 * HALO : 3 * HALO] = jnp.where(nodata_ref[part] == 0, 1.0, 0.0)
        out_ref[3 * HALO : 4 * HALO] = patch_ref[part].astype(F32)


def tall_halves(own_refs, above_ref, below_ref):
    res_ref, ground_ref, nodata_ref, patch_ref = own_refs
    own = [
        res_ref[...],
        ground_ref[...],
        jnp.where(nodata_ref[...] == 0, 1.0, 0.0),
        patch_ref[...].astype(F32),
    ]
    half = own[0].shape[0] // 2
    tall = []
    for which, values in enumerate(own):
        part = pl.ds(which * HALO, HALO)
        tall.append(
            (
                jnp.concatenate([above_ref[part], values[:half]], axis=0),
                jnp.concatenate([values[half:], below_ref[part]], axis=0),
            )
        )
    return tall


def pack_cols_kernel(res_ref, ground_ref, nodata_ref, patch_ref, above_ref, below_ref, right_ref, left_ref):
    tall = tall_halves((res_ref, ground_ref, nodata_ref, patch_ref), above_ref, below_ref)
    shape = right_ref.shape
    group_of = iota(shape, 1) // HALO
    to_right = jnp.zeros(shape, F32)
    to_left = jnp.zeros(shape, F32)
    for which in range(4):
        for side in range(2):
            group = 2 * which + side
            values = tall[which][side]
            here = group_of == group
            to_right = jnp.where(here, rot(values, HALO * group + HALO, 1), to_right)
            to_left = jnp.where(here, rot(values, HALO * group, 1), to_left)
    right_ref[...] = to_right
    left_ref[...] = to_left


def link(resist, validity, near_resist, near_valid):
    return (validity * near_valid) * (2.0 / (resist + near_resist))


def weights_of(diag):
    return OMEGA / jnp.where(diag > 0, diag, 1.0)


def down_kernel(
    res_ref,
    ground_ref,
    nodata_ref,
    patch_ref,
    above_ref,
    below_ref,
    left_ref,
    right_ref,
    payload_ref,
    t1_ref,
    w0_ref,
    ext_ref,
    r1_ref,
    r2_ref,
    r3_ref,
    c1_ref,
    c2_ref,
    c3_ref,
    t3_ref,
    t2_ref,
):
    devices = payload_ref.shape[0]
    tall = tall_halves((res_ref, ground_ref, nodata_ref, patch_ref), above_ref, below_ref)
    quarter = tall[0][0].shape[0]
    lane = iota((quarter, LANES), 1)
    from_left = left_ref[...]
    from_right = right_ref[...]
    for which in range(4):
        for side in range(2):
            group = 2 * which + side
            moved = rot(tall[which][side], HALO, 1)
            tile0 = jnp.where(lane < HALO, rot(from_left, -HALO * group, 1), moved)
            tile1 = jnp.where(
                lane < HALO,
                moved,
                jnp.where(lane < 2 * HALO, rot(from_right, HALO - HALO * group, 1), 0.0),
            )
            if which < 2:
                tile0 = jnp.where(tile0 > 0, tile0, 1.0)
                tile1 = jnp.where(tile1 > 0, tile1, 1.0)
            ext_ref[2 * which, pl.ds(side * quarter, quarter), :] = tile0
            ext_ref[2 * which + 1, pl.ds(side * quarter, quarter), :] = tile1

    n1 = quarter
    odd = lane % 2 == 1

    def parity(which, start):
        return [ext_ref[2 * which + tile, pl.ds(start, n1, stride=2), :] for tile in range(2)]

    res_e, res_o = parity(0, 0), parity(0, 1)
    g_e, g_o = parity(1, 0), parity(1, 1)
    v_e, v_o = parity(2, 0), parity(2, 1)
    p_e, p_o = parity(3, 0), parity(3, 1)

    def left_of(pair):
        first, second = rot(pair[0], 1, 1), rot(pair[1], 1, 1)
        return [first, jnp.where(lane == 0, first, second)]

    def right_of(pair):
        first, second = rot(pair[0], -1, 1), rot(pair[1], -1, 1)
        return [jnp.where(lane == LANES - 1, second, first), second]

    west = {}
    for name, res, val in (("e", res_e, v_e), ("o", res_o, v_o)):
        near_res, near_val = left_of(res), left_of(val)
        west[name] = [link(res[t], val[t], near_res[t], near_val[t]) for t in range(2)]
    east = {name: right_of(pair) for name, pair in west.items()}
    level = []
    coarse = []
    for t in range(2):
        v_in = link(res_e[t], v_e[t], res_o[t], v_o[t])
        v_up = link(res_e[t], v_e[t], rot(res_o[t], 1, 0), rot(v_o[t], 1, 0))
        v_dn = rot(v_up, -1, 0)
        we, wo, ee, eo = west["e"][t], west["o"][t], east["e"][t], east["o"][t]
        w_e = weights_of(g_e[t] + v_up + v_in + we + ee)
        w_o = weights_of(g_o[t] + v_in + v_dn + wo + eo)
        a_e = (1.0 - OMEGA) * v_e[t] + w_e * (v_in + jnp.where(odd, we, ee))
        a_o = (1.0 - OMEGA) * v_o[t] + w_o * (v_in + jnp.where(odd, wo, eo))
        b_e = w_e * jnp.where(odd, ee, we)
        b_o = w_o * jnp.where(odd, eo, wo)
        c_e = rot(w_e * v_up, -1, 0)
        c_o = rot(w_o * v_dn, 1, 0)
        p_es = rot(p_e[t], -1, 0)
        p_os = rot(p_o[t], 1, 0)
        terms = []
        for patch, own, side in ((p_e[t], a_e, b_e), (p_o[t], a_o, b_o), (p_es, c_e, None), (p_os, c_o, None)):
            spread = jnp.where(patch > 0, -0.125, 0.0)
            entry = [patch, 0.875 * own, spread * own]
            if side is not None:
                entry += [0.875 * side, spread * side]
            terms.append(entry)
        level.append((terms, w_e * v_e[t], w_o * v_o[t]))
        coarse.append((g_e[t] + g_o[t], v_up, we + wo))
    own_rows = slice(HALO // 2, n1 - HALO // 2)
    for index in (1, 2):
        moved = jnp.where(lane < LANES - HALO, rot(level[0][index], -HALO, 1), rot(level[1][index], -HALO, 1))
        w0_ref[index - 1] = moved[own_rows]

    m_in = selection(2 * LANES, lambda x, j: x // 2 == j)
    m_out = selection(2 * LANES, lambda x, j: x // 2 + 2 * (x % 2) - 1 == j)
    m_even = selection(2 * LANES, lambda x, j: x == 2 * j)
    m_both = jnp.concatenate([m_in, m_out], axis=0)

    def wide(index):
        return jnp.concatenate([coarse[0][index], coarse[1][index]], axis=1)

    zeros = jnp.zeros((c1_ref.shape[1] - n1, LANES), F32)
    c1_ref[0, 0:n1] = dot01(wide(0), m_in)
    c1_ref[1, 0:n1] = dot01(wide(1), m_in)
    c1_ref[2, 0:n1] = dot01(wide(2), m_even)
    for index in range(3):
        c1_ref[index, n1:] = zeros
    for k in range(RHS):
        parts_a = []
        parts_b = []
        for t in range(2):
            terms = level[t][0]
            tests = [entry[0] == k + 1.0 for entry in terms]
            picked = [jnp.where(test, entry[1], entry[2]) for test, entry in zip(tests, terms)]
            parts_a.append((picked[0] + picked[1]) + (picked[2] + picked[3]))
            parts_b.append(
                jnp.where(tests[0], terms[0][3], terms[0][4]) + jnp.where(tests[1], terms[1][3], terms[1][4])
            )
        r1_ref[k, 0:n1] = dot01(jnp.concatenate(parts_a + parts_b, axis=1), m_both)
        r1_ref[k, n1:] = zeros

    k_in = m_in[:LANES]
    k_out = m_out[:LANES]
    k_even = m_even[:LANES]
    k_both = jnp.concatenate([k_in, k_out], axis=0)
    l_in = selection(LANES, lambda x, j: x // 2 - 1 == j % 8)
    l_out = selection(LANES, lambda x, j: x // 2 + 2 * (x % 2) - 2 == j % 8)
    l_even = selection(LANES, lambda x, j: (x // 2 - 1 == j % 8) & (x % 2 == 0))
    l_both = jnp.concatenate([l_in, l_out], axis=0)
    smooth = []
    for r_ref, c_ref, next_r, next_c in (
        (r1_ref, c1_ref, r2_ref, c2_ref),
        (r2_ref, c2_ref, r3_ref, c3_ref),
        (r3_ref, c3_ref, None, None),
    ):
        half = r_ref.shape[1] // 2
        even, uneven = pl.ds(0, half, stride=2), pl.ds(1, half, stride=2)
        odd_lane = iota((half, LANES), 1) % 2 == 1
        ge, go = c_ref[0, even, :], c_ref[0, uneven, :]
        v_up, v_in = c_ref[1, even, :], c_ref[1, uneven, :]
        we, wo = c_ref[2, even, :], c_ref[2, uneven, :]
        ee, eo = rot(we, -1, 1), rot(wo, -1, 1)
        v_dn = rot(v_up, -1, 0)
        w_e = weights_of(ge + v_up + v_in + we + ee)
        w_o = weights_of(go + v_in + v_dn + wo + eo)
        a_e = (1.0 - OMEGA) + w_e * (v_in + jnp.where(odd_lane, we, ee))
        a_o = (1.0 - OMEGA) + w_o * (v_in + jnp.where(odd_lane, wo, eo))
        b_e = w_e * jnp.where(odd_lane, ee, we)
        b_o = w_o * jnp.where(odd_lane, eo, wo)
        c_e = w_e * v_up
        c_o = w_o * v_dn
        smooth.append((w_e, w_o))
        both, inner, evens = (k_both, k_in, k_even) if next_r is not None else (l_both, l_in, l_even)
        coarser = [dot01(ge + go, inner), dot01(v_up, inner), dot01(we + wo, evens)]
        fields = []
        for k in range(RHS):
            re, ro = r_ref[k, even, :], r_ref[k, uneven, :]
            own = a_e * re + a_o * ro + rot(c_o * ro, 1, 0) + rot(c_e * re, -1, 0)
            side = b_e * re + b_o * ro
            fields.append(dot01(jnp.concatenate([own, side], axis=1), both))
        if next_r is not None:
            for index in range(3):
                next_c[index] = coarser[index]
            for k in range(RHS):
                next_r[k] = fields[k]

    shape = fields[0].shape
    mine = iota(shape, 1) // 8 == iota(shape, 0) - 1

    def flat(field):
        return jnp.sum(jnp.where(mine, field, 0.0), axis=0, keepdims=True)

    sub = iota((8, LANES), 0)
    lane8 = iota((8, LANES), 1)
    links = jnp.where(sub < 4, flat(coarser[1]), flat(coarser[2]))
    turned = rot(links, 96, 1)
    for row in (1, 2):
        turned = jnp.where(sub % 4 == row, rot(links, 96 - 32 * row, 1), turned)
    tile = jnp.broadcast_to(flat(coarser[0]), (8, LANES))
    for k in range(RHS - 1):
        tile = jnp.where(sub == k, flat(fields[k]), tile)
    tile = jnp.where(lane8 < 96, tile, turned)

    @pl.loop(0, devices)
    def _(device):
        payload_ref[device] = tile

    spread = selection(LANES, lambda j, x: x // 2 == j)
    for k in range(RHS):
        w_e, w_o = smooth[2]
        half = w_e.shape[0]
        t3_ref[k, pl.ds(0, half, stride=2), :] = w_e * r3_ref[k, pl.ds(0, half, stride=2), :]
        t3_ref[k, pl.ds(1, half, stride=2), :] = w_o * r3_ref[k, pl.ds(1, half, stride=2), :]
    for k in range(RHS):
        w_e, w_o = smooth[1]
        half = w_e.shape[0]
        finer = dot01(t3_ref[k], spread)
        t2_ref[k, pl.ds(0, half, stride=2), :] = finer + w_e * r2_ref[k, pl.ds(0, half, stride=2), :]
        t2_ref[k, pl.ds(1, half, stride=2), :] = finer + w_o * r2_ref[k, pl.ds(1, half, stride=2), :]
    for k in range(RHS):
        w_e, w_o = smooth[0]
        half = w_e.shape[0]
        finer = dot01(t2_ref[k], spread)
        t1_ref[k, pl.ds(0, half, stride=2), :] = finer + w_e * r1_ref[k, pl.ds(0, half, stride=2), :]
        t1_ref[k, pl.ds(1, half, stride=2), :] = finer + w_o * r1_ref[k, pl.ds(1, half, stride=2), :]


def solve_kernel(grid, me_ref, all_ref, t1_ref, w0_ref, patch_ref, out_ref, coef_ref, x_ref, r_ref, p_ref, q_ref, u_ref):
    grid_rows, grid_cols = grid
    count = grid_rows * grid_cols
    lane = iota((8, LANES), 1)
    sub = iota((8, LANES), 0)
    inside = lane < 96

    def choose(test, yes, no):
        if isinstance(test, bool):
            return yes if test else no
        return jnp.where(test, yes, no)

    def every(body, init):
        if count <= 64:
            for tile in range(count):
                init = body(tile, init)
            return init
        return lax.fori_loop(0, count, body, init)

    def above(ref, t):
        return jnp.where(lane < 8, rot(ref[choose(t >= grid_cols, t - grid_cols, t)], 40, 1), rot(ref[t], 8, 1))

    def below(ref, t):
        near = ref[choose(t + grid_cols < count, t + grid_cols, t)]
        return jnp.where(lane >= 88, rot(near, 88, 1), rot(ref[t], 120, 1))

    def left(ref, t):
        near = ref[choose(t % grid_cols > 0, t - 1, t)]
        return jnp.where(lane % 8 == 0, rot(near, 121, 1), rot(ref[t], 1, 1))

    def right(ref, t):
        near = ref[choose(t % grid_cols < grid_cols - 1, t + 1, t)]
        return jnp.where(lane % 8 == 7, rot(near, 7, 1), rot(ref[t], 127, 1))

    def unpack(t, rr):
        tile = all_ref[t]
        known = jnp.where(inside & (sub < 7), tile, 0.0)
        rhs = jnp.where(sub < 7, known, -jnp.sum(known, axis=0, keepdims=True))
        r_ref[t] = rhs
        p_ref[t] = rhs
        coef_ref[0, t] = jnp.where(inside, jnp.broadcast_to(tile[7:8], (8, LANES)), 0.0)
        turned = jnp.zeros((8, LANES), F32)
        for row in range(3):
            turned = jnp.where((sub % 4 == row) & (lane // 32 == row), rot(tile, 32 * row + 32, 1), turned)
        north = jnp.sum(jnp.where(sub < 4, turned, 0.0), axis=0, keepdims=True)
        west = jnp.sum(jnp.where(sub < 4, 0.0, turned), axis=0, keepdims=True)
        coef_ref[1, t] = jnp.broadcast_to(north, (8, LANES))
        coef_ref[3, t] = jnp.broadcast_to(west, (8, LANES))
        return rr + rhs * rhs

    def total(values):
        return jnp.sum(values, axis=1, keepdims=True)

    zero = jnp.zeros((8, LANES), F32)
    rr = total(every(unpack, zero))

    def finish(t, carry):
        south = below(coef_ref.at[1], t)
        bottom = choose(t + grid_cols < count, 1.0, 0.0)
        south = jnp.where(lane < 88, south, jnp.where(inside, south * bottom, 0.0))
        east = right(coef_ref.at[3], t)
        last = choose(t % grid_cols < grid_cols - 1, 1.0, 0.0)
        east = jnp.where(inside, jnp.where(lane % 8 == 7, east * last, east), 0.0)
        coef_ref[2, t] = south
        coef_ref[4, t] = east
        coef_ref[0, t] = coef_ref[0, t] + coef_ref[1, t] + south + coef_ref[3, t] + east
        return carry

    every(finish, 0)

    def image_of(t, dot):
        here = p_ref[t]
        pulled = coef_ref[1, t] * above(p_ref, t) + coef_ref[2, t] * below(p_ref, t)
        pulled = pulled + coef_ref[3, t] * left(p_ref, t) + coef_ref[4, t] * right(p_ref, t)
        image = coef_ref[0, t] * here - pulled
        q_ref[t] = image
        return dot + here * image

    for sweep in range(ITERS):
        step = jnp.broadcast_to(rr / total(every(image_of, zero)), (8, LANES))

        def advance(t, norm):
            gain = step * p_ref[t]
            x_ref[t] = gain if sweep == 0 else x_ref[t] + gain
            if sweep + 1 == ITERS:
                return norm
            left_over = r_ref[t] - step * q_ref[t]
            r_ref[t] = left_over
            return norm + left_over * left_over

        norm = every(advance, zero)
        if sweep + 1 < ITERS:
            new = total(norm)
            ratio = jnp.broadcast_to(new / rr, (8, LANES))
            rr = new

            def turn(t, carry):
                p_ref[t] = r_ref[t] + ratio * p_ref[t]
                return carry

            every(turn, 0)

    mine = x_ref[me_ref[0]]
    groups = u_ref.shape[0] // 8
    stacked = jnp.concatenate([jnp.where(lane // 8 == i, mine, 0.0) for i in range(groups)], axis=0)
    widen = selection(LANES, lambda x, j: (j >= 8) & (j < 72) & (x % 8 == (j - 8) // 8))
    u_ref[...] = dot01(stacked, widen)
    spread = selection(LANES, lambda j, x: j == x // 2 + 8)
    half = w0_ref.shape[1]
    even, uneven = pl.ds(0, half, stride=2), pl.ds(1, half, stride=2)
    sides = []
    for index, rows in ((0, even), (1, uneven)):
        weight = w0_ref[index]
        patch = patch_ref[rows, :]
        sides.append((rows, patch, 0.875 * weight, jnp.where(patch > 0, -0.125, 0.0) * weight))
    for k in range(RHS):
        coarse = jnp.concatenate(
            [t1_ref[k, pl.ds(8 * i + 8, 8), :] + u_ref[pl.ds(8 * i + k, 1), :] for i in range(groups)], axis=0
        )
        finer = dot01(coarse, spread)
        for rows, patch, chosen, other in sides:
            out_ref[k, rows, :] = finer + jnp.where(patch == k + 1, chosen, other)


def shifted(block, axis, distance):
    devices = range(lax.axis_size(axis))
    return lax.ppermute(block, axis, [(i, i + distance) for i in devices if i + distance in devices])


def shards(resistance, ground, nodata, patch_ids):
    grid = (lax.axis_size("row"), lax.axis_size("col"))
    devices = grid[0] * grid[1]
    rows, cols = resistance.shape
    own = (resistance, ground, nodata, patch_ids)
    shape = jax.ShapeDtypeStruct
    strip = shape((4 * HALO, cols), F32)
    down, up = pl.pallas_call(pack_rows_kernel, out_shape=(strip, strip), name="pack_rows")(*own)
    above = shifted(down, "row", 1)
    below = shifted(up, "row", -1)
    tall = rows + 2 * HALO
    strip = shape((tall // 2, LANES), F32)
    to_right, to_left = pl.pallas_call(pack_cols_kernel, out_shape=(strip, strip), name="pack_cols")(
        *own, above, below
    )
    left = shifted(to_right, "col", 1)
    right = shifted(to_left, "col", -1)
    sizes = [128, 64, 32]
    payload, t1, w0 = pl.pallas_call(
        down_kernel,
        out_shape=(
            shape((devices, 8, LANES), F32),
            shape((RHS, sizes[0], LANES), F32),
            shape((2, rows // 2, LANES), F32),
        ),
        scratch_shapes=[pltpu.VMEM((8, tall, LANES), F32)]
        + [pltpu.VMEM((RHS, size, LANES), F32) for size in sizes]
        + [pltpu.VMEM((3, size, LANES), F32) for size in sizes]
        + [pltpu.VMEM((RHS, size, LANES), F32) for size in sizes[:0:-1]],
        name="down",
    )(*own, above, below, left, right)
    everything = lax.all_to_all(payload, ("row", "col"), 0, 0)
    me = (lax.axis_index("row") * grid[1] + lax.axis_index("col")).reshape(1).astype(jnp.int32)
    field = pltpu.VMEM((devices, 8, LANES), F32)
    vmem = pl.BlockSpec(memory_space=pltpu.VMEM)
    return pl.pallas_call(
        functools.partial(solve_kernel, grid),
        out_shape=shape((RHS, rows, cols), F32),
        in_specs=[pl.BlockSpec(memory_space=pltpu.SMEM)] + [vmem] * 4,
        scratch_shapes=[pltpu.VMEM((5, devices, 8, LANES), F32)]
        + [field] * 4
        + [pltpu.VMEM((rows // 16 * 8, LANES), F32)],
        name="solve",
    )(me, everything, t1, w0, patch_ids)


def solution(mesh):
    spec = P("row", "col")
    return jax.shard_map(shards, mesh=mesh, in_specs=(spec,) * 4, out_specs=P(None, "row", "col"), check_vma=False)
```

time: 573 us -> 49.2 us (0.09); the launches traced: 562 us -> 48.9 us
  blocking collectives: 273 us -> 0 us
  local copies, waits for them, and re-layouts: 78.5 us -> 1.9 us
  starting transfers between devices: 78.8 us -> 16.1 us
  other arithmetic: 62.1 us -> 0 us
  waiting for transfers between devices: 67.7 us -> 16.7 us
  Pallas kernels: 0 us -> 14.2 us
    psum x7 -> x0, blocking collectives: 273 us -> none  [the longest x4 160 us: norm_sum(): return lax.psum(local_dot(values, values), ('row', 'col'))]
    ppermute x40 -> x4, starting transfers between devices: 78.8 us -> 8.81 us  [shifted(): lax.ppermute(block, axis, [(i, i + distance) for i in devices if i + dist...]
    ppermute x40 -> x4, waiting for transfers between devices: 67.7 us -> 8.47 us  [shifted(): lax.ppermute(block, axis, [(i, i + distance) for i in devices if i + dist...]
    squeeze x21 -> x0, local copies, waits for them, and re-layouts: 47.5 us -> none  [the longest x4 10.2 us: coarse_coeffs(): north_link = blocks[1][:, 0].sum(axis=-1)]
    reduce_sum x29 -> x0, other arithmetic: 44.7 us -> none  [the longest x4 19.1 us: restrict_field(): values.reshape(count, rows_here // 2, 2, cols_here // 2, 2).sum(axis=(2, 4))]
    pallas_call x0 -> x4, Pallas kernels: none -> 14.2 us  [the longest x1 5.78 us: shards(): pl.pallas_call(down_kernel, out_shape=(shape((devices, 8, LANES), F32), s...]
    sub x4 -> x0, local copies, waits for them, and re-layouts: 12.2 us -> none  [descend(): remainder = residual - apply_operator(smoothed, coeffs, sides_of(smoothed))]
    all_to_all x0 -> x1, waiting for transfers between devices: none -> 8.2 us  [shards(): everything = lax.all_to_all(payload, ('row', 'col'), 0, 0)]
  transfers between devices with their start and end apart: 40 -> 5, of which waited for: 19 -> 4; matrix products, arithmetic and copies ran while one was open for 6% -> 0% of each run, Pallas kernels for 0% -> 0%
where the time goes in v1:
time: 49.2 us; the launch traced here: 48.9 us
  waiting for transfers between devices  16.7 us (34%)
  starting transfers between devices  16.1 us (33%)
  Pallas kernels  14.2 us (29%)
  local copies, waits for them, and re-layouts  1.9 us (4%)
    ppermute x4, starting transfers between devices, shifted(): lax.ppermute(block, axis, [(i, i + distance) for i in devices if i + dist...  8.81 us
    ppermute x4, waiting for transfers between devices, shifted(): lax.ppermute(block, axis, [(i, i + distance) for i in devices if i + dist...  8.47 us
    all_to_all x1, waiting for transfers between devices, shards(): everything = lax.all_to_all(payload, ('row', 'col'), 0, 0)  8.2 us
    all_to_all x1, starting transfers between devices, shards(): everything = lax.all_to_all(payload, ('row', 'col'), 0, 0)  7.25 us
    pallas_call x1, Pallas kernels, shards(): pl.pallas_call(down_kernel, out_shape=(shape((devices, 8, LANES), F32), s...  5.78 us
    pallas_call x1, Pallas kernels, shards(): pl.pallas_call(functools.partial(solve_kernel, grid), out_shape=shape((RH...  4.85 us
    pallas_call x1, Pallas kernels, shards(): pl.pallas_call(pack_cols_kernel, out_shape=(strip, strip), name='pack_cols')  1.9 us
    unnamed x10, local copies, waits for them, and re-layouts  1.9 us
  transfers between devices with their start and end apart: 5, of which 4 were waited for; matrix products, arithmetic and copies ran while one was open for 0% of the time, Pallas kernels for 0%

profile of v1, /device:TPU:0, one launch (start us, length us, event | category | flops | bytes accessed | tf_op | source)
XLA Modules:
  0.0 48.9 jit_solution(16648141139173137017)
XLA Ops:
  0.0 1.7 %pack_rows.1 = (f32[64,128]{1,0:T(8,128)}, f32[64,128]{1,0:T(8,128)}) custom-call(f32[192,128]{1,0:T(8,128)} %res_ref.5, f32[192,128]{1,0:T(8,128)} %ground_ref.5, s32[192,128]{1,0:T(8,128)} %nodata_ref.5, s32[192,128]{1,0:T(8,128)} %patch_ref.7), custom_call_target="tpu_custom_call" | custom-call | tf_op jit(solution)/shard_map/pack_rows/pallas_call | solution.py:453
  1.7 4.9 %collective-permute-start = (f32[64,128]{1,0:T(8,128)}, f32[64,128]{1,0:T(8,128)S(1)}, u32[]{:S(2)}, u32[]{:S(2)}) collective-permute-start(f32[64,128]{1,0:T(8,128)} %get-tuple-element.12), channel_id=1, source_target_pairs={{0,8},{8,16},{16,24},{1,9},{9,17},{17,25},{2,10},{10,18},{18,26},{... | collective-permute-start | bytes 98312 | tf_op jit(solution)/shard_map/ppermute | solution.py:443
  6.6 1.3 %collective-permute-start.1 = (f32[64,128]{1,0:T(8,128)}, f32[64,128]{1,0:T(8,128)S(1)}, u32[]{:S(2)}, u32[]{:S(2)}) collective-permute-start(f32[64,128]{1,0:T(8,128)} %get-tuple-element.13), channel_id=1, source_target_pairs={{8,0},{16,8},{24,16},{9,1},{17,9},{25,17},{10,2},{18,10},{26,18},{... | collective-permute-start | bytes 98312 | tf_op jit(solution)/shard_map/ppermute | solution.py:443
  7.9 0.6 %collective-permute-done.above_ref = f32[64,128]{1,0:T(8,128)S(1)} collective-permute-done((f32[64,128]{1,0:T(8,128)}, f32[64,128]{1,0:T(8,128)S(1)}, u32[]{:S(2)}, u32[]{:S(2)}) %collective-permute-start) | collective-permute-done | bytes 32800 | tf_op jit(solution)/shard_map/ppermute | solution.py:443
  8.5 0.0 copy-start.1
  8.5 4.1 %collective-permute-done.1.below_ref = f32[64,128]{1,0:T(8,128)S(1)} collective-permute-done((f32[64,128]{1,0:T(8,128)}, f32[64,128]{1,0:T(8,128)S(1)}, u32[]{:S(2)}, u32[]{:S(2)}) %collective-permute-start.1) | collective-permute-done | bytes 32800 | tf_op jit(solution)/shard_map/ppermute | solution.py:443
  12.6 0.0 copy-done.1
  12.6 0.0 copy-start.2
  12.6 0.6 %copy-done.2 = f32[64,128]{1,0:T(8,128)} copy-done((f32[64,128]{1,0:T(8,128)}, f32[64,128]{1,0:T(8,128)S(1)}, u32[]{:S(2)}) %copy-start.2) | copy-done | bytes 32792
  13.2 1.9 %pack_cols.1 = (f32[112,128]{1,0:T(8,128)}, f32[112,128]{1,0:T(8,128)}) custom-call(f32[192,128]{1,0:T(8,128)} %res_ref.5, f32[192,128]{1,0:T(8,128)} %ground_ref.5, s32[192,128]{1,0:T(8,128)} %nodata_ref.5, s32[192,128]{1,0:T(8,128)} %patch_ref.7, f32[64,128]{1,0:T(8,128)} %copy-done.1, f32[64,128]{1,0:T(8,128)} %copy-done.2), custom_call_target="tpu_custom_call" | custom-call | tf_op jit(solution)/shard_map/pack_cols/pallas_call | solution.py:458
  15.1 1.3 %collective-permute-start.2 = (f32[112,128]{1,0:T(8,128)}, f32[112,128]{1,0:T(8,128)S(1)}, u32[]{:S(2)}, u32[]{:S(2)}) collective-permute-start(f32[112,128]{1,0:T(8,128)} %get-tuple-element.14), channel_id=1, source_target_pairs={{0,1},{1,2},{2,3},{3,4},{4,5},{5,6},{6,7},{8,9},{9,10},{10,11},{11... | collective-permute-start | bytes 172040 | tf_op jit(solution)/shard_map/ppermute | solution.py:443
  16.4 1.3 %collective-permute-start.3 = (f32[112,128]{1,0:T(8,128)}, f32[112,128]{1,0:T(8,128)S(1)}, u32[]{:S(2)}, u32[]{:S(2)}) collective-permute-start(f32[112,128]{1,0:T(8,128)} %get-tuple-element.15), channel_id=1, source_target_pairs={{1,0},{2,1},{3,2},{4,3},{5,4},{6,5},{7,6},{9,8},{10,9},{11,10},{12... | collective-permute-start | bytes 172040 | tf_op jit(solution)/shard_map/ppermute | solution.py:443
  17.7 0.0 collective-permute-done.2.left_ref
  17.7 0.0 copy-start.3
  17.7 3.8 %collective-permute-done.3.right_ref = f32[112,128]{1,0:T(8,128)S(1)} collective-permute-done((f32[112,128]{1,0:T(8,128)}, f32[112,128]{1,0:T(8,128)S(1)}, u32[]{:S(2)}, u32[]{:S(2)}) %collective-permute-start.3) | collective-permute-done | bytes 57376 | tf_op jit(solution)/shard_map/ppermute | solution.py:443
  21.5 0.0 copy-done.3
  21.5 0.0 copy-start.4
  21.5 0.6 %copy-done.4 = f32[112,128]{1,0:T(8,128)} copy-done((f32[112,128]{1,0:T(8,128)}, f32[112,128]{1,0:T(8,128)S(1)}, u32[]{:S(2)}) %copy-start.4) | copy-done | bytes 57368
  22.1 5.8 %down.1 = (f32[32,8,128]{2,1,0:T(8,128)}, f32[8,128,128]{2,1,0:T(8,128)}, f32[2,96,128]{2,1,0:T(8,128)}) custom-call(f32[192,128]{1,0:T(8,128)} %res_ref.5, f32[192,128]{1,0:T(8,128)} %ground_ref.5, s32[192,128]{1,0:T(8,128)} %nodata_ref.5, s32[192,128]{1,0:T(8,128)} %patch_ref.7, f32[64,128]{1,0:T(8,128)} %copy-done.1, f32[64,128]{1,0:T(8,128)} %copy-done.2, ...), custom_call_target="tpu_custom_call" | custom-call | tf_op jit(solution)/shard_map/down/pallas_call | solution.py:464
  27.9 7.2 %all-to-all-start = ((f32[32,8,128]{2,1,0:T(8,128)}), f32[32,8,128]{2,1,0:T(8,128)S(1)}, u32[]{:S(2)}, u32[]{:S(2)}) async-start(f32[32,8,128]{2,1,0:T(8,128)} %get-tuple-element.16), calls=%async_computation | async-start | bytes 262144 | tf_op jit(solution)/shard_map/all_to_all | solution.py:477
  35.2 8.2 %all-to-all-done.all_ref = f32[32,8,128]{2,1,0:T(8,128)S(1)} async-done(((f32[32,8,128]{2,1,0:T(8,128)}), f32[32,8,128]{2,1,0:T(8,128)S(1)}, u32[]{:S(2)}, u32[]{:S(2)}) %all-to-all-start) | async-done | bytes 131104 | tf_op jit(solution)/shard_map/all_to_all | solution.py:477
  43.4 0.0 copy-start
  43.4 0.7 %copy-done = f32[32,8,128]{2,1,0:T(8,128)} copy-done((f32[32,8,128]{2,1,0:T(8,128)}, f32[32,8,128]{2,1,0:T(8,128)S(1)}, u32[]{:S(2)}) %copy-start) | copy-done | bytes 131096
  44.0 4.8 %solve.1 = f32[8,192,128]{2,1,0:T(8,128)} custom-call(s32[1]{0:T(128)} %bitcast.me_ref, f32[32,8,128]{2,1,0:T(8,128)} %copy-done, f32[8,128,128]{2,1,0:T(8,128)} %get-tuple-element.17.t1_ref, f32[2,96,128]{2,1,0:T(8,128)} %get-tuple-element.18.w0_ref, s32[192,128]{1,0:T(8,128)} %patch_ref.7), custom_call_target="tpu_custom_call" | custom-call | tf_op jit(solution)/shard_map/solve/pallas_call | solution.py:481
Async XLA Ops:
  1.7 6.8 %collective-permute-start = (f32[64,128]{1,0:T(8,128)}, f32[64,128]{1,0:T(8,128)S(1)}, u32[]{:S(2)}, u32[]{:S(2)}) collective-permute-start(f32[64,128]{1,0:T(8,128)} %get-tuple-element.12), channel_id=1, source_target_pairs={{0,8},{8,16},{16,24},{1,9},{9,17},{17,25},{2,10},{10,18},{18,26},{... | collective-permute-start | bytes 98312 | tf_op jit(solution)/shard_map/ppermute | solution.py:443
  6.6 6.0 %collective-permute-start.1 = (f32[64,128]{1,0:T(8,128)}, f32[64,128]{1,0:T(8,128)S(1)}, u32[]{:S(2)}, u32[]{:S(2)}) collective-permute-start(f32[64,128]{1,0:T(8,128)} %get-tuple-element.13), channel_id=1, source_target_pairs={{8,0},{16,8},{24,16},{9,1},{17,9},{25,17},{10,2},{18,10},{26,18},{... | collective-permute-start | bytes 98312 | tf_op jit(solution)/shard_map/ppermute | solution.py:443
  8.5 4.1 %copy-start.1 = (f32[64,128]{1,0:T(8,128)}, f32[64,128]{1,0:T(8,128)S(1)}, u32[]{:S(2)}) copy-start(f32[64,128]{1,0:T(8,128)S(1)} %collective-permute-done.above_ref) | copy-start | bytes 98308
  12.6 0.6 %copy-start.2 = (f32[64,128]{1,0:T(8,128)}, f32[64,128]{1,0:T(8,128)S(1)}, u32[]{:S(2)}) copy-start(f32[64,128]{1,0:T(8,128)S(1)} %collective-permute-done.1.below_ref) | copy-start | bytes 98308
  15.1 2.6 %collective-permute-start.2 = (f32[112,128]{1,0:T(8,128)}, f32[112,128]{1,0:T(8,128)S(1)}, u32[]{:S(2)}, u32[]{:S(2)}) collective-permute-start(f32[112,128]{1,0:T(8,128)} %get-tuple-element.14), channel_id=1, source_target_pairs={{0,1},{1,2},{2,3},{3,4},{4,5},{5,6},{6,7},{8,9},{9,10},{10,11},{11... | collective-permute-start | bytes 172040 | tf_op jit(solution)/shard_map/ppermute | solution.py:443
  16.4 5.1 %collective-permute-start.3 = (f32[112,128]{1,0:T(8,128)}, f32[112,128]{1,0:T(8,128)S(1)}, u32[]{:S(2)}, u32[]{:S(2)}) collective-permute-start(f32[112,128]{1,0:T(8,128)} %get-tuple-element.15), channel_id=1, source_target_pairs={{1,0},{2,1},{3,2},{4,3},{5,4},{6,5},{7,6},{9,8},{10,9},{11,10},{12... | collective-permute-start | bytes 172040 | tf_op jit(solution)/shard_map/ppermute | solution.py:443
  17.7 3.8 %copy-start.3 = (f32[112,128]{1,0:T(8,128)}, f32[112,128]{1,0:T(8,128)S(1)}, u32[]{:S(2)}) copy-start(f32[112,128]{1,0:T(8,128)S(1)} %collective-permute-done.2.left_ref) | copy-start | bytes 172036
  21.5 0.6 %copy-start.4 = (f32[112,128]{1,0:T(8,128)}, f32[112,128]{1,0:T(8,128)S(1)}, u32[]{:S(2)}) copy-start(f32[112,128]{1,0:T(8,128)S(1)} %collective-permute-done.3.right_ref) | copy-start | bytes 172036
  27.9 15.5 %all-to-all-start = ((f32[32,8,128]{2,1,0:T(8,128)}), f32[32,8,128]{2,1,0:T(8,128)S(1)}, u32[]{:S(2)}, u32[]{:S(2)}) async-start(f32[32,8,128]{2,1,0:T(8,128)} %get-tuple-element.16), calls=%async_computation | async-start | bytes 262144 | tf_op jit(solution)/shard_map/all_to_all | solution.py:477
  43.4 0.7 %copy-start = (f32[32,8,128]{2,1,0:T(8,128)}, f32[32,8,128]{2,1,0:T(8,128)S(1)}, u32[]{:S(2)}) copy-start(f32[32,8,128]{2,1,0:T(8,128)S(1)} %all-to-all-done.all_ref) | copy-start | bytes 393220

commit v2 on v1

--- a/solution.py
+++ b/solution.py
@@ -45,39 +45,30 @@
     return iota(values.shape, 1) if lane is None else lane
 
 
-def pack_rows_kernel(res_ref, ground_ref, nodata_ref, patch_ref, down_ref, up_ref):
+def pack_rows_kernel(res_ref, ground_ref, nodata_ref, patch_ref, own_ref, down_ref, up_ref):
     rows = res_ref.shape[0]
-    for out_ref, start in ((down_ref, rows - HALO), (up_ref, 0)):
-        part = pl.ds(start, HALO)
-        out_ref[0:HALO] = res_ref[part]
-        out_ref[HALO : 2 * HALO] = ground_ref[part]
-        out_ref[2 * HALO : 3 * HALO] = jnp.where(nodata_ref[part] == 0, 1.0, 0.0)
-        out_ref[3 * HALO : 4 * HALO] = patch_ref[part].astype(F32)
-
-
-def tall_halves(own_refs, above_ref, below_ref):
-    res_ref, ground_ref, nodata_ref, patch_ref = own_refs
-    own = [
+    fields = (
         res_ref[...],
         ground_ref[...],
         jnp.where(nodata_ref[...] == 0, 1.0, 0.0),
         patch_ref[...].astype(F32),
-    ]
-    half = own[0].shape[0] // 2
+    )
+    for which, values in enumerate(fields):
+        own_ref[which] = values
+        down_ref[pl.ds(which * HALO, HALO)] = values[rows - HALO :]
+        up_ref[pl.ds(which * HALO, HALO)] = values[:HALO]
+
+
+def pack_cols_kernel(own_ref, above_ref, below_ref, tall_ref, right_ref, left_ref):
+    half = own_ref.shape[1] // 2
     tall = []
-    for which, values in enumerate(own):
+    for which in range(4):
         part = pl.ds(which * HALO, HALO)
-        tall.append(
-            (
-                jnp.concatenate([above_ref[part], values[:half]], axis=0),
-                jnp.concatenate([values[half:], below_ref[part]], axis=0),
-            )
-        )
-    return tall
-
-
-def pack_cols_kernel(res_ref, ground_ref, nodata_ref, patch_ref, above_ref, below_ref, right_ref, left_ref):
-    tall = tall_halves((res_ref, ground_ref, nodata_ref, patch_ref), above_ref, below_ref)
+        upper = jnp.concatenate([above_ref[part], own_ref[which, :half]], axis=0)
+        lower = jnp.concatenate([own_ref[which, half:], below_ref[part]], axis=0)
+        tall_ref[which, : half + HALO] = upper
+        tall_ref[which, half + HALO :] = lower
+        tall.append((upper, lower))
     shape = right_ref.shape
     group_of = iota(shape, 1) // HALO
     to_right = jnp.zeros(shape, F32)
@@ -102,12 +93,7 @@
 
 
 def down_kernel(
-    res_ref,
-    ground_ref,
-    nodata_ref,
-    patch_ref,
-    above_ref,
-    below_ref,
+    tall_ref,
     left_ref,
     right_ref,
     payload_ref,
@@ -124,15 +110,14 @@
     t2_ref,
 ):
     devices = payload_ref.shape[0]
-    tall = tall_halves((res_ref, ground_ref, nodata_ref, patch_ref), above_ref, below_ref)
-    quarter = tall[0][0].shape[0]
+    quarter = tall_ref.shape[1] // 2
     lane = iota((quarter, LANES), 1)
     from_left = left_ref[...]
     from_right = right_ref[...]
     for which in range(4):
         for side in range(2):
             group = 2 * which + side
-            moved = rot(tall[which][side], HALO, 1)
+            moved = rot(tall_ref[which, pl.ds(side * quarter, quarter)], HALO, 1)
             tile0 = jnp.where(lane < HALO, rot(from_left, -HALO * group, 1), moved)
             tile1 = jnp.where(
                 lane < HALO,
@@ -449,35 +434,41 @@
     rows, cols = resistance.shape
     own = (resistance, ground, nodata, patch_ids)
     shape = jax.ShapeDtypeStruct
-    strip = shape((4 * HALO, cols), F32)
-    down, up = pl.pallas_call(pack_rows_kernel, out_shape=(strip, strip), name="pack_rows")(*own)
-    above = shifted(down, "row", 1)
-    below = shifted(up, "row", -1)
-    tall = rows + 2 * HALO
-    strip = shape((tall // 2, LANES), F32)
-    to_right, to_left = pl.pallas_call(pack_cols_kernel, out_shape=(strip, strip), name="pack_cols")(
-        *own, above, below
-    )
-    left = shifted(to_right, "col", 1)
-    right = shifted(to_left, "col", -1)
+    vmem = pl.BlockSpec(memory_space=pltpu.VMEM)
+
+    def near(value):
+        return pltpu.with_memory_space_constraint(value, pltpu.VMEM)
+
+    strip = pltpu.VMEM((4 * HALO, cols), F32)
+    kept, down, up = pl.pallas_call(
+        pack_rows_kernel, out_shape=(pltpu.VMEM((4, rows, cols), F32), strip, strip), name="pack_rows"
+    )(*own)
+    above = near(shifted(down, "row", 1))
+    below = near(shifted(up, "row", -1))
+    tall_rows = rows + 2 * HALO
+    strip = pltpu.VMEM((tall_rows // 2, LANES), F32)
+    tall, to_right, to_left = pl.pallas_call(
+        pack_cols_kernel, out_shape=(pltpu.VMEM((4, tall_rows, cols), F32), strip, strip), name="pack_cols"
+    )(near(kept), above, below)
+    left = near(shifted(to_right, "col", 1))
+    right = near(shifted(to_left, "col", -1))
     sizes = [128, 64, 32]
     payload, t1, w0 = pl.pallas_call(
         down_kernel,
         out_shape=(
-            shape((devices, 8, LANES), F32),
-            shape((RHS, sizes[0], LANES), F32),
-            shape((2, rows // 2, LANES), F32),
+            pltpu.VMEM((devices, 8, LANES), F32),
+            pltpu.VMEM((RHS, sizes[0], LANES), F32),
+            pltpu.VMEM((2, rows // 2, LANES), F32),
         ),
-        scratch_shapes=[pltpu.VMEM((8, tall, LANES), F32)]
+        scratch_shapes=[pltpu.VMEM((8, tall_rows, LANES), F32)]
         + [pltpu.VMEM((RHS, size, LANES), F32) for size in sizes]
         + [pltpu.VMEM((3, size, LANES), F32) for size in sizes]
         + [pltpu.VMEM((RHS, size, LANES), F32) for size in sizes[:0:-1]],
         name="down",
-    )(*own, above, below, left, right)
-    everything = lax.all_to_all(payload, ("row", "col"), 0, 0)
+    )(near(tall), left, right)
+    everything = near(lax.all_to_all(payload, ("row", "col"), 0, 0))
     me = (lax.axis_index("row") * grid[1] + lax.axis_index("col")).reshape(1).astype(jnp.int32)
     field = pltpu.VMEM((devices, 8, LANES), F32)
-    vmem = pl.BlockSpec(memory_space=pltpu.VMEM)
     return pl.pallas_call(
         functools.partial(solve_kernel, grid),
         out_shape=shape((RHS, rows, cols), F32),
@@ -486,7 +477,7 @@
         + [field] * 4
         + [pltpu.VMEM((rows // 16 * 8, LANES), F32)],
         name="solve",
-    )(me, everything, t1, w0, patch_ids)
+    )(me, everything, near(t1), near(w0), patch_ids)
 
 
 def solution(mesh):

time: 49.2 us -> 42.6 us (0.87)
  Pallas kernels: 14.2 us -> 9.93 us
  local copies, waits for them, and re-layouts: 1.9 us -> 0 us
    pallas_call x3, Pallas kernels: 9.33 us -> 5.32 us  [the longest x1 3.98 us: shards(): pl.pallas_call(down_kernel, out_shape=(pltpu.VMEM((devices, 8, LANES), F3...]
    unnamed x10 -> x0, local copies, waits for them, and re-layouts: 1.9 us -> none
where the time goes in v2:
time: 42.6 us; the launch traced here: 42.3 us
  waiting for transfers between devices  16.3 us (38%)
  starting transfers between devices  16.1 us (38%)
  Pallas kernels  9.93 us (23%)
    ppermute x4, starting transfers between devices, shifted(): lax.ppermute(block, axis, [(i, i + distance) for i in devices if i + dist...  8.83 us
    all_to_all x1, waiting for transfers between devices, shards(): everything = near(lax.all_to_all(payload, ('row', 'col'), 0, 0))  8.2 us
    ppermute x4, waiting for transfers between devices, shifted(): lax.ppermute(block, axis, [(i, i + distance) for i in devices if i + dist...  8.06 us
    all_to_all x1, starting transfers between devices, shards(): everything = near(lax.all_to_all(payload, ('row', 'col'), 0, 0))  7.25 us
    pallas_call x1, Pallas kernels, shards(): pl.pallas_call(functools.partial(solve_kernel, grid), out_shape=shape((RH...  4.62 us
    pallas_call x1, Pallas kernels, shards(): pl.pallas_call(down_kernel, out_shape=(pltpu.VMEM((devices, 8, LANES), F3...  3.98 us
    pallas_call x1, Pallas kernels, shards(): pl.pallas_call(pack_rows_kernel, out_shape=(pltpu.VMEM((4, rows, cols), F...  1.07 us
  transfers between devices with their start and end apart: 5, of which 4 were waited for; matrix products, arithmetic and copies ran while one was open for 0% of the time, Pallas kernels for 0%

profile of v2, /device:TPU:0, one launch (start us, length us, event | category | flops | bytes accessed | tf_op | source)
XLA Modules:
  0.0 42.3 jit_solution(4165350062908248562)
XLA Ops:
  0.0 1.1 %pack_rows.1 = (f32[4,192,128]{2,1,0:T(8,128)S(1)}, f32[64,128]{1,0:T(8,128)S(1)}, f32[64,128]{1,0:T(8,128)S(1)}) custom-call(f32[192,128]{1,0:T(8,128)} %res_ref.1, f32[192,128]{1,0:T(8,128)} %ground_ref.1, s32[192,128]{1,0:T(8,128)} %nodata_ref.1, s32[192,128]{1,0:T(8,128)} %patch_ref.3), custom_call_target="tpu_custom_call" | custom-call | tf_op jit(solution)/shard_map/pack_rows/pallas_call | solution.py:443
  1.1 5.0 %collective-permute-start = (f32[64,128]{1,0:T(8,128)S(1)}, f32[64,128]{1,0:T(8,128)S(1)}, u32[]{:S(2)}, u32[]{:S(2)}) collective-permute-start(f32[64,128]{1,0:T(8,128)S(1)} %get-tuple-element.15), channel_id=1, source_target_pairs={{0,8},{8,16},{16,24},{1,9},{9,17},{17,25},{2,10},{10,18},{18,26},{... | collective-permute-start | bytes 98312 | tf_op jit(solution)/shard_map/ppermute | solution.py:428
  6.0 1.3 %collective-permute-start.1 = (f32[64,128]{1,0:T(8,128)S(1)}, f32[64,128]{1,0:T(8,128)S(1)}, u32[]{:S(2)}, u32[]{:S(2)}) collective-permute-start(f32[64,128]{1,0:T(8,128)S(1)} %get-tuple-element.16), channel_id=1, source_target_pairs={{8,0},{16,8},{24,16},{9,1},{17,9},{25,17},{10,2},{18,10},{26,18},{... | collective-permute-start | bytes 98312 | tf_op jit(solution)/shard_map/ppermute | solution.py:428
  7.3 0.3 collective-permute-done.above_ref
  7.6 4.2 %collective-permute-done.1.below_ref = f32[64,128]{1,0:T(8,128)S(1)} collective-permute-done((f32[64,128]{1,0:T(8,128)S(1)}, f32[64,128]{1,0:T(8,128)S(1)}, u32[]{:S(2)}, u32[]{:S(2)}) %collective-permute-start.1) | collective-permute-done | bytes 32800 | tf_op jit(solution)/shard_map/ppermute | solution.py:428
  11.8 0.3 pack_cols.1
  12.1 1.3 %collective-permute-start.2 = (f32[112,128]{1,0:T(8,128)S(1)}, f32[112,128]{1,0:T(8,128)S(1)}, u32[]{:S(2)}, u32[]{:S(2)}) collective-permute-start(f32[112,128]{1,0:T(8,128)S(1)} %get-tuple-element.18), channel_id=1, source_target_pairs={{0,1},{1,2},{2,3},{3,4},{4,5},{5,6},{6,7},{8,9},{9,10},{10,11},{11... | collective-permute-start | bytes 172040 | tf_op jit(solution)/shard_map/ppermute | solution.py:428
  13.4 1.3 %collective-permute-start.3 = (f32[112,128]{1,0:T(8,128)S(1)}, f32[112,128]{1,0:T(8,128)S(1)}, u32[]{:S(2)}, u32[]{:S(2)}) collective-permute-start(f32[112,128]{1,0:T(8,128)S(1)} %get-tuple-element.19), channel_id=1, source_target_pairs={{1,0},{2,1},{3,2},{4,3},{5,4},{6,5},{7,6},{9,8},{10,9},{11,10},{12... | collective-permute-start | bytes 172040 | tf_op jit(solution)/shard_map/ppermute | solution.py:428
  14.7 0.0 collective-permute-done.2.left_ref
  14.7 3.5 %collective-permute-done.3.right_ref = f32[112,128]{1,0:T(8,128)S(1)} collective-permute-done((f32[112,128]{1,0:T(8,128)S(1)}, f32[112,128]{1,0:T(8,128)S(1)}, u32[]{:S(2)}, u32[]{:S(2)}) %collective-permute-start.3) | collective-permute-done | bytes 57376 | tf_op jit(solution)/shard_map/ppermute | solution.py:428
  18.3 4.0 %down.1 = (f32[32,8,128]{2,1,0:T(8,128)}, f32[8,128,128]{2,1,0:T(8,128)S(1)}, f32[2,96,128]{2,1,0:T(8,128)S(1)}) custom-call(f32[4,224,128]{2,1,0:T(8,128)S(1)} %get-tuple-element.17.tall_ref, f32[112,128]{1,0:T(8,128)S(1)} %collective-permute-done.2.left_ref, f32[112,128]{1,0:T(8,128)S(1)} %collective-permute-done.3.right_ref), custom_call_target="tpu_custom_call" | custom-call | tf_op jit(solution)/shard_map/down/pallas_call | solution.py:456
  22.3 7.2 %all-to-all-start = ((f32[32,8,128]{2,1,0:T(8,128)}), f32[32,8,128]{2,1,0:T(8,128)S(1)}, u32[]{:S(2)}, u32[]{:S(2)}) async-start(f32[32,8,128]{2,1,0:T(8,128)} %get-tuple-element.20), calls=%async_computation | async-start | bytes 262144 | tf_op jit(solution)/shard_map/all_to_all | solution.py:469
  29.5 8.2 %all-to-all-done.all_ref = f32[32,8,128]{2,1,0:T(8,128)S(1)} async-done(((f32[32,8,128]{2,1,0:T(8,128)}), f32[32,8,128]{2,1,0:T(8,128)S(1)}, u32[]{:S(2)}, u32[]{:S(2)}) %all-to-all-start) | async-done | bytes 131104 | tf_op jit(solution)/shard_map/all_to_all | solution.py:469
  37.7 4.6 %solve.1 = f32[8,192,128]{2,1,0:T(8,128)} custom-call(s32[1]{0:T(128)} %bitcast.me_ref, f32[32,8,128]{2,1,0:T(8,128)S(1)} %all-to-all-done.all_ref, f32[8,128,128]{2,1,0:T(8,128)S(1)} %get-tuple-element.21.t1_ref, f32[2,96,128]{2,1,0:T(8,128)S(1)} %get-tuple-element.22.w0_ref, s32[192,128]{1,0:T(8,128)} %patch_ref.3), custom_call_target="tpu_custom_call" | custom-call | tf_op jit(solution)/shard_map/solve/pallas_call | solution.py:472
Async XLA Ops:
  1.1 6.5 %collective-permute-start = (f32[64,128]{1,0:T(8,128)S(1)}, f32[64,128]{1,0:T(8,128)S(1)}, u32[]{:S(2)}, u32[]{:S(2)}) collective-permute-start(f32[64,128]{1,0:T(8,128)S(1)} %get-tuple-element.15), channel_id=1, source_target_pairs={{0,8},{8,16},{16,24},{1,9},{9,17},{17,25},{2,10},{10,18},{18,26},{... | collective-permute-start | bytes 98312 | tf_op jit(solution)/shard_map/ppermute | solution.py:428
  6.0 5.8 %collective-permute-start.1 = (f32[64,128]{1,0:T(8,128)S(1)}, f32[64,128]{1,0:T(8,128)S(1)}, u32[]{:S(2)}, u32[]{:S(2)}) collective-permute-start(f32[64,128]{1,0:T(8,128)S(1)} %get-tuple-element.16), channel_id=1, source_target_pairs={{8,0},{16,8},{24,16},{9,1},{17,9},{25,17},{10,2},{18,10},{26,18},{... | collective-permute-start | bytes 98312 | tf_op jit(solution)/shard_map/ppermute | solution.py:428
  12.1 2.6 %collective-permute-start.2 = (f32[112,128]{1,0:T(8,128)S(1)}, f32[112,128]{1,0:T(8,128)S(1)}, u32[]{:S(2)}, u32[]{:S(2)}) collective-permute-start(f32[112,128]{1,0:T(8,128)S(1)} %get-tuple-element.18), channel_id=1, source_target_pairs={{0,1},{1,2},{2,3},{3,4},{4,5},{5,6},{6,7},{8,9},{9,10},{10,11},{11... | collective-permute-start | bytes 172040 | tf_op jit(solution)/shard_map/ppermute | solution.py:428
  13.4 4.9 %collective-permute-start.3 = (f32[112,128]{1,0:T(8,128)S(1)}, f32[112,128]{1,0:T(8,128)S(1)}, u32[]{:S(2)}, u32[]{:S(2)}) collective-permute-start(f32[112,128]{1,0:T(8,128)S(1)} %get-tuple-element.19), channel_id=1, source_target_pairs={{1,0},{2,1},{3,2},{4,3},{5,4},{6,5},{7,6},{9,8},{10,9},{11,10},{12... | collective-permute-start | bytes 172040 | tf_op jit(solution)/shard_map/ppermute | solution.py:428
  22.3 15.5 %all-to-all-start = ((f32[32,8,128]{2,1,0:T(8,128)}), f32[32,8,128]{2,1,0:T(8,128)S(1)}, u32[]{:S(2)}, u32[]{:S(2)}) async-start(f32[32,8,128]{2,1,0:T(8,128)} %get-tuple-element.20), calls=%async_computation | async-start | bytes 262144 | tf_op jit(solution)/shard_map/all_to_all | solution.py:469

commit v3 on v2

--- a/solution.py
+++ b/solution.py
@@ -14,7 +14,8 @@
 LANES = 128
 F32 = jnp.float32
 BF16 = jnp.bfloat16
-PIECES = 3
+PIECES = 2
+VMEM_LIMIT = 32 * 2**20
 
 
 def iota(shape, dim):
@@ -45,43 +46,65 @@
     return iota(values.shape, 1) if lane is None else lane
 
 
-def pack_rows_kernel(res_ref, ground_ref, nodata_ref, patch_ref, own_ref, down_ref, up_ref):
+def pack_rows_kernel(
+    res_ref, ground_ref, nodata_ref, patch_ref, own_ref, first_ref, second_ref, nodata_near_ref, patch_near_ref, sem_ref
+):
     rows = res_ref.shape[0]
-    fields = (
-        res_ref[...],
-        ground_ref[...],
-        jnp.where(nodata_ref[...] == 0, 1.0, 0.0),
-        patch_ref[...].astype(F32),
-    )
-    for which, values in enumerate(fields):
-        own_ref[which] = values
-        down_ref[pl.ds(which * HALO, HALO)] = values[rows - HALO :]
-        up_ref[pl.ds(which * HALO, HALO)] = values[:HALO]
-
-
-def pack_cols_kernel(own_ref, above_ref, below_ref, tall_ref, right_ref, left_ref):
+    copies = [
+        pltpu.make_async_copy(source, target, sem_ref.at[which])
+        for which, (source, target) in enumerate(
+            (
+                (res_ref, own_ref.at[0]),
+                (ground_ref, own_ref.at[1]),
+                (nodata_ref, nodata_near_ref),
+                (patch_ref, patch_near_ref),
+            )
+        )
+    ]
+    for copy in copies:
+        copy.start()
+    for copy in copies:
+        copy.wait()
+    own_ref[2] = jnp.where(nodata_near_ref[...] == 0, 1.0, 0.0)
+    own_ref[3] = patch_near_ref[...].astype(F32)
+    odd = lax.axis_index("row") % 2 == 1
+    for which in range(4):
+        top = own_ref[which, :HALO]
+        bottom = own_ref[which, rows - HALO :]
+        part = pl.ds(which * HALO, HALO)
+        first_ref[part] = jnp.where(odd, top, bottom)
+        second_ref[part] = jnp.where(odd, bottom, top)
+
+
+def before_after(axis, first, second):
+    index = lax.axis_index(axis)
+    odd = index % 2 == 1
+    before = jnp.where(index > 0, jnp.where(odd, first, second), 0.0)
+    after = jnp.where(index < lax.axis_size(axis) - 1, jnp.where(odd, second, first), 0.0)
+    return before, after
+
+
+def pack_cols_kernel(own_ref, from_first_ref, from_second_ref, tall_ref, first_ref, second_ref):
     half = own_ref.shape[1] // 2
-    tall = []
-    for which in range(4):
-        part = pl.ds(which * HALO, HALO)
-        upper = jnp.concatenate([above_ref[part], own_ref[which, :half]], axis=0)
-        lower = jnp.concatenate([own_ref[which, half:], below_ref[part]], axis=0)
-        tall_ref[which, : half + HALO] = upper
-        tall_ref[which, half + HALO :] = lower
-        tall.append((upper, lower))
-    shape = right_ref.shape
+    shape = first_ref.shape
     group_of = iota(shape, 1) // HALO
+    odd = lax.axis_index("col") % 2 == 1
+    above, below = before_after("row", from_first_ref[...], from_second_ref[...])
     to_right = jnp.zeros(shape, F32)
     to_left = jnp.zeros(shape, F32)
     for which in range(4):
-        for side in range(2):
+        part = slice(which * HALO, which * HALO + HALO)
+        upper = jnp.concatenate([above[part], own_ref[which, :half]], axis=0)
+        lower = jnp.concatenate([own_ref[which, half:], below[part]], axis=0)
+        tall_ref[which, : half + HALO] = upper
+        tall_ref[which, half + HALO :] = lower
+        for side, values in enumerate((upper, lower)):
             group = 2 * which + side
-            values = tall[which][side]
             here = group_of == group
             to_right = jnp.where(here, rot(values, HALO * group + HALO, 1), to_right)
             to_left = jnp.where(here, rot(values, HALO * group, 1), to_left)
-    right_ref[...] = to_right
-    left_ref[...] = to_left
+    first_ref[...] = jnp.where(odd, to_left, to_right)
+    second_ref[...] = jnp.where(odd, to_right, to_left)
 
 
 def link(resist, validity, near_resist, near_valid):
@@ -94,26 +117,25 @@
 
 def down_kernel(
     tall_ref,
-    left_ref,
-    right_ref,
+    from_first_ref,
+    from_second_ref,
     payload_ref,
-    t1_ref,
     w0_ref,
-    ext_ref,
     r1_ref,
     r2_ref,
     r3_ref,
+    w1_ref,
+    w2_ref,
+    w3_ref,
+    ext_ref,
     c1_ref,
     c2_ref,
     c3_ref,
-    t3_ref,
-    t2_ref,
 ):
     devices = payload_ref.shape[0]
     quarter = tall_ref.shape[1] // 2
     lane = iota((quarter, LANES), 1)
-    from_left = left_ref[...]
-    from_right = right_ref[...]
+    from_left, from_right = before_after("col", from_first_ref[...], from_second_ref[...])
     for which in range(4):
         for side in range(2):
             group = 2 * which + side
@@ -221,11 +243,10 @@
     l_out = selection(LANES, lambda x, j: x // 2 + 2 * (x % 2) - 2 == j % 8)
     l_even = selection(LANES, lambda x, j: (x // 2 - 1 == j % 8) & (x % 2 == 0))
     l_both = jnp.concatenate([l_in, l_out], axis=0)
-    smooth = []
-    for r_ref, c_ref, next_r, next_c in (
-        (r1_ref, c1_ref, r2_ref, c2_ref),
-        (r2_ref, c2_ref, r3_ref, c3_ref),
-        (r3_ref, c3_ref, None, None),
+    for r_ref, c_ref, w_ref, next_r, next_c in (
+        (r1_ref, c1_ref, w1_ref, r2_ref, c2_ref),
+        (r2_ref, c2_ref, w2_ref, r3_ref, c3_ref),
+        (r3_ref, c3_ref, w3_ref, None, None),
     ):
         half = r_ref.shape[1] // 2
         even, uneven = pl.ds(0, half, stride=2), pl.ds(1, half, stride=2)
@@ -243,7 +264,8 @@
         b_o = w_o * jnp.where(odd_lane, eo, wo)
         c_e = w_e * v_up
         c_o = w_o * v_dn
-        smooth.append((w_e, w_o))
+        w_ref[0] = w_e
+        w_ref[1] = w_o
         both, inner, evens = (k_both, k_in, k_even) if next_r is not None else (l_both, l_in, l_even)
         coarser = [dot01(ge + go, inner), dot01(v_up, inner), dot01(we + wo, evens)]
         fields = []
@@ -279,27 +301,36 @@
     def _(device):
         payload_ref[device] = tile
 
+
+def up_kernel(own_ref, w0_ref, r1_ref, r2_ref, r3_ref, w1_ref, w2_ref, w3_ref, base_ref, t3_ref, t2_ref, t1_ref):
     spread = selection(LANES, lambda j, x: x // 2 == j)
+    for r_ref, w_ref, coarse_ref, t_ref in (
+        (r3_ref, w3_ref, None, t3_ref),
+        (r2_ref, w2_ref, t3_ref, t2_ref),
+        (r1_ref, w1_ref, t2_ref, t1_ref),
+    ):
+        half = w_ref.shape[1]
+        for k in range(RHS):
+            finer = None if coarse_ref is None else dot01(coarse_ref[k], spread)
+            for index in range(2):
+                rows = pl.ds(index, half, stride=2)
+                smoothed = w_ref[index] * r_ref[k, rows, :]
+                t_ref[k, rows, :] = smoothed if finer is None else finer + smoothed
+    inner = selection(LANES, lambda j, x: j == x // 2 + HALO // 2)
+    half = w0_ref.shape[1]
+    sides = []
+    for index in range(2):
+        rows = pl.ds(index, half, stride=2)
+        patch = own_ref[3, rows, :]
+        weight = w0_ref[index]
+        sides.append((rows, patch, 0.875 * weight, jnp.where(patch > 0, -0.125, 0.0) * weight))
     for k in range(RHS):
-        w_e, w_o = smooth[2]
-        half = w_e.shape[0]
-        t3_ref[k, pl.ds(0, half, stride=2), :] = w_e * r3_ref[k, pl.ds(0, half, stride=2), :]
-        t3_ref[k, pl.ds(1, half, stride=2), :] = w_o * r3_ref[k, pl.ds(1, half, stride=2), :]
-    for k in range(RHS):
-        w_e, w_o = smooth[1]
-        half = w_e.shape[0]
-        finer = dot01(t3_ref[k], spread)
-        t2_ref[k, pl.ds(0, half, stride=2), :] = finer + w_e * r2_ref[k, pl.ds(0, half, stride=2), :]
-        t2_ref[k, pl.ds(1, half, stride=2), :] = finer + w_o * r2_ref[k, pl.ds(1, half, stride=2), :]
-    for k in range(RHS):
-        w_e, w_o = smooth[0]
-        half = w_e.shape[0]
-        finer = dot01(t2_ref[k], spread)
-        t1_ref[k, pl.ds(0, half, stride=2), :] = finer + w_e * r1_ref[k, pl.ds(0, half, stride=2), :]
-        t1_ref[k, pl.ds(1, half, stride=2), :] = finer + w_o * r1_ref[k, pl.ds(1, half, stride=2), :]
-
-
-def solve_kernel(grid, me_ref, all_ref, t1_ref, w0_ref, patch_ref, out_ref, coef_ref, x_ref, r_ref, p_ref, q_ref, u_ref):
+        finer = dot01(t1_ref[k, pl.ds(HALO // 2, half)], inner)
+        for rows, patch, chosen, other in sides:
+            base_ref[k, rows, :] = finer + jnp.where(patch == k + 1, chosen, other)
+
+
+def solve_kernel(grid, all_ref, base_ref, out_ref, coef_ref, x_ref, r_ref, p_ref, q_ref, u_ref, done_ref, sem_ref):
     grid_rows, grid_cols = grid
     count = grid_rows * grid_cols
     lane = iota((8, LANES), 1)
@@ -401,83 +432,111 @@
 
             every(turn, 0)
 
-    mine = x_ref[me_ref[0]]
+    mine = x_ref[lax.axis_index("row") * grid_cols + lax.axis_index("col")]
     groups = u_ref.shape[0] // 8
     stacked = jnp.concatenate([jnp.where(lane // 8 == i, mine, 0.0) for i in range(groups)], axis=0)
-    widen = selection(LANES, lambda x, j: (j >= 8) & (j < 72) & (x % 8 == (j - 8) // 8))
+    widen = selection(LANES, lambda x, j: x % 8 == j // HALO)
     u_ref[...] = dot01(stacked, widen)
-    spread = selection(LANES, lambda j, x: j == x // 2 + 8)
-    half = w0_ref.shape[1]
-    even, uneven = pl.ds(0, half, stride=2), pl.ds(1, half, stride=2)
-    sides = []
-    for index, rows in ((0, even), (1, uneven)):
-        weight = w0_ref[index]
-        patch = patch_ref[rows, :]
-        sides.append((rows, patch, 0.875 * weight, jnp.where(patch > 0, -0.125, 0.0) * weight))
+    copies = []
     for k in range(RHS):
-        coarse = jnp.concatenate(
-            [t1_ref[k, pl.ds(8 * i + 8, 8), :] + u_ref[pl.ds(8 * i + k, 1), :] for i in range(groups)], axis=0
-        )
-        finer = dot01(coarse, spread)
-        for rows, patch, chosen, other in sides:
-            out_ref[k, rows, :] = finer + jnp.where(patch == k + 1, chosen, other)
-
-
-def shifted(block, axis, distance):
-    devices = range(lax.axis_size(axis))
-    return lax.ppermute(block, axis, [(i, i + distance) for i in devices if i + distance in devices])
+        for i in range(groups):
+            rows = pl.ds(HALO * i, HALO)
+            done_ref[k, rows, :] = base_ref[k, rows, :] + u_ref[pl.ds(8 * i + k, 1), :]
+        copy = pltpu.make_async_copy(done_ref.at[k], out_ref.at[k], sem_ref.at[k])
+        copy.start()
+        copies.append(copy)
+    for copy in copies:
+        copy.wait()
+
+
+def exchanged(first, second, axis, other):
+    sizes = {name: lax.axis_size(name) for name in (axis, other)}
+
+    def pairs(step):
+        found = []
+        for i in range(sizes["row"]):
+            for j in range(sizes["col"]):
+                place = {"row": i, "col": j}
+                target = dict(place)
+                at = place[axis]
+                if step == 0:
+                    target[axis] = at ^ 1
+                elif at in (0, sizes[axis] - 1):
+                    target[other] = place[other] ^ 1
+                else:
+                    target[axis] = at + 1 if at % 2 else at - 1
+                found.append((i * sizes["col"] + j, target["row"] * sizes["col"] + target["col"]))
+        return found
+
+    return [lax.ppermute(part, ("row", "col"), pairs(step)) for step, part in enumerate((first, second))]
 
 
 def shards(resistance, ground, nodata, patch_ids):
     grid = (lax.axis_size("row"), lax.axis_size("col"))
     devices = grid[0] * grid[1]
     rows, cols = resistance.shape
-    own = (resistance, ground, nodata, patch_ids)
-    shape = jax.ShapeDtypeStruct
-    vmem = pl.BlockSpec(memory_space=pltpu.VMEM)
-
+    own = [pltpu.with_memory_space_constraint(part, pltpu.HBM) for part in (resistance, ground, nodata, patch_ids)]
     def near(value):
         return pltpu.with_memory_space_constraint(value, pltpu.VMEM)
 
-    strip = pltpu.VMEM((4 * HALO, cols), F32)
-    kept, down, up = pl.pallas_call(
-        pack_rows_kernel, out_shape=(pltpu.VMEM((4, rows, cols), F32), strip, strip), name="pack_rows"
-    )(*own)
-    above = near(shifted(down, "row", 1))
-    below = near(shifted(up, "row", -1))
+    def call(kernel, outs, scratch, *args, **options):
+        outs = tuple(pltpu.VMEM(out, F32) for out in outs)
+        scratch = [pltpu.VMEM(part, F32) if isinstance(part, tuple) else part for part in scratch]
+        name = kernel.__name__
+        params = pltpu.CompilerParams(vmem_limit_bytes=VMEM_LIMIT)
+        return pl.pallas_call(
+            kernel, out_shape=outs, scratch_shapes=scratch, name=name, compiler_params=params, **options
+        )(*args)
+
+    def all_near(values):
+        return [near(value) for value in values]
+
+    strip = (4 * HALO, cols)
+    kept, first, second = call(
+        pack_rows_kernel,
+        [(4, rows, cols), strip, strip],
+        [pltpu.VMEM((rows, cols), jnp.int32)] * 2 + [pltpu.SemaphoreType.DMA((4,))],
+        *own,
+        in_specs=[pl.BlockSpec(memory_space=pltpu.HBM)] * 4,
+    )
+    first, second = exchanged(first, second, "row", "col")
     tall_rows = rows + 2 * HALO
-    strip = pltpu.VMEM((tall_rows // 2, LANES), F32)
-    tall, to_right, to_left = pl.pallas_call(
-        pack_cols_kernel, out_shape=(pltpu.VMEM((4, tall_rows, cols), F32), strip, strip), name="pack_cols"
-    )(near(kept), above, below)
-    left = near(shifted(to_right, "col", 1))
-    right = near(shifted(to_left, "col", -1))
+    strip = (tall_rows // 2, LANES)
+    kept = near(kept)
+    tall, first, second = call(
+        pack_cols_kernel, [(4, tall_rows, cols), strip, strip], [], kept, near(first), near(second)
+    )
+    first, second = exchanged(first, second, "col", "row")
     sizes = [128, 64, 32]
-    payload, t1, w0 = pl.pallas_call(
+    payload, w0, *levels = call(
         down_kernel,
-        out_shape=(
-            pltpu.VMEM((devices, 8, LANES), F32),
-            pltpu.VMEM((RHS, sizes[0], LANES), F32),
-            pltpu.VMEM((2, rows // 2, LANES), F32),
-        ),
-        scratch_shapes=[pltpu.VMEM((8, tall_rows, LANES), F32)]
-        + [pltpu.VMEM((RHS, size, LANES), F32) for size in sizes]
-        + [pltpu.VMEM((3, size, LANES), F32) for size in sizes]
-        + [pltpu.VMEM((RHS, size, LANES), F32) for size in sizes[:0:-1]],
-        name="down",
-    )(near(tall), left, right)
+        [(devices, 8, LANES), (2, rows // 2, LANES)]
+        + [(RHS, size, LANES) for size in sizes]
+        + [(2, size // 2, LANES) for size in sizes],
+        [(8, tall_rows, LANES)] + [(3, size, LANES) for size in sizes],
+        *all_near((tall, first, second)),
+    )
     everything = near(lax.all_to_all(payload, ("row", "col"), 0, 0))
-    me = (lax.axis_index("row") * grid[1] + lax.axis_index("col")).reshape(1).astype(jnp.int32)
+    (base,) = call(
+        up_kernel,
+        [(RHS, rows, cols)],
+        [(RHS, size, LANES) for size in sizes[::-1]],
+        kept,
+        *all_near([w0] + levels),
+        cost_estimate=pl.CostEstimate(flops=10**8, bytes_accessed=10**6, transcendentals=0),
+    )
     field = pltpu.VMEM((devices, 8, LANES), F32)
     return pl.pallas_call(
         functools.partial(solve_kernel, grid),
-        out_shape=shape((RHS, rows, cols), F32),
-        in_specs=[pl.BlockSpec(memory_space=pltpu.SMEM)] + [vmem] * 4,
+        out_shape=jax.ShapeDtypeStruct((RHS, rows, cols), F32),
+        out_specs=pl.BlockSpec(memory_space=pl.ANY),
         scratch_shapes=[pltpu.VMEM((5, devices, 8, LANES), F32)]
         + [field] * 4
-        + [pltpu.VMEM((rows // 16 * 8, LANES), F32)],
-        name="solve",
-    )(me, everything, near(t1), near(w0), patch_ids)
+        + [pltpu.VMEM((rows // HALO * 8, LANES), F32), pltpu.VMEM((RHS, rows, cols), F32)]
+        + [pltpu.SemaphoreType.DMA((RHS,))],
+        compiler_params=pltpu.CompilerParams(vmem_limit_bytes=VMEM_LIMIT),
+        name="solve_kernel",
+    )(everything, near(base))
 
 
 def solution(mesh):

time: 42.6 us -> 32.6 us (0.77)
  waiting for transfers between devices: 16.3 us -> 11.6 us
  starting transfers between devices: 16.1 us -> 11.8 us
  Pallas kernels: 9.93 us -> 8.9 us
    ppermute x4, waiting for transfers between devices: 8.06 us -> 4.05 us  [exchanged(): lax.ppermute(part, ('row', 'col'), pairs(step))]
    ppermute x4, starting transfers between devices: 8.83 us -> 6.4 us  [exchanged(): lax.ppermute(part, ('row', 'col'), pairs(step))]
    all_to_all x1, starting transfers between devices: 7.25 us -> 5.39 us  [shards(): everything = near(lax.all_to_all(payload, ('row', 'col'), 0, 0))]
    pallas_call x4 -> x5, Pallas kernels: 9.93 us -> 8.9 us  [the longest x4 5.47 us: call(): pl.pallas_call(kernel, out_shape=outs, scratch_shapes=scratch, name=name,...]
    all_to_all x1, waiting for transfers between devices: 8.2 us -> 7.57 us  [shards(): everything = near(lax.all_to_all(payload, ('row', 'col'), 0, 0))]
  transfers between devices with their start and end apart: 5 -> 5, of which waited for: 4 -> 3; matrix products, arithmetic and copies ran while one was open for 0% -> 0% of each run, Pallas kernels for 0% -> 2%
where the time goes in v3:
time: 32.6 us; the launch traced here: 32.4 us
  starting transfers between devices  11.8 us (36%)
  waiting for transfers between devices  11.6 us (36%)
  Pallas kernels  8.9 us (27%)
    all_to_all x1, waiting for transfers between devices, shards(): everything = near(lax.all_to_all(payload, ('row', 'col'), 0, 0))  7.57 us
    ppermute x4, starting transfers between devices, exchanged(): lax.ppermute(part, ('row', 'col'), pairs(step))  6.4 us
    pallas_call x4, Pallas kernels, call(): pl.pallas_call(kernel, out_shape=outs, scratch_shapes=scratch, name=name,...  5.47 us
    all_to_all x1, starting transfers between devices, shards(): everything = near(lax.all_to_all(payload, ('row', 'col'), 0, 0))  5.39 us
    ppermute x4, waiting for transfers between devices, exchanged(): lax.ppermute(part, ('row', 'col'), pairs(step))  4.05 us
    pallas_call x1, Pallas kernels, shards(): pl.pallas_call(functools.partial(solve_kernel, grid), out_shape=jax.Shape...  3.44 us
  transfers between devices with their start and end apart: 5, of which 3 were waited for; matrix products, arithmetic and copies ran while one was open for 0% of the time, Pallas kernels for 2%

profile of v3, /device:TPU:0, one launch (start us, length us, event | category | flops | bytes accessed | tf_op | source)
XLA Modules:
  0.0 32.4 jit_solution(8422471203642602355)
XLA Ops:
  0.0 1.1 %pack_rows_kernel.1 = (f32[4,192,128]{2,1,0:T(8,128)S(1)}, f32[64,128]{1,0:T(8,128)S(1)}, f32[64,128]{1,0:T(8,128)S(1)}) custom-call(f32[192,128]{1,0:T(8,128)} %res_ref.1, f32[192,128]{1,0:T(8,128)} %ground_ref.1, s32[192,128]{1,0:T(8,128)} %nodata_ref.1, s32[192,128]{1,0:T(8,128)} %patch_ref.1), custom_call_target="tpu_custom_call" | custom-call | tf_op jit(solution)/shard_map/pack_rows_kernel/pallas_call | solution.py:487
  1.1 3.1 %collective-permute-start = (f32[64,128]{1,0:T(8,128)S(1)}, f32[64,128]{1,0:T(8,128)S(1)}, u32[]{:S(2)}, u32[]{:S(2)}) collective-permute-start(f32[64,128]{1,0:T(8,128)S(1)} %get-tuple-element.20), channel_id=1, source_target_pairs={{0,8},{1,9},{2,10},{3,11},{4,12},{5,13},{6,14},{7,15},{8,0},{9,1},... | collective-permute-start | bytes 98312 | tf_op jit(solution)/shard_map/ppermute | solution.py:471
  4.2 0.0 collective-permute-start.1
  4.2 1.9 %collective-permute-done.from_first_ref = f32[64,128]{1,0:T(8,128)S(1)} collective-permute-done((f32[64,128]{1,0:T(8,128)S(1)}, f32[64,128]{1,0:T(8,128)S(1)}, u32[]{:S(2)}, u32[]{:S(2)}) %collective-permute-start) | collective-permute-done | bytes 32800 | tf_op jit(solution)/shard_map/ppermute | solution.py:471
  6.1 0.0 collective-permute-done.1.from_second_ref
  6.1 0.3 pack_cols_kernel.1
  6.4 0.1 collective-permute-start.2
  6.5 3.2 %collective-permute-start.3 = (f32[112,128]{1,0:T(8,128)S(1)}, f32[112,128]{1,0:T(8,128)S(1)}, u32[]{:S(2)}, u32[]{:S(2)}) collective-permute-start(f32[112,128]{1,0:T(8,128)S(1)} %get-tuple-element.24), channel_id=1, source_target_pairs={{0,8},{1,2},{2,1},{3,4},{4,3},{5,6},{6,5},{7,15},{8,0},{9,10},{10,... | collective-permute-start | bytes 172040 | tf_op jit(solution)/shard_map/ppermute | solution.py:471
  9.7 0.0 collective-permute-done.2.from_first_ref
  9.7 2.2 %collective-permute-done.3.from_second_ref = f32[112,128]{1,0:T(8,128)S(1)} collective-permute-done((f32[112,128]{1,0:T(8,128)S(1)}, f32[112,128]{1,0:T(8,128)S(1)}, u32[]{:S(2)}, u32[]{:S(2)}) %collective-permute-start.3) | collective-permute-done | bytes 57376 | tf_op jit(solution)/shard_map/ppermute | solution.py:471
  11.8 3.5 %down_kernel.1 = (f32[32,8,128]{2,1,0:T(8,128)}, f32[2,96,128]{2,1,0:T(8,128)S(1)}, f32[8,128,128]{2,1,0:T(8,128)S(1)}, f32[8,64,128]{2,1,0:T(8,128)S(1)}, f32[8...) custom-call(f32[4,224,128]{2,1,0:T(8,128)S(1)} %get-tuple-element.22.ta, ...), custom_call_target="tpu_custom_call" | custom-call | tf_op jit(solution)/shard_map/down_kernel/pallas_call | solution.py:487
  15.3 5.4 %all-to-all-start = ((f32[32,8,128]{2,1,0:T(8,128)}), f32[32,8,128]{2,1,0:T(8,128)S(1)}, u32[]{:S(2)}, u32[]{:S(2)}) async-start(f32[32,8,128]{2,1,0:T(8,128)} %get-tuple-element.25), calls=%async_computation | async-start | bytes 262144 | tf_op jit(solution)/shard_map/all_to_all | solution.py:519
  20.7 0.6 %up_kernel.1.base_ref = f32[8,192,128]{2,1,0:T(8,128)S(1)} custom-call(f32[4,192,128]{2,1,0:T(8,128)S(1)} %get-tuple-element.19.own_ref, f32[2,96,128]{2,1,0:T(8,128)S(1)} %get-tuple-element.26.w0_ref, f32[8,128,128]{2,1,0:T(8,128)S(1)} %get-tuple-element.27.r1_ref, f32[8,64,128]{2,1,0:T(8,128)S(1)} %get-tuple-element.28.r2_ref, ...), custom_call_target="tpu_custom_call" | custom-call | flops 100000000 | bytes 1000000 | tf_op jit(solution)/shard_map/up_kernel/pallas_call | solution.py:487
  21.4 7.6 %all-to-all-done.all_ref = f32[32,8,128]{2,1,0:T(8,128)S(1)} async-done(((f32[32,8,128]{2,1,0:T(8,128)}), f32[32,8,128]{2,1,0:T(8,128)S(1)}, u32[]{:S(2)}, u32[]{:S(2)}) %all-to-all-start) | async-done | bytes 131104 | tf_op jit(solution)/shard_map/all_to_all | solution.py:519
  28.9 3.4 %solve_kernel.1 = f32[8,192,128]{2,1,0:T(8,128)} custom-call(f32[32,8,128]{2,1,0:T(8,128)S(1)} %all-to-all-done.all_ref, f32[8,192,128]{2,1,0:T(8,128)S(1)} %up_kernel.1.base_ref), custom_call_target="tpu_custom_call" | custom-call | tf_op jit(solution)/shard_map/solve_kernel/pallas_call | solution.py:529
Async XLA Ops:
  1.1 5.0 %collective-permute-start = (f32[64,128]{1,0:T(8,128)S(1)}, f32[64,128]{1,0:T(8,128)S(1)}, u32[]{:S(2)}, u32[]{:S(2)}) collective-permute-start(f32[64,128]{1,0:T(8,128)S(1)} %get-tuple-element.20), channel_id=1, source_target_pairs={{0,8},{1,9},{2,10},{3,11},{4,12},{5,13},{6,14},{7,15},{8,0},{9,1},... | collective-permute-start | bytes 98312 | tf_op jit(solution)/shard_map/ppermute | solution.py:471
  4.2 1.9 %collective-permute-start.1 = (f32[64,128]{1,0:T(8,128)S(1)}, f32[64,128]{1,0:T(8,128)S(1)}, u32[]{:S(2)}, u32[]{:S(2)}) collective-permute-start(f32[64,128]{1,0:T(8,128)S(1)} %get-tuple-element.21), channel_id=1, source_target_pairs={{0,1},{1,0},{2,3},{3,2},{4,5},{5,4},{6,7},{7,6},{8,16},{9,17},{10,... | collective-permute-start | bytes 98312 | tf_op jit(solution)/shard_map/ppermute | solution.py:471
  6.4 3.3 %collective-permute-start.2 = (f32[112,128]{1,0:T(8,128)S(1)}, f32[112,128]{1,0:T(8,128)S(1)}, u32[]{:S(2)}, u32[]{:S(2)}) collective-permute-start(f32[112,128]{1,0:T(8,128)S(1)} %get-tuple-element.23), channel_id=1, source_target_pairs={{0,1},{1,0},{2,3},{3,2},{4,5},{5,4},{6,7},{7,6},{8,9},{9,8},{10,11... | collective-permute-start | bytes 172040 | tf_op jit(solution)/shard_map/ppermute | solution.py:471
  6.5 5.4 %collective-permute-start.3 = (f32[112,128]{1,0:T(8,128)S(1)}, f32[112,128]{1,0:T(8,128)S(1)}, u32[]{:S(2)}, u32[]{:S(2)}) collective-permute-start(f32[112,128]{1,0:T(8,128)S(1)} %get-tuple-element.24), channel_id=1, source_target_pairs={{0,8},{1,2},{2,1},{3,4},{4,3},{5,6},{6,5},{7,15},{8,0},{9,10},{10,... | collective-permute-start | bytes 172040 | tf_op jit(solution)/shard_map/ppermute | solution.py:471
  15.3 13.6 %all-to-all-start = ((f32[32,8,128]{2,1,0:T(8,128)}), f32[32,8,128]{2,1,0:T(8,128)S(1)}, u32[]{:S(2)}, u32[]{:S(2)}) async-start(f32[32,8,128]{2,1,0:T(8,128)} %get-tuple-element.25), calls=%async_computation | async-start | bytes 262144 | tf_op jit(solution)/shard_map/all_to_all | solution.py:519

commit v4 on v3

v4 whole, which is shorter than its diff:
```python
import functools

import jax
import jax.numpy as jnp
from jax import lax
from jax.experimental import pallas as pl
from jax.experimental.pallas import tpu as pltpu
from jax.sharding import PartitionSpec as P

RHS = 8
ITERS = 4
OMEGA = 0.8
HALO = 16
LANES = 128
F32 = jnp.float32
BF16 = jnp.bfloat16
PIECES = 2
VMEM_LIMIT = 32 * 2**20


def iota(shape, dim):
    return lax.broadcasted_iota(jnp.int32, shape, dim)


def selection(rows, test):
    shape = (rows, LANES)
    return jnp.where(test(iota(shape, 0), iota(shape, 1)), 1.0, 0.0).astype(BF16)


def split(values):
    pieces = []
    for piece in range(PIECES):
        pieces.append(values.astype(BF16))
        if piece + 1 < PIECES:
            values = values - pieces[-1].astype(F32)
    return pieces


def stacked(matrix):
    return jnp.concatenate([matrix] * PIECES, axis=0)


def dot01(parts, matrix):
    pieces = [split(part) for part in parts]
    rows = jnp.concatenate([piece[i] for i in range(PIECES) for piece in pieces], axis=1)
    return jnp.dot(rows, matrix, preferred_element_type=F32)


def rot(values, shift, axis):
    return pltpu.roll(values, shift % values.shape[axis], axis)


def column(x):
    return jnp.where(x < 16, x + 1, x + 127)


def outward(x):
    return x // 2 + 2 * (x % 2) - 1


def turn_test(first):
    def test(x, j):
        y = x - 64 * first
        own = (y >= 0) & (y < 32) & (column(y) // 2 == j)
        return own | ((y >= 32) & (y < 64) & (outward(column(y - 32)) == j))

    return test


def level_tests(shift, places):
    m_in = lambda x, j: x // 2 - shift == j % places
    m_out = lambda x, j: outward(x) - shift == j % places
    m_even = lambda x, j: (x // 2 - shift == j % places) & (x % 2 == 0)
    return [[m_in, m_out], [m_in], [m_even]]


TABLES = (
    [
        [lambda c, j: (c + HALO) // 2 == j, lambda c, j: outward(c + HALO) == j],
        [lambda c, j: (c + HALO) // 2 == j],
        [lambda c, j: (c + HALO == 2 * j) & (c > 0)],
        [lambda x, j: (x < 32) & (x != 15) & (x != 16) & (column(x) // 2 == j)],
        [lambda x, j: (x < 32) & (column(x) == 2 * j)],
        [turn_test(0)],
        [turn_test(1)],
    ]
    + level_tests(0, LANES)
    + level_tests(1, 8)
    + [
        [lambda j, x: x // 2 == j],
        [lambda j, x: j == x // 2 + HALO // 2],
        [lambda x, j: x % 8 == j // HALO],
    ]
)


def tables_kernel(own_ref, *out_refs):
    for tests, out_ref in zip(TABLES, out_refs):
        out_ref[...] = stacked(jnp.concatenate([selection(LANES, test) for test in tests], axis=0))


def pack_rows_kernel(
    res_ref, ground_ref, nodata_ref, patch_ref, own_ref, first_ref, second_ref, nodata_near_ref, patch_near_ref, sem_ref
):
    rows = res_ref.shape[0]
    copies = [
        pltpu.make_async_copy(source, target, sem_ref.at[which])
        for which, (source, target) in enumerate(
            (
                (res_ref, own_ref.at[0]),
                (ground_ref, own_ref.at[1]),
                (nodata_ref, nodata_near_ref),
                (patch_ref, patch_near_ref),
            )
        )
    ]
    for copy in copies:
        copy.start()
    for copy in copies:
        copy.wait()
    own_ref[2] = jnp.where(nodata_near_ref[...] == 0, 1.0, 0.0)
    own_ref[3] = patch_near_ref[...].astype(F32)
    odd = lax.axis_index("row") % 2 == 1
    for which in range(4):
        top = own_ref[which, :HALO]
        bottom = own_ref[which, rows - HALO :]
        part = pl.ds(which * HALO, HALO)
        first_ref[part] = jnp.where(odd, top, bottom)
        second_ref[part] = jnp.where(odd, bottom, top)


def before_after(axis, first, second):
    index = lax.axis_index(axis)
    odd = index % 2 == 1
    before = jnp.where(index > 0, jnp.where(odd, first, second), 0.0)
    after = jnp.where(index < lax.axis_size(axis) - 1, jnp.where(odd, second, first), 0.0)
    return before, after


def pack_cols_kernel(own_ref, from_first_ref, from_second_ref, order_ref, tall_ref, first_ref, second_ref):
    half = own_ref.shape[1] // 2
    shape = first_ref.shape
    group_of = iota(shape, 1) // HALO
    odd = lax.axis_index("col") % 2 == 1
    above, below = before_after("row", from_first_ref[...], from_second_ref[...])
    to_right = jnp.zeros(shape, F32)
    to_left = jnp.zeros(shape, F32)
    for which in range(4):
        part = slice(which * HALO, which * HALO + HALO)
        upper = jnp.concatenate([above[part], own_ref[which, :half]], axis=0)
        lower = jnp.concatenate([own_ref[which, half:], below[part]], axis=0)
        if which < 2:
            upper = jnp.where(upper > 0, upper, 1.0)
            lower = jnp.where(lower > 0, lower, 1.0)
        tall_ref[which, : half + HALO] = upper
        tall_ref[which, half + HALO :] = lower
        for side, values in enumerate((upper, lower)):
            group = 2 * which + side
            here = group_of == group
            to_right = jnp.where(here, rot(values, HALO * group + HALO, 1), to_right)
            to_left = jnp.where(here, rot(values, HALO * group, 1), to_left)
    first_ref[...] = jnp.where(odd, to_left, to_right)
    second_ref[...] = jnp.where(odd, to_right, to_left)


def link(resist, validity, near_resist, near_valid):
    return (validity * near_valid) * (2.0 / (resist + near_resist))


def weights_of(diag):
    return OMEGA / jnp.where(diag > 0, diag, 1.0)


def level_0(fields, odd_column, west, east):
    res, ground, val, patch = fields
    link_w = [west(res[i], val[i], i) for i in range(2)]
    link_e = [east(link_w[i], i) for i in range(2)]
    v_in = link(res[0], val[0], res[1], val[1])
    v_up = link(res[0], val[0], rot(res[1], 1, 0), rot(val[1], 1, 0))
    v_dn = rot(v_up, -1, 0)
    vertical = (v_up, v_dn)
    weight, own, side, away = [], [], [], []
    for i in range(2):
        w = weights_of(ground[i] + v_in + vertical[i] + link_w[i] + link_e[i])
        own.append((1.0 - OMEGA) * val[i] + w * (v_in + jnp.where(odd_column, link_w[i], link_e[i])))
        side.append(w * jnp.where(odd_column, link_e[i], link_w[i]))
        away.append(w * vertical[i])
        weight.append(w * val[i])
    away = [rot(away[0], -1, 0), rot(away[1], 1, 0)]
    return weight, own, side, away, link_w, v_up


def choices(patch, values):
    spread = jnp.where(patch > 0, -0.125, 0.0)
    return [(0.875 * value, spread * value) for value in values]


def pick(test, choice):
    return jnp.where(test, choice[0], choice[1])


def rows_by_parity(ref, which):
    half = ref.shape[1] // 2
    return [ref[which, pl.ds(start, half, stride=2), :] for start in range(2)]


def inner_kernel(tall_ref, both_ref, sum_ref, even_ref, r1_ref, c1_ref, w0_ref, edge_ref, west_ref):
    half = tall_ref.shape[1] // 2
    lane = iota((half, LANES), 1)
    fields = [rows_by_parity(tall_ref, which) for which in range(4)]
    patch = fields[3]
    odd = lane % 2 == 1
    weight, own, side, away, west, v_up = level_0(
        fields,
        odd,
        lambda res, val, i: link(res, val, rot(res, 1, 1), rot(val, 1, 1)),
        lambda value, i: rot(value, -1, 1),
    )
    inside = (lane > 0) & (lane < LANES - 1)
    own, side, away = ([jnp.where(inside, value, 0.0) for value in pair] for pair in (own, side, away))
    kept = slice(HALO // 2, half - HALO // 2)
    for i in range(2):
        w0_ref[i] = weight[i][kept]
        west_ref[i] = jnp.where(lane == 15, rot(west[i], 14, 1), rot(west[i], 17, 1))
    whole_lane = iota((2 * half, LANES), 1)
    for which in range(4):
        value = tall_ref[which]
        edge_ref[which] = jnp.where(whole_lane == 15, rot(value, 15, 1), rot(value, 17, 1))
    c1_ref[0] = dot01([fields[1][0] + fields[1][1]], sum_ref[...])
    c1_ref[1] = dot01([v_up], sum_ref[...])
    c1_ref[2] = dot01([west[0] + west[1]], even_ref[...])
    near = [choices(patch[i], (own[i], side[i])) for i in range(2)]
    patch_away = [rot(patch[0], -1, 0), rot(patch[1], 1, 0)]
    far = [choices(patch_away[i], (away[i],)) for i in range(2)]
    for k in range(RHS - 1):
        tests = [patch[i] == k + 1.0 for i in range(2)]
        tests_away = [patch_away[i] == k + 1.0 for i in range(2)]
        to_own = pick(tests[0], near[0][0]) + pick(tests[1], near[1][0])
        to_own = to_own + (pick(tests_away[0], far[0][0]) + pick(tests_away[1], far[1][0]))
        to_side = pick(tests[0], near[0][1]) + pick(tests[1], near[1][1])
        r1_ref[k] = dot01([to_own, to_side], both_ref[...])


def down_kernel(
    from_first_ref,
    from_second_ref,
    r1_inner_ref,
    c1_inner_ref,
    w0_inner_ref,
    edge_ref,
    west_ref,
    sum_ref,
    even_ref,
    turn_first_ref,
    turn_second_ref,
    usual_both_ref,
    usual_sum_ref,
    usual_even_ref,
    last_both_ref,
    last_sum_ref,
    last_even_ref,
    payload_ref,
    w0_ref,
    r1_ref,
    r2_ref,
    r3_ref,
    w1_ref,
    w2_ref,
    w3_ref,
    ext_ref,
    c1_ref,
    c2_ref,
    c3_ref,
):
    devices = payload_ref.shape[0]
    n1 = edge_ref.shape[1] // 2
    lane = iota((n1, LANES), 1)
    from_left, from_right = before_after("col", from_first_ref[...], from_second_ref[...])
    at_left = (lane < 15) | (lane == LANES - 1)
    at_edge = (lane == 15) | (lane == 16)
    at_right = (lane > 16) & (lane < 33)
    for which in range(4):
        for part in range(2):
            group = 2 * which + part
            rows = pl.ds(part * n1, n1)
            value = jnp.where(at_right, rot(from_right, 17 - HALO * group, 1), 0.0)
            value = jnp.where(at_left, rot(from_left, -1 - HALO * group, 1), value)
            value = jnp.where(at_edge, edge_ref[which, rows, :], value)
            if which < 2:
                value = jnp.where(value > 0, value, 1.0)
            ext_ref[which, rows, :] = value
    fields = [rows_by_parity(ext_ref, which) for which in range(4)]
    weight, own, side, away, west, v_up = level_0(
        fields,
        lane % 2 == 0,
        lambda res, val, i: jnp.where(
            lane == 16, west_ref[i], link(res, val, rot(res, 1, 1), rot(val, 1, 1))
        ),
        lambda value, i: jnp.where(lane == 15, west_ref[i], rot(value, -1, 1)),
    )
    kept = slice(HALO // 2, n1 - HALO // 2)
    for i in range(2):
        value = weight[i][kept]
        full = iota(value.shape, 1)
        w0_ref[i] = jnp.where(
            full == 0, value[:, 15:16], jnp.where(full == LANES - 1, value[:, 16:17], w0_inner_ref[i])
        )

    zeros = jnp.zeros((c1_ref.shape[1] - n1, LANES), F32)
    c1_ref[0, 0:n1] = c1_inner_ref[0] + dot01([fields[1][0] + fields[1][1]], sum_ref[...])
    c1_ref[1, 0:n1] = c1_inner_ref[1] + dot01([v_up], sum_ref[...])
    c1_ref[2, 0:n1] = c1_inner_ref[2] + dot01([west[0] + west[1]], even_ref[...])
    for index in range(3):
        c1_ref[index, n1:] = zeros

    outer = lane < 32

    def twice(value):
        return value + rot(value, 64, 1)

    own, side, away, patch = (
        [jnp.where(outer, value, 0.0) for value in pair] for pair in (own, side, away, fields[3])
    )
    patch = [value + rot(value, 32, 1) for value in patch]
    later = jnp.where(lane >= 64, 1.0, 0.0)
    patch = [twice(value) for value in patch]
    both = [twice(own[i] + rot(side[i], 32, 1)) for i in range(2)]
    away = [twice(value) for value in away]
    patch_away = [rot(patch[0], -1, 0), rot(patch[1], 1, 0)]
    terms = []
    for value, entry in ((patch[0], both[0]), (patch[1], both[1]), (patch_away[0], away[0]), (patch_away[1], away[1])):
        terms.append((value - later, choices(value, (entry,))[0]))

    turns = (turn_first_ref, turn_second_ref)
    for first in range(0, RHS, 2):
        picked = [pick(value == first + 1.0, choice) for value, choice in terms]
        outer_part = (picked[0] + picked[1]) + (picked[2] + picked[3])
        for k in range(first, min(first + 2, RHS - 1)):
            r1_ref[k, 0:n1] = r1_inner_ref[k] + dot01([outer_part], turns[k - first][...])
            r1_ref[k, n1:] = zeros

    usual = (usual_both_ref, usual_sum_ref, usual_even_ref)
    last = (last_both_ref, last_sum_ref, last_even_ref)
    for r_ref, c_ref, w_ref, next_r, next_c in (
        (r1_ref, c1_ref, w1_ref, r2_ref, c2_ref),
        (r2_ref, c2_ref, w2_ref, r3_ref, c3_ref),
        (r3_ref, c3_ref, w3_ref, None, None),
    ):
        half = r_ref.shape[1] // 2
        even, uneven = pl.ds(0, half, stride=2), pl.ds(1, half, stride=2)
        odd_lane = iota((half, LANES), 1) % 2 == 1
        ge, go = c_ref[0, even, :], c_ref[0, uneven, :]
        v_up, v_in = c_ref[1, even, :], c_ref[1, uneven, :]
        we, wo = c_ref[2, even, :], c_ref[2, uneven, :]
        ee, eo = rot(we, -1, 1), rot(wo, -1, 1)
        v_dn = rot(v_up, -1, 0)
        w_e = weights_of(ge + v_up + v_in + we + ee)
        w_o = weights_of(go + v_in + v_dn + wo + eo)
        a_e = (1.0 - OMEGA) + w_e * (v_in + jnp.where(odd_lane, we, ee))
        a_o = (1.0 - OMEGA) + w_o * (v_in + jnp.where(odd_lane, wo, eo))
        b_e = w_e * jnp.where(odd_lane, ee, we)
        b_o = w_o * jnp.where(odd_lane, eo, wo)
        c_e = w_e * v_up
        c_o = w_o * v_dn
        w_ref[0] = w_e
        w_ref[1] = w_o
        both, inner, evens = (table[...] for table in (usual if next_r is not None else last))
        coarser = [dot01([ge + go], inner), dot01([v_up], inner), dot01([we + wo], evens)]
        fields = []
        for k in range(RHS - 1):
            re, ro = r_ref[k, even, :], r_ref[k, uneven, :]
            own = a_e * re + a_o * ro + rot(c_o * ro, 1, 0) + rot(c_e * re, -1, 0)
            side = b_e * re + b_o * ro
            fields.append(dot01([own, side], both))
        if next_r is not None:
            for index in range(3):
                next_c[index] = coarser[index]
            for k in range(RHS - 1):
                next_r[k] = fields[k]

    shape = fields[0].shape
    mine = iota(shape, 1) // 8 == iota(shape, 0) - 1

    def flat(field):
        return jnp.sum(jnp.where(mine, field, 0.0), axis=0, keepdims=True)

    sub = iota((8, LANES), 0)
    lane8 = iota((8, LANES), 1)
    links = jnp.where(sub < 4, flat(coarser[1]), flat(coarser[2]))
    turned = rot(links, 96, 1)
    for row in (1, 2):
        turned = jnp.where(sub % 4 == row, rot(links, 96 - 32 * row, 1), turned)
    tile = jnp.broadcast_to(flat(coarser[0]), (8, LANES))
    for k in range(RHS - 1):
        tile = jnp.where(sub == k, flat(fields[k]), tile)
    tile = jnp.where(lane8 < 96, tile, turned)

    @pl.loop(0, devices)
    def _(device):
        payload_ref[device] = tile


def up_kernel(
    own_ref,
    w0_ref,
    r1_ref,
    r2_ref,
    r3_ref,
    w1_ref,
    w2_ref,
    w3_ref,
    spread_ref,
    finest_ref,
    base_ref,
    t3_ref,
    t2_ref,
    t1_ref,
):
    for r_ref, w_ref, coarse_ref, t_ref in (
        (r3_ref, w3_ref, None, t3_ref),
        (r2_ref, w2_ref, t3_ref, t2_ref),
        (r1_ref, w1_ref, t2_ref, t1_ref),
    ):
        half = w_ref.shape[1]
        for k in range(RHS - 1):
            finer = None if coarse_ref is None else dot01([coarse_ref[k]], spread_ref[...])
            for index in range(2):
                rows = pl.ds(index, half, stride=2)
                smoothed = w_ref[index] * r_ref[k, rows, :]
                t_ref[k, rows, :] = smoothed if finer is None else finer + smoothed
    half = w0_ref.shape[1]
    sides = []
    for index in range(2):
        rows = pl.ds(index, half, stride=2)
        patch = own_ref[3, rows, :]
        sides.append((rows, patch, choices(patch, (w0_ref[index],))[0]))
    left_over = None
    for k in range(RHS):
        if k + 1 < RHS:
            coarse = t1_ref[k, pl.ds(HALO // 2, half)]
            left_over = -coarse if left_over is None else left_over - coarse
        else:
            coarse = left_over
        finer = dot01([coarse], finest_ref[...])
        for rows, patch, choice in sides:
            base_ref[k, rows, :] = finer + pick(patch == k + 1.0, choice)


def solve_kernel(
    grid,
    all_ref,
    base_ref,
    widen_ref,
    out_ref,
    coef_ref,
    x_ref,
    r_ref,
    q_ref,
    p_ref,
    p_up_ref,
    p_down_ref,
    p_first_ref,
    p_last_ref,
    u_ref,
    done_ref,
    sem_ref,
):
    grid_rows, grid_cols = grid
    count = grid_rows * grid_cols
    lane = iota((8, LANES), 1)
    column = lane % 8

    def choose(test, yes, no):
        if isinstance(test, bool):
            return yes if test else no
        return jnp.where(test, yes, no)

    def at(t):
        return pl.ds(8 * t if isinstance(t, int) else pl.multiple_of(8 * t, 8), 8)

    def every(body, init):
        if count <= 64:
            for tile in range(count):
                init = body(tile, init)
            return init
        return lax.fori_loop(0, count, body, init)

    all_lane = iota((count, LANES), 1)
    inside = all_lane < 96
    rows = [all_ref[pl.ds(i, count, stride=8), :] for i in range(8)]
    north, west = (
        jnp.where(
            all_lane < 32,
            rot(rows[i], 32, 1),
            jnp.where(all_lane < 64, rot(rows[i + 1], 64, 1), rot(rows[i + 2], 96, 1)),
        )
        for i in (0, 4)
    )
    north, west = jnp.where(inside, north, 0.0), jnp.where(inside, west, 0.0)
    north_below = jnp.concatenate([north[grid_cols:], jnp.zeros((grid_cols, LANES), F32)], axis=0)
    south = jnp.where(all_lane >= 88, rot(north_below, 88, 1), rot(north, 120, 1))
    west_right = jnp.where(iota((count, LANES), 0) % grid_cols < grid_cols - 1, rot(west, -1, 0), 0.0)
    east = jnp.where(all_lane % 8 == 7, rot(west_right, 7, 1), rot(west, 127, 1))
    south, east = jnp.where(inside, south, 0.0), jnp.where(inside, east, 0.0)
    coef_ref[0] = jnp.where(inside, rows[7], 0.0) + north + south + west + east
    coef_ref[1] = north
    coef_ref[2] = south
    coef_ref[3] = west
    coef_ref[4] = east
    others = ((rows[0] + rows[1]) + (rows[2] + rows[3])) + ((rows[4] + rows[5]) + rows[6])
    r_ref[...] = jnp.where(iota(r_ref.shape, 1) < 96, all_ref[...], 0.0)
    r_ref[pl.ds(7, count, stride=8), :] = jnp.where(inside, -others, 0.0)

    def total(values):
        return jnp.sum(values, axis=1, keepdims=True)

    def direct(t, values):
        p_ref[at(t), :] = values
        p_up_ref[at(t), :] = rot(values, 8, 1)
        p_down_ref[at(t), :] = rot(values, 120, 1)
        p_last_ref[at(t), :] = rot(values, 40, 1)
        p_first_ref[at(t), :] = rot(values, 88, 1)

    def begin(t, norm):
        values = r_ref[at(t), :]
        direct(t, values)
        return norm + values * values

    zero = jnp.zeros((8, LANES), F32)
    rr = total(every(begin, zero))

    def image_of(t, dot):
        here = p_ref[at(t), :]
        up = p_last_ref[at(choose(t >= grid_cols, t - grid_cols, t)), :]
        down = p_first_ref[at(choose(t + grid_cols < count, t + grid_cols, t)), :]
        left = p_down_ref[at(choose(t % grid_cols > 0, t - 1, t)), :]
        right = p_up_ref[at(choose(t % grid_cols < grid_cols - 1, t + 1, t)), :]
        up = jnp.where(lane < 8, up, p_up_ref[at(t), :])
        down = jnp.where(lane >= 88, down, p_down_ref[at(t), :])
        left = rot(jnp.where(column == 7, left, here), 1, 1)
        right = rot(jnp.where(column == 0, right, here), -1, 1)
        pulled = coef_ref[1, pl.ds(t, 1), :] * up + coef_ref[2, pl.ds(t, 1), :] * down
        pulled = pulled + coef_ref[3, pl.ds(t, 1), :] * left + coef_ref[4, pl.ds(t, 1), :] * right
        image = coef_ref[0, pl.ds(t, 1), :] * here - pulled
        q_ref[at(t), :] = image
        return dot + here * image

    for sweep in range(ITERS - 1):
        step = jnp.broadcast_to(rr / total(every(image_of, zero)), (8, LANES))

        def advance(t, norm):
            left_over = r_ref[at(t), :] - step * q_ref[at(t), :]
            r_ref[at(t), :] = left_over
            return norm + left_over * left_over

        new = total(every(advance, zero))
        ratio = jnp.broadcast_to(new / rr, (8, LANES))
        rr = new

        def turn(t, carry):
            values = p_ref[at(t), :]
            gain = step * values
            x_ref[at(t), :] = gain if sweep == 0 else x_ref[at(t), :] + gain
            direct(t, r_ref[at(t), :] + ratio * values)
            return carry

        every(turn, 0)

    step = jnp.broadcast_to(rr / total(every(image_of, zero)), (8, LANES))
    device = lax.axis_index("row") * grid_cols + lax.axis_index("col")
    mine = x_ref[at(device), :] + step * p_ref[at(device), :]
    groups = u_ref.shape[0] // 8
    placed = jnp.concatenate([jnp.where(lane // 8 == i, mine, 0.0) for i in range(groups)], axis=0)
    u_ref[...] = dot01([placed], widen_ref[...])
    copies = []
    for k in range(RHS):
        for i in range(groups):
            rows = pl.ds(HALO * i, HALO)
            done_ref[k, rows, :] = base_ref[k, rows, :] + u_ref[pl.ds(8 * i + k, 1), :]
        copy = pltpu.make_async_copy(done_ref.at[k], out_ref.at[k], sem_ref.at[k])
        copy.start()
        copies.append(copy)
    for copy in copies:
        copy.wait()


def exchanged(first, second, axis, other):
    sizes = {name: lax.axis_size(name) for name in (axis, other)}

    def pairs(step):
        found = []
        for i in range(sizes["row"]):
            for j in range(sizes["col"]):
                place = {"row": i, "col": j}
                target = dict(place)
                at = place[axis]
                if step == 0:
                    target[axis] = at ^ 1
                elif at in (0, sizes[axis] - 1):
                    target[other] = place[other] ^ 1
                else:
                    target[axis] = at + 1 if at % 2 else at - 1
                found.append((i * sizes["col"] + j, target["row"] * sizes["col"] + target["col"]))
        return found

    return [lax.ppermute(part, ("row", "col"), pairs(step)) for step, part in enumerate((first, second))]


def shards(resistance, ground, nodata, patch_ids):
    grid = (lax.axis_size("row"), lax.axis_size("col"))
    devices = grid[0] * grid[1]
    rows, cols = resistance.shape
    own = [pltpu.with_memory_space_constraint(part, pltpu.HBM) for part in (resistance, ground, nodata, patch_ids)]
    def near(value):
        return pltpu.with_memory_space_constraint(value, pltpu.VMEM)

    def call(kernel, outs, scratch, *args, **options):
        outs = tuple(pltpu.VMEM(out, F32) if isinstance(out, tuple) else out for out in outs)
        scratch = [pltpu.VMEM(part, F32) if isinstance(part, tuple) else part for part in scratch]
        name = kernel.__name__
        params = pltpu.CompilerParams(vmem_limit_bytes=VMEM_LIMIT)
        return pl.pallas_call(
            kernel, out_shape=outs, scratch_shapes=scratch, name=name, compiler_params=params, **options
        )(*args)

    def all_near(values):
        return [near(value) for value in values]

    strip = (4 * HALO, cols)
    kept, first, second = call(
        pack_rows_kernel,
        [(4, rows, cols), strip, strip],
        [pltpu.VMEM((rows, cols), jnp.int32)] * 2 + [pltpu.SemaphoreType.DMA((4,))],
        *own,
        in_specs=[pl.BlockSpec(memory_space=pltpu.HBM)] * 4,
    )
    first, second = exchanged(first, second, "row", "col")
    tall_rows = rows + 2 * HALO
    strip = (tall_rows // 2, LANES)
    kept = near(kept)
    tables = all_near(
        call(
            tables_kernel,
            [pltpu.VMEM((PIECES * LANES * len(tests), LANES), BF16) for tests in TABLES],
            [],
            kept,
            cost_estimate=pl.CostEstimate(flops=10**7, bytes_accessed=10**6, transcendentals=0),
        )
    )
    tall, first, second = call(
        pack_cols_kernel, [(4, tall_rows, cols), strip, strip], [], kept, near(first), near(second), tables[0]
    )
    first, second = exchanged(first, second, "col", "row")
    sizes = [128, 64, 32]
    n1 = tall_rows // 2
    inner = call(
        inner_kernel,
        [(RHS - 1, n1, LANES), (3, n1, LANES), (2, rows // 2, LANES), (4, tall_rows, LANES), (2, n1, LANES)],
        [],
        near(tall),
        *tables[:3],
        cost_estimate=pl.CostEstimate(flops=10**8, bytes_accessed=10**6, transcendentals=0),
    )
    payload, w0, *levels = call(
        down_kernel,
        [(devices, 8, LANES), (2, rows // 2, LANES)]
        + [(RHS - 1, size, LANES) for size in sizes]
        + [(2, size // 2, LANES) for size in sizes],
        [(4, tall_rows, LANES)] + [(3, size, LANES) for size in sizes],
        *all_near((first, second, *inner)),
        *tables[3:13],
    )
    everything = lax.all_to_all(payload, ("row", "col"), 0, 0)
    (base,) = call(
        up_kernel,
        [(RHS, rows, cols)],
        [(RHS - 1, size, LANES) for size in sizes[::-1]],
        kept,
        *all_near([w0] + levels),
        *tables[13:15],
        cost_estimate=pl.CostEstimate(flops=10**8, bytes_accessed=10**6, transcendentals=0),
    )
    return pl.pallas_call(
        functools.partial(solve_kernel, grid),
        out_shape=jax.ShapeDtypeStruct((RHS, rows, cols), F32),
        out_specs=pl.BlockSpec(memory_space=pl.ANY),
        scratch_shapes=[pltpu.VMEM((5, devices, LANES), F32)]
        + [pltpu.VMEM((devices * 8, LANES), F32)] * 8
        + [pltpu.VMEM((rows // HALO * 8, LANES), F32), pltpu.VMEM((RHS, rows, cols), F32)]
        + [pltpu.SemaphoreType.DMA((RHS,))],
        compiler_params=pltpu.CompilerParams(vmem_limit_bytes=VMEM_LIMIT),
        name="solve_kernel",
    )(near(everything.reshape(devices * 8, LANES)), near(base), tables[15])


def solution(mesh):
    spec = P("row", "col")
    return jax.shard_map(shards, mesh=mesh, in_specs=(spec,) * 4, out_specs=P(None, "row", "col"), check_vma=False)
```

time: 32.6 us -> 30.8 us (0.945)
  waiting for transfers between devices: 11.6 us -> 10.7 us
  Pallas kernels: 8.9 us -> 8.11 us
    ppermute x4, waiting for transfers between devices: 4.05 us -> 3.04 us  [exchanged(): lax.ppermute(part, ('row', 'col'), pairs(step))]
    pallas_call x1, Pallas kernels: 3.44 us -> 2.87 us  [shards(): pl.pallas_call(functools.partial(solve_kernel, grid), out_shape=jax.Shape...]
    pallas_call x4 -> x6, Pallas kernels: 5.47 us -> 5.24 us  [call(): pl.pallas_call(kernel, out_shape=outs, scratch_shapes=scratch, name=name,...]
  transfers between devices with their start and end apart: 5 -> 5, of which waited for: 3 -> 3; matrix products, arithmetic and copies ran while one was open for 0% -> 0% of each run, Pallas kernels for 2% -> 5%
where the time goes in v4:
time: 30.8 us; the launch traced here: 30.7 us
  starting transfers between devices  11.8 us (38%)
  waiting for transfers between devices  10.7 us (35%)
  Pallas kernels  8.11 us (26%)
    all_to_all x1, waiting for transfers between devices, shards(): everything = lax.all_to_all(payload, ('row', 'col'), 0, 0)  7.65 us
    ppermute x4, starting transfers between devices, exchanged(): lax.ppermute(part, ('row', 'col'), pairs(step))  6.4 us
    all_to_all x1, starting transfers between devices, shards(): everything = lax.all_to_all(payload, ('row', 'col'), 0, 0)  5.39 us
    pallas_call x6, Pallas kernels, call(): pl.pallas_call(kernel, out_shape=outs, scratch_shapes=scratch, name=name,...  5.24 us
    ppermute x4, waiting for transfers between devices, exchanged(): lax.ppermute(part, ('row', 'col'), pairs(step))  3.04 us
    pallas_call x1, Pallas kernels, shards(): pl.pallas_call(functools.partial(solve_kernel, grid), out_shape=jax.Shape...  2.87 us
  transfers between devices with their start and end apart: 5, of which 3 were waited for; matrix products, arithmetic and copies ran while one was open for 0% of the time, Pallas kernels for 5%

profile of v4, /device:TPU:0, one launch (start us, length us, event | category | flops | bytes accessed | tf_op | source)
XLA Modules:
  0.0 30.7 jit_solution(13534838597682540003)
XLA Ops:
  0.0 1.1 %pack_rows_kernel.1 = (f32[4,192,128]{2,1,0:T(8,128)S(1)}, f32[64,128]{1,0:T(8,128)S(1)}, f32[64,128]{1,0:T(8,128)S(1)}) custom-call(f32[192,128]{1,0:T(8,128)} %res_ref.1, f32[192,128]{1,0:T(8,128)} %ground_ref.1, s32[192,128]{1,0:T(8,128)} %nodata_ref.1, s32[192,128]{1,0:T(8,128)} %patch_ref.1), custom_call_target="tpu_custom_call" | custom-call | tf_op jit(solution)/shard_map/pack_rows_kernel/pallas_call | solution.py:622
  1.1 3.1 %collective-permute-start = (f32[64,128]{1,0:T(8,128)S(1)}, f32[64,128]{1,0:T(8,128)S(1)}, u32[]{:S(2)}, u32[]{:S(2)}) collective-permute-start(f32[64,128]{1,0:T(8,128)S(1)} %get-tuple-element.41), channel_id=1, source_target_pairs={{0,8},{1,9},{2,10},{3,11},{4,12},{5,13},{6,14},{7,15},{8,0},{9,1},... | collective-permute-start | bytes 98312 | tf_op jit(solution)/shard_map/ppermute | solution.py:606
  4.2 0.0 collective-permute-start.1
  4.2 0.1 tables_kernel.1
  4.4 1.7 %collective-permute-done.from_first_ref = f32[64,128]{1,0:T(8,128)S(1)} collective-permute-done((f32[64,128]{1,0:T(8,128)S(1)}, f32[64,128]{1,0:T(8,128)S(1)}, u32[]{:S(2)}, u32[]{:S(2)}) %collective-permute-start) | collective-permute-done | bytes 32800 | tf_op jit(solution)/shard_map/ppermute | solution.py:606
  6.1 0.0 collective-permute-done.1.from_second_ref
  6.1 0.3 pack_cols_kernel.1
  6.4 0.1 collective-permute-start.2
  6.5 3.2 %collective-permute-start.3 = (f32[112,128]{1,0:T(8,128)S(1)}, f32[112,128]{1,0:T(8,128)S(1)}, u32[]{:S(2)}, u32[]{:S(2)}) collective-permute-start(f32[112,128]{1,0:T(8,128)S(1)} %get-tuple-element.45), channel_id=1, source_target_pairs={{0,8},{1,2},{2,1},{3,4},{4,3},{5,6},{6,5},{7,15},{8,0},{9,10},{10,... | collective-permute-start | bytes 172040 | tf_op jit(solution)/shard_map/ppermute | solution.py:606
  9.7 0.8 %inner_kernel.1 = (f32[7,112,128]{2,1,0:T(8,128)S(1)}, f32[3,112,128]{2,1,0:T(8,128)S(1)}, f32[2,96,128]{2,1,0:T(8,128)S(1)}, f32[4,224,128]{2,1,0:T(8,128)S(1)}, f32[2,112,128]{2,1,0:T(8,128)S(1)}) custom-call(f32[4,224,128]{2,1,0:T(8,128)S(1)} %get-tuple-element.46.tall_ref, bf16[512,128]{1,0:T(8,128)(2,1)S(1)} %get-tuple-element.43.order_ref.both_ref, ...), custom_call_target="tpu_custom_call" | custom-call | flops 100000000 | bytes 1000000 | tf_op jit(solution)/shard_map/inner_kernel/pallas_call | solution.py:622
  10.5 0.0 collective-permute-done.2.from_first_ref
  10.6 1.3 %collective-permute-done.3.from_second_ref = f32[112,128]{1,0:T(8,128)S(1)} collective-permute-done((f32[112,128]{1,0:T(8,128)S(1)}, f32[112,128]{1,0:T(8,128)S(1)}, u32[]{:S(2)}, u32[]{:S(2)}) %collective-permute-start.3) | collective-permute-done | bytes 57376 | tf_op jit(solution)/shard_map/ppermute | solution.py:606
  11.8 2.3 %down_kernel.1 = (f32[32,8,128]{2,1,0:T(8,128)}, f32[2,96,128]{2,1,0:T(8,128)S(1)}, f32[7,128,128]{2,1,0:T(8,128)S(1)}, f32[7,64,128]{2,1,0:T(8,128)S(1)}, f32[7...) custom-call(f32[112,128]{1,0:T(8,128)S(1)} %collective-permute-done.2.f, ...), custom_call_target="tpu_custom_call" | custom-call | tf_op jit(solution)/shard_map/down_kernel/pallas_call | solution.py:622
  14.2 5.4 %all-to-all-start = ((f32[32,8,128]{2,1,0:T(8,128)}), f32[32,8,128]{2,1,0:T(8,128)S(1)}, u32[]{:S(2)}, u32[]{:S(2)}) async-start(f32[32,8,128]{2,1,0:T(8,128)} %get-tuple-element.64), calls=%async_computation | async-start | bytes 262144 | tf_op jit(solution)/shard_map/all_to_all | solution.py:673
  19.6 0.5 %up_kernel.1.base_ref = f32[8,192,128]{2,1,0:T(8,128)S(1)} custom-call(f32[4,192,128]{2,1,0:T(8,128)S(1)} %get-tuple-element.40.own_ref, f32[2,96,128]{2,1,0:T(8,128)S(1)} %get-tuple-element.65.w0_ref, f32[7,128,128]{2,1,0:T(8,128)S(1)} %get-tuple-element.66.r1_ref, f32[7,64,128]{2,1,0:T(8,128)S(1)} %get-tuple-element.67.r2_ref, ...), custom_call_target="tpu_custom_call" | custom-call | flops 100000000 | bytes 1000000 | tf_op jit(solution)/shard_map/up_kernel/pallas_call | solution.py:622
  20.1 7.7 %all-to-all-done = f32[32,8,128]{2,1,0:T(8,128)S(1)} async-done(((f32[32,8,128]{2,1,0:T(8,128)}), f32[32,8,128]{2,1,0:T(8,128)S(1)}, u32[]{:S(2)}, u32[]{:S(2)}) %all-to-all-start) | async-done | bytes 131104 | tf_op jit(solution)/shard_map/all_to_all | solution.py:673
  27.8 2.9 %solve_kernel.1 = f32[8,192,128]{2,1,0:T(8,128)} custom-call(f32[256,128]{1,0:T(8,128)S(1)} %bitcast.1, f32[8,192,128]{2,1,0:T(8,128)S(1)} %up_kernel.1.base_ref, bf16[256,128]{1,0:T(8,128)(2,1)S(1)} %get-tuple-element.74.widen_ref), custom_call_target="tpu_custom_call" | custom-call | tf_op jit(solution)/shard_map/solve_kernel/pallas_call | solution.py:683
Async XLA Ops:
  1.1 5.0 %collective-permute-start = (f32[64,128]{1,0:T(8,128)S(1)}, f32[64,128]{1,0:T(8,128)S(1)}, u32[]{:S(2)}, u32[]{:S(2)}) collective-permute-start(f32[64,128]{1,0:T(8,128)S(1)} %get-tuple-element.41), channel_id=1, source_target_pairs={{0,8},{1,9},{2,10},{3,11},{4,12},{5,13},{6,14},{7,15},{8,0},{9,1},... | collective-permute-start | bytes 98312 | tf_op jit(solution)/shard_map/ppermute | solution.py:606
  4.2 1.9 %collective-permute-start.1 = (f32[64,128]{1,0:T(8,128)S(1)}, f32[64,128]{1,0:T(8,128)S(1)}, u32[]{:S(2)}, u32[]{:S(2)}) collective-permute-start(f32[64,128]{1,0:T(8,128)S(1)} %get-tuple-element.42), channel_id=1, source_target_pairs={{0,1},{1,0},{2,3},{3,2},{4,5},{5,4},{6,7},{7,6},{8,16},{9,17},{10,... | collective-permute-start | bytes 98312 | tf_op jit(solution)/shard_map/ppermute | solution.py:606
  6.4 4.1 %collective-permute-start.2 = (f32[112,128]{1,0:T(8,128)S(1)}, f32[112,128]{1,0:T(8,128)S(1)}, u32[]{:S(2)}, u32[]{:S(2)}) collective-permute-start(f32[112,128]{1,0:T(8,128)S(1)} %get-tuple-element.44), channel_id=1, source_target_pairs={{0,1},{1,0},{2,3},{3,2},{4,5},{5,4},{6,7},{7,6},{8,9},{9,8},{10,11... | collective-permute-start | bytes 172040 | tf_op jit(solution)/shard_map/ppermute | solution.py:606
  6.5 5.4 %collective-permute-start.3 = (f32[112,128]{1,0:T(8,128)S(1)}, f32[112,128]{1,0:T(8,128)S(1)}, u32[]{:S(2)}, u32[]{:S(2)}) collective-permute-start(f32[112,128]{1,0:T(8,128)S(1)} %get-tuple-element.45), channel_id=1, source_target_pairs={{0,8},{1,2},{2,1},{3,4},{4,3},{5,6},{6,5},{7,15},{8,0},{9,10},{10,... | collective-permute-start | bytes 172040 | tf_op jit(solution)/shard_map/ppermute | solution.py:606
  14.2 13.6 %all-to-all-start = ((f32[32,8,128]{2,1,0:T(8,128)}), f32[32,8,128]{2,1,0:T(8,128)S(1)}, u32[]{:S(2)}, u32[]{:S(2)}) async-start(f32[32,8,128]{2,1,0:T(8,128)} %get-tuple-element.64), calls=%async_computation | async-start | bytes 262144 | tf_op jit(solution)/shard_map/all_to_all | solution.py:673

commit v5 on v4

--- a/solution.py
+++ b/solution.py
@@ -94,21 +94,44 @@
 )
 
 
-def tables_kernel(own_ref, *out_refs):
-    for tests, out_ref in zip(TABLES, out_refs):
-        out_ref[...] = stacked(jnp.concatenate([selection(LANES, test) for test in tests], axis=0))
-
-
-def pack_rows_kernel(
-    res_ref, ground_ref, nodata_ref, patch_ref, own_ref, first_ref, second_ref, nodata_near_ref, patch_near_ref, sem_ref
-):
+def pack_rows_kernel(res_ref, ground_ref, nodata_ref, patch_ref, first_ref, second_ref, real_ref, whole_ref, sem_ref):
     rows = res_ref.shape[0]
+    starts = (0, rows - HALO)
+    copies = []
+    for which, source in enumerate((res_ref, ground_ref, nodata_ref, patch_ref)):
+        near_ref = real_ref if which < 2 else whole_ref
+        for end in range(2):
+            target = near_ref.at[2 * (which % 2) + end]
+            part = source.at[pl.ds(starts[end], HALO)]
+            copies.append(pltpu.make_async_copy(part, target, sem_ref.at[2 * which + end]))
+    for copy in copies:
+        copy.start()
+    for copy in copies:
+        copy.wait()
+    odd = lax.axis_index("row") % 2 == 1
+    for which in range(4):
+        if which < 2:
+            top, bottom = real_ref[2 * which], real_ref[2 * which + 1]
+        elif which == 2:
+            top, bottom = (jnp.where(whole_ref[end] == 0, 1.0, 0.0) for end in range(2))
+        else:
+            top, bottom = whole_ref[2].astype(F32), whole_ref[3].astype(F32)
+        part = pl.ds(which * HALO, HALO)
+        first_ref[part] = jnp.where(odd, top, bottom)
+        second_ref[part] = jnp.where(odd, bottom, top)
+
+
+def prepare_kernel(res_ref, ground_ref, nodata_ref, patch_ref, order_ref, tall_ref, first_ref, second_ref, *rest):
+    table_refs = rest[: len(TABLES)]
+    nodata_near_ref, patch_near_ref, sem_ref = rest[len(TABLES) :]
+    rows = res_ref.shape[0]
+    middle = pl.ds(HALO, rows)
     copies = [
         pltpu.make_async_copy(source, target, sem_ref.at[which])
         for which, (source, target) in enumerate(
             (
-                (res_ref, own_ref.at[0]),
-                (ground_ref, own_ref.at[1]),
+                (res_ref, tall_ref.at[0, middle]),
+                (ground_ref, tall_ref.at[1, middle]),
                 (nodata_ref, nodata_near_ref),
                 (patch_ref, patch_near_ref),
             )
@@ -116,44 +139,22 @@
     ]
     for copy in copies:
         copy.start()
+    for tests, table_ref in zip(TABLES, table_refs):
+        table_ref[...] = stacked(jnp.concatenate([selection(LANES, test) for test in tests], axis=0))
     for copy in copies:
         copy.wait()
-    own_ref[2] = jnp.where(nodata_near_ref[...] == 0, 1.0, 0.0)
-    own_ref[3] = patch_near_ref[...].astype(F32)
-    odd = lax.axis_index("row") % 2 == 1
-    for which in range(4):
-        top = own_ref[which, :HALO]
-        bottom = own_ref[which, rows - HALO :]
-        part = pl.ds(which * HALO, HALO)
-        first_ref[part] = jnp.where(odd, top, bottom)
-        second_ref[part] = jnp.where(odd, bottom, top)
-
-
-def before_after(axis, first, second):
-    index = lax.axis_index(axis)
-    odd = index % 2 == 1
-    before = jnp.where(index > 0, jnp.where(odd, first, second), 0.0)
-    after = jnp.where(index < lax.axis_size(axis) - 1, jnp.where(odd, second, first), 0.0)
-    return before, after
-
-
-def pack_cols_kernel(own_ref, from_first_ref, from_second_ref, order_ref, tall_ref, first_ref, second_ref):
-    half = own_ref.shape[1] // 2
+    tall_ref[2, middle] = jnp.where(nodata_near_ref[...] == 0, 1.0, 0.0)
+    tall_ref[3, middle] = patch_near_ref[...].astype(F32)
+    half = rows // 2
     shape = first_ref.shape
     group_of = iota(shape, 1) // HALO
     odd = lax.axis_index("col") % 2 == 1
-    above, below = before_after("row", from_first_ref[...], from_second_ref[...])
     to_right = jnp.zeros(shape, F32)
     to_left = jnp.zeros(shape, F32)
+    edge = jnp.zeros((HALO, shape[1]), F32)
     for which in range(4):
-        part = slice(which * HALO, which * HALO + HALO)
-        upper = jnp.concatenate([above[part], own_ref[which, :half]], axis=0)
-        lower = jnp.concatenate([own_ref[which, half:], below[part]], axis=0)
-        if which < 2:
-            upper = jnp.where(upper > 0, upper, 1.0)
-            lower = jnp.where(lower > 0, lower, 1.0)
-        tall_ref[which, : half + HALO] = upper
-        tall_ref[which, half + HALO :] = lower
+        upper = jnp.concatenate([edge, tall_ref[which, pl.ds(HALO, half)]], axis=0)
+        lower = jnp.concatenate([tall_ref[which, pl.ds(HALO + half, half)], edge], axis=0)
         for side, values in enumerate((upper, lower)):
             group = 2 * which + side
             here = group_of == group
@@ -161,6 +162,40 @@
             to_left = jnp.where(here, rot(values, HALO * group, 1), to_left)
     first_ref[...] = jnp.where(odd, to_left, to_right)
     second_ref[...] = jnp.where(odd, to_right, to_left)
+
+
+def before_after(axis, first, second):
+    index = lax.axis_index(axis)
+    odd = index % 2 == 1
+    before = jnp.where(index > 0, jnp.where(odd, first, second), 0.0)
+    after = jnp.where(index < lax.axis_size(axis) - 1, jnp.where(odd, second, first), 0.0)
+    return before, after
+
+
+def pack_cols_kernel(
+    from_first_ref, from_second_ref, tall_in_ref, first_in_ref, second_in_ref, tall_ref, first_ref, second_ref
+):
+    rows = tall_ref.shape[1]
+    ends = (pl.ds(0, HALO), pl.ds(rows // 2 - HALO, HALO))
+    odd = lax.axis_index("col") % 2 == 1
+    nearby = before_after("row", from_first_ref[...], from_second_ref[...])
+    group_of = iota((HALO, LANES), 1) // HALO
+    for side in range(2):
+        first = first_in_ref[ends[side], :]
+        second = second_in_ref[ends[side], :]
+        for which in range(4):
+            values = nearby[side][which * HALO : which * HALO + HALO]
+            if which < 2:
+                values = jnp.where(values > 0, values, 1.0)
+            tall_ref[which, pl.ds(side * (rows - HALO), HALO)] = values
+            group = 2 * which + side
+            here = group_of == group
+            to_right = rot(values, HALO * group + HALO, 1)
+            to_left = rot(values, HALO * group, 1)
+            first = jnp.where(here, jnp.where(odd, to_left, to_right), first)
+            second = jnp.where(here, jnp.where(odd, to_right, to_left), second)
+        first_ref[ends[side], :] = first
+        second_ref[ends[side], :] = second
 
 
 def link(resist, validity, near_resist, near_valid):
@@ -401,7 +436,7 @@
 
 
 def up_kernel(
-    own_ref,
+    tall_ref,
     w0_ref,
     r1_ref,
     r2_ref,
@@ -432,7 +467,7 @@
     sides = []
     for index in range(2):
         rows = pl.ds(index, half, stride=2)
-        patch = own_ref[3, rows, :]
+        patch = tall_ref[3, pl.ds(HALO + index, half, stride=2), :]
         sides.append((rows, patch, choices(patch, (w0_ref[index],))[0]))
     left_over = None
     for k in range(RHS):
@@ -529,6 +564,9 @@
     zero = jnp.zeros((8, LANES), F32)
     rr = total(every(begin, zero))
 
+    def coef_of(index, t):
+        return coef_ref[index, pl.ds(t, 8, stride=0), :]
+
     def image_of(t, dot):
         here = p_ref[at(t), :]
         up = p_last_ref[at(choose(t >= grid_cols, t - grid_cols, t)), :]
@@ -539,9 +577,9 @@
         down = jnp.where(lane >= 88, down, p_down_ref[at(t), :])
         left = rot(jnp.where(column == 7, left, here), 1, 1)
         right = rot(jnp.where(column == 0, right, here), -1, 1)
-        pulled = coef_ref[1, pl.ds(t, 1), :] * up + coef_ref[2, pl.ds(t, 1), :] * down
-        pulled = pulled + coef_ref[3, pl.ds(t, 1), :] * left + coef_ref[4, pl.ds(t, 1), :] * right
-        image = coef_ref[0, pl.ds(t, 1), :] * here - pulled
+        pulled = coef_of(1, t) * up + coef_of(2, t) * down
+        pulled = pulled + coef_of(3, t) * left + coef_of(4, t) * right
+        image = coef_of(0, t) * here - pulled
         q_ref[at(t), :] = image
         return dot + here * image
 
@@ -575,8 +613,10 @@
     copies = []
     for k in range(RHS):
         for i in range(groups):
-            rows = pl.ds(HALO * i, HALO)
-            done_ref[k, rows, :] = base_ref[k, rows, :] + u_ref[pl.ds(8 * i + k, 1), :]
+            coarse = u_ref[pl.ds(8 * i + k, 8, stride=0), :]
+            for part in range(HALO // 8):
+                rows = pl.ds(HALO * i + 8 * part, 8)
+                done_ref[k, rows, :] = base_ref[k, rows, :] + coarse
         copy = pltpu.make_async_copy(done_ref.at[k], out_ref.at[k], sem_ref.at[k])
         copy.start()
         copies.append(copy)
@@ -627,37 +667,49 @@
         return [near(value) for value in values]
 
     strip = (4 * HALO, cols)
-    kept, first, second = call(
+    hbm = [pl.BlockSpec(memory_space=pltpu.HBM)] * 4
+    near_whole = pltpu.VMEM((4, HALO, cols), jnp.int32)
+    first, second = call(
         pack_rows_kernel,
-        [(4, rows, cols), strip, strip],
-        [pltpu.VMEM((rows, cols), jnp.int32)] * 2 + [pltpu.SemaphoreType.DMA((4,))],
+        [strip, strip],
+        [(4, HALO, cols), near_whole, pltpu.SemaphoreType.DMA((8,))],
         *own,
-        in_specs=[pl.BlockSpec(memory_space=pltpu.HBM)] * 4,
+        in_specs=hbm,
+    )
+    tall_rows = rows + 2 * HALO
+    n1 = tall_rows // 2
+    tall, first_cols, second_cols, *tables = all_near(
+        call(
+            prepare_kernel,
+            [(4, tall_rows, cols), (n1, LANES), (n1, LANES)]
+            + [pltpu.VMEM((PIECES * LANES * len(tests), LANES), BF16) for tests in TABLES],
+            [pltpu.VMEM((rows, cols), jnp.int32)] * 2 + [pltpu.SemaphoreType.DMA((4,))],
+            *own,
+            near(first),
+            in_specs=hbm + [pl.BlockSpec(memory_space=pltpu.VMEM)],
+            cost_estimate=pl.CostEstimate(flops=10**8, bytes_accessed=10**6, transcendentals=0),
+        )
     )
     first, second = exchanged(first, second, "row", "col")
-    tall_rows = rows + 2 * HALO
-    strip = (tall_rows // 2, LANES)
-    kept = near(kept)
-    tables = all_near(
-        call(
-            tables_kernel,
-            [pltpu.VMEM((PIECES * LANES * len(tests), LANES), BF16) for tests in TABLES],
-            [],
-            kept,
-            cost_estimate=pl.CostEstimate(flops=10**7, bytes_accessed=10**6, transcendentals=0),
-        )
-    )
     tall, first, second = call(
-        pack_cols_kernel, [(4, tall_rows, cols), strip, strip], [], kept, near(first), near(second), tables[0]
-    )
+        pack_cols_kernel,
+        [(4, tall_rows, cols), (n1, LANES), (n1, LANES)],
+        [],
+        near(first),
+        near(second),
+        tall,
+        first_cols,
+        second_cols,
+        input_output_aliases={2: 0, 3: 1, 4: 2},
+    )
+    tall = near(tall)
     first, second = exchanged(first, second, "col", "row")
     sizes = [128, 64, 32]
-    n1 = tall_rows // 2
     inner = call(
         inner_kernel,
         [(RHS - 1, n1, LANES), (3, n1, LANES), (2, rows // 2, LANES), (4, tall_rows, LANES), (2, n1, LANES)],
         [],
-        near(tall),
+        tall,
         *tables[:3],
         cost_estimate=pl.CostEstimate(flops=10**8, bytes_accessed=10**6, transcendentals=0),
     )
@@ -675,7 +727,7 @@
         up_kernel,
         [(RHS, rows, cols)],
         [(RHS - 1, size, LANES) for size in sizes[::-1]],
-        kept,
+        tall,
         *all_near([w0] + levels),
         *tables[13:15],
         cost_estimate=pl.CostEstimate(flops=10**8, bytes_accessed=10**6, transcendentals=0),

time: 30.8 us -> 30.1 us (0.977)
  waiting for transfers between devices: 10.7 us -> 9.49 us
  Pallas kernels: 8.11 us -> 8.92 us
  starting transfers between devices: 11.8 us -> 11.3 us
    ppermute x4, waiting for transfers between devices: 3.04 us -> 1.84 us  [exchanged(): lax.ppermute(part, ('row', 'col'), pairs(step))]
    all_to_all x1, starting transfers between devices: 5.39 us -> 4.46 us  [shards(): everything = lax.all_to_all(payload, ('row', 'col'), 0, 0)]
    pallas_call x6, Pallas kernels: 5.24 us -> 6.05 us  [call(): pl.pallas_call(kernel, out_shape=outs, scratch_shapes=scratch, name=name,...]
    ppermute x4, starting transfers between devices: 6.4 us -> 6.85 us  [exchanged(): lax.ppermute(part, ('row', 'col'), pairs(step))]
  transfers between devices with their start and end apart: 5 -> 5, of which waited for: 3 -> 3; matrix products, arithmetic and copies ran while one was open for 0% -> 0% of each run, Pallas kernels for 5% -> 9%
where the time goes in v5:
time: 30.1 us; the launch traced here: 29.8 us
  starting transfers between devices  11.3 us (38%)
  waiting for transfers between devices  9.49 us (32%)
  Pallas kernels  8.92 us (30%)
    all_to_all x1, waiting for transfers between devices, shards(): everything = lax.all_to_all(payload, ('row', 'col'), 0, 0)  7.65 us
    ppermute x4, starting transfers between devices, exchanged(): lax.ppermute(part, ('row', 'col'), pairs(step))  6.85 us
    pallas_call x6, Pallas kernels, call(): pl.pallas_call(kernel, out_shape=outs, scratch_shapes=scratch, name=name,...  6.05 us
    all_to_all x1, starting transfers between devices, shards(): everything = lax.all_to_all(payload, ('row', 'col'), 0, 0)  4.46 us
    pallas_call x1, Pallas kernels, shards(): pl.pallas_call(functools.partial(solve_kernel, grid), out_shape=jax.Shape...  2.87 us
    ppermute x4, waiting for transfers between devices, exchanged(): lax.ppermute(part, ('row', 'col'), pairs(step))  1.84 us
  transfers between devices with their start and end apart: 5, of which 3 were waited for; matrix products, arithmetic and copies ran while one was open for 0% of the time, Pallas kernels for 9%

profile of v5, /device:TPU:0, one launch (start us, length us, event | category | flops | bytes accessed | tf_op | source)
XLA Modules:
  0.0 29.8 jit_solution(13134083488844338434)
XLA Ops:
  0.0 0.9 %pack_rows_kernel.1 = (f32[64,128]{1,0:T(8,128)S(1)}, f32[64,128]{1,0:T(8,128)S(1)}) custom-call(f32[192,128]{1,0:T(8,128)} %res_ref.3, f32[192,128]{1,0:T(8,128)} %ground_ref.3, s32[192,128]{1,0:T(8,128)} %nodata_ref.3, s32[192,128]{1,0:T(8,128)} %patch_ref.3), custom_call_target="tpu_custom_call" | custom-call | tf_op jit(solution)/shard_map/pack_rows_kernel/pallas_call | solution.py:662
  0.9 0.6 %collective-permute-start.1 = (f32[64,128]{1,0:T(8,128)S(1)}, f32[64,128]{1,0:T(8,128)S(1)}, u32[]{:S(2)}, u32[]{:S(2)}) collective-permute-start(f32[64,128]{1,0:T(8,128)S(1)} %get-tuple-element.43), channel_id=1, source_target_pairs={{0,1},{1,0},{2,3},{3,2},{4,5},{5,4},{6,7},{7,6},{8,16},{9,17},{10,... | collective-permute-start | bytes 98312 | tf_op jit(solution)/shard_map/ppermute | solution.py:646
  1.5 4.1 %collective-permute-start = (f32[64,128]{1,0:T(8,128)S(1)}, f32[64,128]{1,0:T(8,128)S(1)}, u32[]{:S(2)}, u32[]{:S(2)}) collective-permute-start(f32[64,128]{1,0:T(8,128)S(1)} %get-tuple-element.42.order_ref), channel_id=1, source_target_pairs={{0,8},{1,9},{2,10},{3,11},{4,12},{5,13},{6,14},{7,15},{8,0},{9,1},... | collective-permute-start | bytes 98312 | tf_op jit(solution)/shard_map/ppermute | solution.py:646
  5.6 1.3 %prepare_kernel.1 = (f32[4,224,128]{2,1,0:T(8,128)S(1)}, f32[112,128]{1,0:T(8,128)S(1)}, f32[112,128]{1,0:T(8,128)S(1)}, bf16[512,128]{1,0:T(8,128)(2,1)S(1)}, b...) custom-call(f32[192,128]{1,0:T(8,128)} %res_ref.3, ...), custom_call_target="tpu_custom_call" | custom-call | flops 100000000 | bytes 1000000 | tf_op jit(solution)/shard_map/prepare_kernel/pallas_call | solution.py:662
  6.9 0.0 collective-permute-done.1.from_second_ref
  6.9 0.5 %collective-permute-done.from_first_ref = f32[64,128]{1,0:T(8,128)S(1)} collective-permute-done((f32[64,128]{1,0:T(8,128)S(1)}, f32[64,128]{1,0:T(8,128)S(1)}, u32[]{:S(2)}, u32[]{:S(2)}) %collective-permute-start) | collective-permute-done | bytes 32800 | tf_op jit(solution)/shard_map/ppermute | solution.py:646
  7.5 0.1 pack_cols_kernel.1
  7.6 0.1 collective-permute-start.2
  7.7 2.1 %collective-permute-start.3 = (f32[112,128]{1,0:T(8,128)S(1)}, f32[112,128]{1,0:T(8,128)S(1)}, u32[]{:S(2)}, u32[]{:S(2)}) collective-permute-start(f32[112,128]{1,0:T(8,128)S(1)} %get-tuple-element.48), channel_id=1, source_target_pairs={{0,8},{1,2},{2,1},{3,4},{4,3},{5,6},{6,5},{7,15},{8,0},{9,10},{10,... | collective-permute-start | bytes 172040 | tf_op jit(solution)/shard_map/ppermute | solution.py:646
  9.8 0.8 %inner_kernel.1 = (f32[7,112,128]{2,1,0:T(8,128)S(1)}, f32[3,112,128]{2,1,0:T(8,128)S(1)}, f32[2,96,128]{2,1,0:T(8,128)S(1)}, f32[4,224,128]{2,1,0:T(8,128)S(1)}, f32[2,112,128]{2,1,0:T(8,128)S(1)}) custom-call(f32[4,224,128]{2,1,0:T(8,128)S(1)} %get-tuple-element.49.tall_ref, bf16[512,128]{1,0:T(8,128)(2,1)S(1)} %get-tuple-element.50.both_ref, ...), custom_call_target="tpu_custom_call" | custom-call | flops 100000000 | bytes 1000000 | tf_op jit(solution)/shard_map/inner_kernel/pallas_call | solution.py:662
  10.6 0.0 collective-permute-done.2.from_first_ref
  10.6 1.3 %collective-permute-done.3.from_second_ref = f32[112,128]{1,0:T(8,128)S(1)} collective-permute-done((f32[112,128]{1,0:T(8,128)S(1)}, f32[112,128]{1,0:T(8,128)S(1)}, u32[]{:S(2)}, u32[]{:S(2)}) %collective-permute-start.3) | collective-permute-done | bytes 57376 | tf_op jit(solution)/shard_map/ppermute | solution.py:646
  11.9 2.3 %down_kernel.1 = (f32[32,8,128]{2,1,0:T(8,128)}, f32[2,96,128]{2,1,0:T(8,128)S(1)}, f32[7,128,128]{2,1,0:T(8,128)S(1)}, f32[7,64,128]{2,1,0:T(8,128)S(1)}, f32[7...) custom-call(f32[112,128]{1,0:T(8,128)S(1)} %collective-permute-done.2.f, ...), custom_call_target="tpu_custom_call" | custom-call | tf_op jit(solution)/shard_map/down_kernel/pallas_call | solution.py:662
  14.3 4.5 %all-to-all-start = ((f32[32,8,128]{2,1,0:T(8,128)}), f32[32,8,128]{2,1,0:T(8,128)S(1)}, u32[]{:S(2)}, u32[]{:S(2)}) async-start(f32[32,8,128]{2,1,0:T(8,128)} %get-tuple-element.68), calls=%async_computation | async-start | bytes 262144 | tf_op jit(solution)/shard_map/all_to_all | solution.py:725
  18.7 0.5 %up_kernel.1.base_ref = f32[8,192,128]{2,1,0:T(8,128)S(1)} custom-call(f32[4,224,128]{2,1,0:T(8,128)S(1)} %get-tuple-element.49.tall_ref, f32[2,96,128]{2,1,0:T(8,128)S(1)} %get-tuple-element.69.w0_ref, f32[7,128,128]{2,1,0:T(8,128)S(1)} %get-tuple-element.70.r1_ref, f32[7,64,128]{2,1,0:T(8,128)S(1)} %get-tuple-element.71.r2_ref, ...), custom_call_target="tpu_custom_call" | custom-call | flops 100000000 | bytes 1000000 | tf_op jit(solution)/shard_map/up_kernel/pallas_call | solution.py:662
  19.3 7.7 %all-to-all-done = f32[32,8,128]{2,1,0:T(8,128)S(1)} async-done(((f32[32,8,128]{2,1,0:T(8,128)}), f32[32,8,128]{2,1,0:T(8,128)S(1)}, u32[]{:S(2)}, u32[]{:S(2)}) %all-to-all-start) | async-done | bytes 131104 | tf_op jit(solution)/shard_map/all_to_all | solution.py:725
  26.9 2.9 %solve_kernel.1 = f32[8,192,128]{2,1,0:T(8,128)} custom-call(f32[256,128]{1,0:T(8,128)S(1)} %bitcast.1, f32[8,192,128]{2,1,0:T(8,128)S(1)} %up_kernel.1.base_ref, bf16[256,128]{1,0:T(8,128)(2,1)S(1)} %get-tuple-element.78.widen_ref), custom_call_target="tpu_custom_call" | custom-call | tf_op jit(solution)/shard_map/solve_kernel/pallas_call | solution.py:735
Async XLA Ops:
  0.9 6.0 %collective-permute-start.1 = (f32[64,128]{1,0:T(8,128)S(1)}, f32[64,128]{1,0:T(8,128)S(1)}, u32[]{:S(2)}, u32[]{:S(2)}) collective-permute-start(f32[64,128]{1,0:T(8,128)S(1)} %get-tuple-element.43), channel_id=1, source_target_pairs={{0,1},{1,0},{2,3},{3,2},{4,5},{5,4},{6,7},{7,6},{8,16},{9,17},{10,... | collective-permute-start | bytes 98312 | tf_op jit(solution)/shard_map/ppermute | solution.py:646
  1.5 6.0 %collective-permute-start = (f32[64,128]{1,0:T(8,128)S(1)}, f32[64,128]{1,0:T(8,128)S(1)}, u32[]{:S(2)}, u32[]{:S(2)}) collective-permute-start(f32[64,128]{1,0:T(8,128)S(1)} %get-tuple-element.42.order_ref), channel_id=1, source_target_pairs={{0,8},{1,9},{2,10},{3,11},{4,12},{5,13},{6,14},{7,15},{8,0},{9,1},... | collective-permute-start | bytes 98312 | tf_op jit(solution)/shard_map/ppermute | solution.py:646
  7.6 3.0 %collective-permute-start.2 = (f32[112,128]{1,0:T(8,128)S(1)}, f32[112,128]{1,0:T(8,128)S(1)}, u32[]{:S(2)}, u32[]{:S(2)}) collective-permute-start(f32[112,128]{1,0:T(8,128)S(1)} %get-tuple-element.47), channel_id=1, source_target_pairs={{0,1},{1,0},{2,3},{3,2},{4,5},{5,4},{6,7},{7,6},{8,9},{9,8},{10,11... | collective-permute-start | bytes 172040 | tf_op jit(solution)/shard_map/ppermute | solution.py:646
  7.7 4.2 %collective-permute-start.3 = (f32[112,128]{1,0:T(8,128)S(1)}, f32[112,128]{1,0:T(8,128)S(1)}, u32[]{:S(2)}, u32[]{:S(2)}) collective-permute-start(f32[112,128]{1,0:T(8,128)S(1)} %get-tuple-element.48), channel_id=1, source_target_pairs={{0,8},{1,2},{2,1},{3,4},{4,3},{5,6},{6,5},{7,15},{8,0},{9,10},{10,... | collective-permute-start | bytes 172040 | tf_op jit(solution)/shard_map/ppermute | solution.py:646
  14.3 12.7 %all-to-all-start = ((f32[32,8,128]{2,1,0:T(8,128)}), f32[32,8,128]{2,1,0:T(8,128)S(1)}, u32[]{:S(2)}, u32[]{:S(2)}) async-start(f32[32,8,128]{2,1,0:T(8,128)} %get-tuple-element.68), calls=%async_computation | async-start | bytes 262144 | tf_op jit(solution)/shard_map/all_to_all | solution.py:725

commit v6 on v5

--- a/solution.py
+++ b/solution.py
@@ -307,19 +307,19 @@
     c2_ref,
     c3_ref,
 ):
-    devices = payload_ref.shape[0]
     n1 = edge_ref.shape[1] // 2
     lane = iota((n1, LANES), 1)
     from_left, from_right = before_after("col", from_first_ref[...], from_second_ref[...])
-    at_left = (lane < 15) | (lane == LANES - 1)
+    from_right = rot(from_right, 18, 1)
     at_edge = (lane == 15) | (lane == 16)
-    at_right = (lane > 16) & (lane < 33)
+    at_halo = (lane < 33) | (lane == LANES - 1)
     for which in range(4):
         for part in range(2):
             group = 2 * which + part
             rows = pl.ds(part * n1, n1)
-            value = jnp.where(at_right, rot(from_right, 17 - HALO * group, 1), 0.0)
-            value = jnp.where(at_left, rot(from_left, -1 - HALO * group, 1), value)
+            offset = (lane - HALO * group) % LANES
+            value = jnp.where(offset < HALO, from_left, from_right)
+            value = jnp.where(at_halo, rot(value, -1 - HALO * group, 1), 0.0)
             value = jnp.where(at_edge, edge_ref[which, rows, :], value)
             if which < 2:
                 value = jnp.where(value > 0, value, 1.0)
@@ -430,9 +430,7 @@
         tile = jnp.where(sub == k, flat(fields[k]), tile)
     tile = jnp.where(lane8 < 96, tile, turned)
 
-    @pl.loop(0, devices)
-    def _(device):
-        payload_ref[device] = tile
+    payload_ref[...] = jnp.broadcast_to(tile, payload_ref.shape)
 
 
 def up_kernel(
@@ -494,8 +492,6 @@
     p_ref,
     p_up_ref,
     p_down_ref,
-    p_first_ref,
-    p_last_ref,
     u_ref,
     done_ref,
     sem_ref,
@@ -537,11 +533,11 @@
     west_right = jnp.where(iota((count, LANES), 0) % grid_cols < grid_cols - 1, rot(west, -1, 0), 0.0)
     east = jnp.where(all_lane % 8 == 7, rot(west_right, 7, 1), rot(west, 127, 1))
     south, east = jnp.where(inside, south, 0.0), jnp.where(inside, east, 0.0)
-    coef_ref[0] = jnp.where(inside, rows[7], 0.0) + north + south + west + east
-    coef_ref[1] = north
-    coef_ref[2] = south
-    coef_ref[3] = west
-    coef_ref[4] = east
+    diagonal = jnp.where(inside, rows[7], 0.0) + north + south + west + east
+    for index, value in enumerate((diagonal, north, south, west, east)):
+        for row in range(grid_rows):
+            part = slice(row * grid_cols, (row + 1) * grid_cols)
+            coef_ref[index, part] = rot(value[part], 96 * row, 1)
     others = ((rows[0] + rows[1]) + (rows[2] + rows[3])) + ((rows[4] + rows[5]) + rows[6])
     r_ref[...] = jnp.where(iota(r_ref.shape, 1) < 96, all_ref[...], 0.0)
     r_ref[pl.ds(7, count, stride=8), :] = jnp.where(inside, -others, 0.0)
@@ -553,11 +549,10 @@
         p_ref[at(t), :] = values
         p_up_ref[at(t), :] = rot(values, 8, 1)
         p_down_ref[at(t), :] = rot(values, 120, 1)
-        p_last_ref[at(t), :] = rot(values, 40, 1)
-        p_first_ref[at(t), :] = rot(values, 88, 1)
 
     def begin(t, norm):
-        values = r_ref[at(t), :]
+        values = pltpu.roll(r_ref[at(t), :], 96 * (t // grid_cols) % LANES, 1)
+        r_ref[at(t), :] = values
         direct(t, values)
         return norm + values * values
 
@@ -569,12 +564,13 @@
 
     def image_of(t, dot):
         here = p_ref[at(t), :]
-        up = p_last_ref[at(choose(t >= grid_cols, t - grid_cols, t)), :]
-        down = p_first_ref[at(choose(t + grid_cols < count, t + grid_cols, t)), :]
+        up = p_up_ref[at(choose(t >= grid_cols, t - grid_cols, t)), :]
+        down = p_down_ref[at(choose(t + grid_cols < count, t + grid_cols, t)), :]
         left = p_down_ref[at(choose(t % grid_cols > 0, t - 1, t)), :]
         right = p_up_ref[at(choose(t % grid_cols < grid_cols - 1, t + 1, t)), :]
-        up = jnp.where(lane < 8, up, p_up_ref[at(t), :])
-        down = jnp.where(lane >= 88, down, p_down_ref[at(t), :])
+        start = 12 * (t // grid_cols)
+        up = jnp.where(lane // 8 == start % 16, up, p_up_ref[at(t), :])
+        down = jnp.where(lane // 8 == (start + 11) % 16, down, p_down_ref[at(t), :])
         left = rot(jnp.where(column == 7, left, here), 1, 1)
         right = rot(jnp.where(column == 0, right, here), -1, 1)
         pulled = coef_of(1, t) * up + coef_of(2, t) * down
@@ -607,9 +603,10 @@
     step = jnp.broadcast_to(rr / total(every(image_of, zero)), (8, LANES))
     device = lax.axis_index("row") * grid_cols + lax.axis_index("col")
     mine = x_ref[at(device), :] + step * p_ref[at(device), :]
-    groups = u_ref.shape[0] // 8
+    mine = pltpu.roll(mine, 32 * lax.axis_index("row") % LANES, 1)
+    groups = u_ref.shape[0] // 8 - 1
     placed = jnp.concatenate([jnp.where(lane // 8 == i, mine, 0.0) for i in range(groups)], axis=0)
-    u_ref[...] = dot01([placed], widen_ref[...])
+    u_ref[0 : 8 * groups] = dot01([placed], widen_ref[...])
     copies = []
     for k in range(RHS):
         for i in range(groups):
@@ -736,9 +733,9 @@
         functools.partial(solve_kernel, grid),
         out_shape=jax.ShapeDtypeStruct((RHS, rows, cols), F32),
         out_specs=pl.BlockSpec(memory_space=pl.ANY),
-        scratch_shapes=[pltpu.VMEM((5, devices, LANES), F32)]
-        + [pltpu.VMEM((devices * 8, LANES), F32)] * 8
-        + [pltpu.VMEM((rows // HALO * 8, LANES), F32), pltpu.VMEM((RHS, rows, cols), F32)]
+        scratch_shapes=[pltpu.VMEM((5, devices + 8, LANES), F32)]
+        + [pltpu.VMEM((devices * 8, LANES), F32)] * 6
+        + [pltpu.VMEM((rows // HALO * 8 + 8, LANES), F32), pltpu.VMEM((RHS, rows, cols), F32)]
         + [pltpu.SemaphoreType.DMA((RHS,))],
         compiler_params=pltpu.CompilerParams(vmem_limit_bytes=VMEM_LIMIT),
         name="solve_kernel",

time: 30.1 us -> 29.9 us (level)
  no operation moved by 1% of the time
where the time goes in v6:
time: 29.9 us; the launch traced here: 29.6 us
  starting transfers between devices  11.3 us (38%)
  waiting for transfers between devices  9.5 us (32%)
  Pallas kernels  8.73 us (29%)
    all_to_all x1, waiting for transfers between devices, shards(): everything = lax.all_to_all(payload, ('row', 'col'), 0, 0)  7.65 us
    ppermute x4, starting transfers between devices, exchanged(): lax.ppermute(part, ('row', 'col'), pairs(step))  6.85 us
    pallas_call x6, Pallas kernels, call(): pl.pallas_call(kernel, out_shape=outs, scratch_shapes=scratch, name=name,...  5.92 us
    all_to_all x1, starting transfers between devices, shards(): everything = lax.all_to_all(payload, ('row', 'col'), 0, 0)  4.46 us
    pallas_call x1, Pallas kernels, shards(): pl.pallas_call(functools.partial(solve_kernel, grid), out_shape=jax.Shape...  2.82 us
    ppermute x4, waiting for transfers between devices, exchanged(): lax.ppermute(part, ('row', 'col'), pairs(step))  1.84 us
  transfers between devices with their start and end apart: 5, of which 3 were waited for; matrix products, arithmetic and copies ran while one was open for 0% of the time, Pallas kernels for 9%

profile of v6, /device:TPU:0, one launch (start us, length us, event | category | flops | bytes accessed | tf_op | source)
XLA Modules:
  0.0 29.6 jit_solution(4170655678216891617)
XLA Ops:
  0.0 0.9 %pack_rows_kernel.1 = (f32[64,128]{1,0:T(8,128)S(1)}, f32[64,128]{1,0:T(8,128)S(1)}) custom-call(f32[192,128]{1,0:T(8,128)} %res_ref.3, f32[192,128]{1,0:T(8,128)} %ground_ref.3, s32[192,128]{1,0:T(8,128)} %nodata_ref.3, s32[192,128]{1,0:T(8,128)} %patch_ref.3), custom_call_target="tpu_custom_call" | custom-call | tf_op jit(solution)/shard_map/pack_rows_kernel/pallas_call | solution.py:659
  0.9 0.6 %collective-permute-start.1 = (f32[64,128]{1,0:T(8,128)S(1)}, f32[64,128]{1,0:T(8,128)S(1)}, u32[]{:S(2)}, u32[]{:S(2)}) collective-permute-start(f32[64,128]{1,0:T(8,128)S(1)} %get-tuple-element.43), channel_id=1, source_target_pairs={{0,1},{1,0},{2,3},{3,2},{4,5},{5,4},{6,7},{7,6},{8,16},{9,17},{10,... | collective-permute-start | bytes 98312 | tf_op jit(solution)/shard_map/ppermute | solution.py:643
  1.5 4.1 %collective-permute-start = (f32[64,128]{1,0:T(8,128)S(1)}, f32[64,128]{1,0:T(8,128)S(1)}, u32[]{:S(2)}, u32[]{:S(2)}) collective-permute-start(f32[64,128]{1,0:T(8,128)S(1)} %get-tuple-element.42.order_ref), channel_id=1, source_target_pairs={{0,8},{1,9},{2,10},{3,11},{4,12},{5,13},{6,14},{7,15},{8,0},{9,1},... | collective-permute-start | bytes 98312 | tf_op jit(solution)/shard_map/ppermute | solution.py:643
  5.6 1.3 %prepare_kernel.1 = (f32[4,224,128]{2,1,0:T(8,128)S(1)}, f32[112,128]{1,0:T(8,128)S(1)}, f32[112,128]{1,0:T(8,128)S(1)}, bf16[512,128]{1,0:T(8,128)(2,1)S(1)}, b...) custom-call(f32[192,128]{1,0:T(8,128)} %res_ref.3, ...), custom_call_target="tpu_custom_call" | custom-call | flops 100000000 | bytes 1000000 | tf_op jit(solution)/shard_map/prepare_kernel/pallas_call | solution.py:659
  6.9 0.0 collective-permute-done.1.from_second_ref
  6.9 0.5 %collective-permute-done.from_first_ref = f32[64,128]{1,0:T(8,128)S(1)} collective-permute-done((f32[64,128]{1,0:T(8,128)S(1)}, f32[64,128]{1,0:T(8,128)S(1)}, u32[]{:S(2)}, u32[]{:S(2)}) %collective-permute-start) | collective-permute-done | bytes 32800 | tf_op jit(solution)/shard_map/ppermute | solution.py:643
  7.5 0.1 pack_cols_kernel.1
  7.6 0.1 collective-permute-start.2
  7.7 2.1 %collective-permute-start.3 = (f32[112,128]{1,0:T(8,128)S(1)}, f32[112,128]{1,0:T(8,128)S(1)}, u32[]{:S(2)}, u32[]{:S(2)}) collective-permute-start(f32[112,128]{1,0:T(8,128)S(1)} %get-tuple-element.48), channel_id=1, source_target_pairs={{0,8},{1,2},{2,1},{3,4},{4,3},{5,6},{6,5},{7,15},{8,0},{9,10},{10,... | collective-permute-start | bytes 172040 | tf_op jit(solution)/shard_map/ppermute | solution.py:643
  9.8 0.8 %inner_kernel.1 = (f32[7,112,128]{2,1,0:T(8,128)S(1)}, f32[3,112,128]{2,1,0:T(8,128)S(1)}, f32[2,96,128]{2,1,0:T(8,128)S(1)}, f32[4,224,128]{2,1,0:T(8,128)S(1)}, f32[2,112,128]{2,1,0:T(8,128)S(1)}) custom-call(f32[4,224,128]{2,1,0:T(8,128)S(1)} %get-tuple-element.49.tall_ref, bf16[512,128]{1,0:T(8,128)(2,1)S(1)} %get-tuple-element.50.both_ref, ...), custom_call_target="tpu_custom_call" | custom-call | flops 100000000 | bytes 1000000 | tf_op jit(solution)/shard_map/inner_kernel/pallas_call | solution.py:659
  10.6 0.0 collective-permute-done.2.from_first_ref
  10.6 1.3 %collective-permute-done.3.from_second_ref = f32[112,128]{1,0:T(8,128)S(1)} collective-permute-done((f32[112,128]{1,0:T(8,128)S(1)}, f32[112,128]{1,0:T(8,128)S(1)}, u32[]{:S(2)}, u32[]{:S(2)}) %collective-permute-start.3) | collective-permute-done | bytes 57376 | tf_op jit(solution)/shard_map/ppermute | solution.py:643
  11.9 2.2 %down_kernel.1 = (f32[32,8,128]{2,1,0:T(8,128)}, f32[2,96,128]{2,1,0:T(8,128)S(1)}, f32[7,128,128]{2,1,0:T(8,128)S(1)}, f32[7,64,128]{2,1,0:T(8,128)S(1)}, f32[7...) custom-call(f32[112,128]{1,0:T(8,128)S(1)} %collective-permute-done.2.f, ...), custom_call_target="tpu_custom_call" | custom-call | tf_op jit(solution)/shard_map/down_kernel/pallas_call | solution.py:659
  14.1 4.5 %all-to-all-start = ((f32[32,8,128]{2,1,0:T(8,128)}), f32[32,8,128]{2,1,0:T(8,128)S(1)}, u32[]{:S(2)}, u32[]{:S(2)}) async-start(f32[32,8,128]{2,1,0:T(8,128)} %get-tuple-element.68), calls=%async_computation | async-start | bytes 262144 | tf_op jit(solution)/shard_map/all_to_all | solution.py:722
  18.6 0.5 %up_kernel.1.base_ref = f32[8,192,128]{2,1,0:T(8,128)S(1)} custom-call(f32[4,224,128]{2,1,0:T(8,128)S(1)} %get-tuple-element.49.tall_ref, f32[2,96,128]{2,1,0:T(8,128)S(1)} %get-tuple-element.69.w0_ref, f32[7,128,128]{2,1,0:T(8,128)S(1)} %get-tuple-element.70.r1_ref, f32[7,64,128]{2,1,0:T(8,128)S(1)} %get-tuple-element.71.r2_ref, ...), custom_call_target="tpu_custom_call" | custom-call | flops 100000000 | bytes 1000000 | tf_op jit(solution)/shard_map/up_kernel/pallas_call | solution.py:659
  19.1 7.7 %all-to-all-done = f32[32,8,128]{2,1,0:T(8,128)S(1)} async-done(((f32[32,8,128]{2,1,0:T(8,128)}), f32[32,8,128]{2,1,0:T(8,128)S(1)}, u32[]{:S(2)}, u32[]{:S(2)}) %all-to-all-start) | async-done | bytes 131104 | tf_op jit(solution)/shard_map/all_to_all | solution.py:722
  26.8 2.8 %solve_kernel.1 = f32[8,192,128]{2,1,0:T(8,128)} custom-call(f32[256,128]{1,0:T(8,128)S(1)} %bitcast.1, f32[8,192,128]{2,1,0:T(8,128)S(1)} %up_kernel.1.base_ref, bf16[256,128]{1,0:T(8,128)(2,1)S(1)} %get-tuple-element.78.widen_ref), custom_call_target="tpu_custom_call" | custom-call | tf_op jit(solution)/shard_map/solve_kernel/pallas_call | solution.py:732
Async XLA Ops:
  0.9 6.0 %collective-permute-start.1 = (f32[64,128]{1,0:T(8,128)S(1)}, f32[64,128]{1,0:T(8,128)S(1)}, u32[]{:S(2)}, u32[]{:S(2)}) collective-permute-start(f32[64,128]{1,0:T(8,128)S(1)} %get-tuple-element.43), channel_id=1, source_target_pairs={{0,1},{1,0},{2,3},{3,2},{4,5},{5,4},{6,7},{7,6},{8,16},{9,17},{10,... | collective-permute-start | bytes 98312 | tf_op jit(solution)/shard_map/ppermute | solution.py:643
  1.5 6.0 %collective-permute-start = (f32[64,128]{1,0:T(8,128)S(1)}, f32[64,128]{1,0:T(8,128)S(1)}, u32[]{:S(2)}, u32[]{:S(2)}) collective-permute-start(f32[64,128]{1,0:T(8,128)S(1)} %get-tuple-element.42.order_ref), channel_id=1, source_target_pairs={{0,8},{1,9},{2,10},{3,11},{4,12},{5,13},{6,14},{7,15},{8,0},{9,1},... | collective-permute-start | bytes 98312 | tf_op jit(solution)/shard_map/ppermute | solution.py:643
  7.6 3.0 %collective-permute-start.2 = (f32[112,128]{1,0:T(8,128)S(1)}, f32[112,128]{1,0:T(8,128)S(1)}, u32[]{:S(2)}, u32[]{:S(2)}) collective-permute-start(f32[112,128]{1,0:T(8,128)S(1)} %get-tuple-element.47), channel_id=1, source_target_pairs={{0,1},{1,0},{2,3},{3,2},{4,5},{5,4},{6,7},{7,6},{8,9},{9,8},{10,11... | collective-permute-start | bytes 172040 | tf_op jit(solution)/shard_map/ppermute | solution.py:643
  7.7 4.2 %collective-permute-start.3 = (f32[112,128]{1,0:T(8,128)S(1)}, f32[112,128]{1,0:T(8,128)S(1)}, u32[]{:S(2)}, u32[]{:S(2)}) collective-permute-start(f32[112,128]{1,0:T(8,128)S(1)} %get-tuple-element.48), channel_id=1, source_target_pairs={{0,8},{1,2},{2,1},{3,4},{4,3},{5,6},{6,5},{7,15},{8,0},{9,10},{10,... | collective-permute-start | bytes 172040 | tf_op jit(solution)/shard_map/ppermute | solution.py:643
  14.1 12.7 %all-to-all-start = ((f32[32,8,128]{2,1,0:T(8,128)}), f32[32,8,128]{2,1,0:T(8,128)S(1)}, u32[]{:S(2)}, u32[]{:S(2)}) async-start(f32[32,8,128]{2,1,0:T(8,128)} %get-tuple-element.68), calls=%async_computation | async-start | bytes 262144 | tf_op jit(solution)/shard_map/all_to_all | solution.py:722
